TPU v7x, 32 devices: a whole 2x2x4 slice. The times are simulated.
32 devices in a mesh: ax: 8 (over z, y), ty: 2 (over x), tz: 2 (over core).
Axes of the slice: x: 2, y: 2, z: 4, core: 2. Of those that a mesh axis runs over, the one named last changes fastest.
Arguments:
- adjoint: float32 [5, 128, 32, 256], P(None, 'ax', 'ty', 'tz'), may hold values from -6 to 6
- velocity: float32 [3, 128, 32, 256], P(None, 'ax', 'ty', 'tz'), may hold values from -0.5 to 0.5
- sound_speed: float32 [128, 32, 256], P('ax', 'ty', 'tz'), may hold values from 0.6 to 1.2
- sponge: float32 [128, 32, 256], P('ax', 'ty', 'tz'), may hold values from 0.05 to 0.5
- source: float32 [5, 128, 32, 256], P(None, 'ax', 'ty', 'tz'), may hold values from -6 to 6
- mode_basis: float32 [8, 128, 128], P('ax'), may hold values from -0.5 to 0.5
- block_owner: int32 [8, 2, 2, 32, 1], P('ax', 'ty', 'tz'), may hold values from 0 to 7; in each aligned block of 32 rows (0 to 31, 32 to 63, ..., all dimensions but the last counted through in order) at most 8 rows name the same one
Outputs:
- adjoint_out: float32 [5, 128, 32, 256], P(None, 'ax', 'ty', 'tz')
- sensitivity: float32 [8, 5, 128], P('ax', None, ('ty', 'tz'))
Inputs may be any that keep to these rules, and one draw needn't show every extreme that they name: `block_owner`: of the 32 face blocks of one brick, at most 8 have the same owner, and in every draw some brick gives exactly 8 to one owner.
All inputs are finite; a program needn't handle non-finite values.
Results may differ from a plain program's by a relative error of at most 0.000092.
Values sent between devices are 32-bit elements; how exact they have to be, the bound alone decides.
No kernel may reach another device: no remote copies, remote signals or barrier semaphores. Data moves between devices by JAX's collectives and lax.ppermute only.
A program may use at most 128 MiB of HBM per device.

v0:
```python
import math

import jax
import jax.numpy as jnp
from jax import lax
from jax.sharding import PartitionSpec as P

FACE_PLANES = 2


time_step = 0.6
weights_fd = (45.0 / 60.0, -9.0 / 60.0, 1.0 / 60.0)


def padded_2(cells, sides, width):
    for axis, dim in sides:
        count = lax.axis_size(axis)
        ends = count - 1
        head = lax.slice_in_dim(cells, 0, width, axis=dim)
        tail = lax.slice_in_dim(cells, cells.shape[dim] - width, cells.shape[dim], axis=dim)
        cells = jnp.concatenate(
            [
                lax.ppermute(tail, axis, [(i, (i + 1) % count) for i in range(ends)]),
                cells,
                lax.ppermute(head, axis, [((i + 1) % count, i) for i in range(ends)]),
            ],
            axis=dim,
        )
    return cells


def difference(padded, direction, length):
    summed = None
    for s in range(1, 4):
        forward = lax.slice_in_dim(padded, 3 + s, 3 + s + length, axis=direction)
        backward = lax.slice_in_dim(padded, 3 - s, 3 - s + length, axis=direction)
        contrib = weights_fd[s - 1] * (forward - backward)
        summed = contrib if summed is None else summed + contrib
    return summed


def combine(gradients, velocity, sound_speed, sponge, source, current):
    advect = [
        velocity[0] * gradients[0][k]
        + velocity[1] * gradients[1][k]
        + velocity[2] * gradients[2][k]
        for k in range(5)
    ]
    pieces = [advect[0]]
    for d in range(3):
        pieces.append(advect[1 + d] + sound_speed * gradients[d][4])
    pieces.append(advect[4] + sound_speed * (gradients[0][1] + gradients[1][2] + gradients[2][3]))
    return jnp.stack(pieces) - sponge * current + source


def section_rate(current, velocity, sound_speed, sponge, source):
    trimmed = [
        padded_2(current, (("ax", 1),), 3),
        padded_2(current, (("ty", 2),), 3),
        padded_2(current, (("tz", 3),), 3),
    ]
    gradients = [difference(trimmed[d], d + 1, current.shape[d + 1]) for d in range(3)]
    return combine(gradients, velocity, sound_speed, sponge, source, current)


def on_device(adjoint, velocity, sound_speed, sponge, source, mode_basis, block_owner):
    first = section_rate(adjoint, velocity, sound_speed, sponge, source)
    middle = adjoint + time_step * first
    second = section_rate(middle, velocity, sound_speed, sponge, source)
    adjoint_out = adjoint + 0.5 * time_step * (first + second)
    owners_count = lax.axis_size("ax")
    depth = adjoint.shape[3]
    block_count = FACE_PLANES * adjoint.shape[2]
    capacity = max(2, 2 * ((block_count + owners_count - 1) // owners_count))
    face_rows = jnp.transpose(adjoint_out[:, :FACE_PLANES], (1, 2, 0, 3)).reshape(
        block_count, 5 * depth
    )
    owners = block_owner.reshape(block_count)
    onehot = (owners[:, None] == jnp.arange(owners_count, dtype=jnp.int32)[None, :]).astype(
        jnp.int32
    )
    before = jnp.cumsum(onehot, axis=0) - onehot
    position = jnp.sum(before * onehot, axis=1)
    target = owners * capacity + position
    placing = (
        target[:, None] == jnp.arange(owners_count * capacity, dtype=jnp.int32)[None, :]
    ).astype(jnp.float32)
    outgoing = jnp.dot(placing.T, face_rows, precision=lax.Precision.HIGHEST).reshape(
        owners_count, capacity, 5 * depth
    )
    own_basis = mode_basis[0]
    received = lax.all_to_all(outgoing, "ax", split_axis=0, concat_axis=0, tiled=True)
    shaped = received.reshape(received.shape[0], received.shape[1], 5, depth)
    coefficients = jnp.einsum("ajkc,cm->ajkm", shaped, own_basis, precision=lax.Precision.HIGHEST)
    local_sum = jnp.sum(coefficients, axis=(0, 1))[None]
    scale = 1.0 / math.sqrt(block_count * lax.axis_size("ty") * lax.axis_size("tz"))
    sensitivity = lax.psum_scatter(local_sum * scale, ("ty", "tz"), scatter_dimension=2, tiled=True)
    return (adjoint_out, sensitivity)


def solution(mesh):
    return jax.shard_map(
        on_device,
        mesh=mesh,
        in_specs=(
            P(None, "ax", "ty", "tz"),
            P(None, "ax", "ty", "tz"),
            P("ax", "ty", "tz"),
            P("ax", "ty", "tz"),
            P(None, "ax", "ty", "tz"),
            P("ax", None, None),
            P("ax", "ty", "tz", None, None),
        ),
        out_specs=(P(None, "ax", "ty", "tz"), P("ax", None, ("ty", "tz"))),
        check_vma=False,
    )
```

profile of v0, /device:TPU:0, one launch (start us, length us, event | category | flops | bytes accessed | tf_op | source)
XLA Modules:
  0.0 115.1 jit_solution(2140037814559848345)
XLA Ops:
  7.2 1.2 %fusion.128 = (f32[5,16,3,128]{3,2,1,0:T(4,128)S(1)}, f32[5,16,3,128]{3,2,1,0:T(4,128)S(1)}) fusion(f32[5,16,16,128]{3,2,1,0:T(8,128)} %param.7), kind=kLoop, calls=%fused_computation.238 | loop fusion | bytes 491520 | tf_op jit(solution)/shard_map/slice | solution.py:19
  8.4 1.3 %collective-permute-start.2 = (f32[5,16,3,128]{3,1,2,0:T(8,128)S(1)}, f32[5,16,3,128]{3,1,2,0:T(8,128)S(1)}, u32[]{:S(2)}, u32[]{:S(2)}) collective-permute-start(f32[5,16,3,128]{3,1,2,0:T(8,128)S(1)} %copy.92), channel_id=1, source_target_pairs={{2,0},{3,1},{6,4},{7,5},{10,8},{11,9},{14,12},{15,13},{18,16},{19,... | collective-permute-start | bytes 368648 | tf_op jit(solution)/shard_map/ppermute | solution.py:25
  9.8 0.2 fusion.129
  10.0 0.6 copy.94
  10.6 1.3 %collective-permute-start.4 = (f32[5,16,16,3]{2,1,3,0:T(8,128)S(1)}, f32[5,16,16,3]{2,1,3,0:T(8,128)S(1)}, u32[]{:S(2)}, u32[]{:S(2)}) collective-permute-start(f32[5,16,16,3]{2,1,3,0:T(8,128)S(1)} %copy.94), channel_id=1, source_target_pairs={{1,0},{3,2},{5,4},{7,6},{9,8},{11,10},{13,12},{15,14},{17,16},{19,... | collective-permute-start | bytes 46088 | tf_op jit(solution)/shard_map/ppermute | solution.py:25
  11.9 0.6 copy.95
  12.5 3.7 %collective-permute-start.5 = (f32[5,16,16,3]{2,1,3,0:T(8,128)S(1)}, f32[5,16,16,3]{2,1,3,0:T(8,128)}, u32[]{:S(2)}, u32[]{:S(2)}) collective-permute-start(f32[5,16,16,3]{2,1,3,0:T(8,128)S(1)} %copy.95), channel_id=1, source_target_pairs={{0,1},{2,3},{4,5},{6,7},{8,9},{10,11},{12,13},{14,15},{16,17},{18,... | collective-permute-start | bytes 46088 | tf_op jit(solution)/shard_map/ppermute | solution.py:23
  16.1 0.7 fusion.127
  16.9 4.9 %collective-permute-start.1 = (f32[5,3,16,128]{3,2,1,0:T(8,128)}, f32[5,3,16,128]{3,2,1,0:T(8,128)S(1)}, u32[]{:S(2)}, u32[]{:S(2)}) collective-permute-start(f32[5,3,16,128]{3,2,1,0:T(8,128)} %get-tuple-element.13), channel_id=1, source_target_pairs={{0,4},{4,8},{8,12},{12,16},{16,20},{20,24},{24,28},{1,5},{5,9},{9,... | collective-permute-start | bytes 368648 | tf_op jit(solution)/shard_map/ppermute | solution.py:23
  21.7 0.7 copy.93
  22.4 5.2 %collective-permute-start.3 = (f32[5,16,3,128]{3,1,2,0:T(8,128)}, f32[5,16,3,128]{3,1,2,0:T(8,128)}, u32[]{:S(2)}, u32[]{:S(2)}) collective-permute-start(f32[5,16,3,128]{3,1,2,0:T(8,128)} %copy.93), channel_id=1, source_target_pairs={{0,2},{1,3},{4,6},{5,7},{8,10},{9,11},{12,14},{13,15},{16,18},{17,... | collective-permute-start | bytes 368648 | tf_op jit(solution)/shard_map/ppermute | solution.py:23
  27.6 0.1 fusion.123
  27.6 0.1 reduce_window_sum.11
  27.7 0.2 select_reduce_fusion
  28.0 1.3 %collective-permute-start = (f32[5,3,16,128]{3,2,1,0:T(8,128)}, f32[5,3,16,128]{3,2,1,0:T(8,128)S(1)}, u32[]{:S(2)}, u32[]{:S(2)}) collective-permute-start(f32[5,3,16,128]{3,2,1,0:T(8,128)} %get-tuple-element.12), channel_id=1, source_target_pairs={{4,0},{8,4},{12,8},{16,12},{20,16},{24,20},{28,24},{5,1},{9,5},{13... | collective-permute-start | bytes 368648 | tf_op jit(solution)/shard_map/ppermute | solution.py:25
  29.3 0.5 copy.77
  29.8 1.4 %copy.79 = f32[5,16,16,3]{3,2,1,0:T(8,128)S(1)} copy(f32[5,16,16,3]{2,1,3,0:T(8,128)} %collective-permute-done.5) | data formatting | bytes 30720 | tf_op jit(solution)/shard_map/ppermute | solution.py:23
  31.3 1.0 copy.75
  32.3 0.1 copy_dynamic-update-slice_fusion
  32.4 2.5 %constant_dynamic-update-slice_fusion.1 = (f32[5,19,16,128]{3,2,1,0:T(8,128)S(1)}, f32[5,16,16,128]{3,2,1,0:T(8,128)S(1)}, f32[5,16,16,128]{3,2,1,0:T(8,128)S(1)}, f32[5,19,16,128]{3,2,1,0:T(8,128)S(1)}) fusion(f32[5,16,16,128]{3,2,1,0:T(8,128)S(1)} %copy-done.2, f32[5,16,16,3]{3,2,1,0:T(8,128)S(1)} %copy.79, f32[5,16,16,3]{3,2,1,0:T(8,128)S(1)} %copy.77, ...), kind=kLoop, calls=%fused_computation.220 | loop fusion | flops 4095999 | bytes 6717440
  34.8 0.1 collective-permute-done
  35.0 0.3 fusion.59
  35.3 0.7 copy-done.1
  36.0 0.1 fusion.110
  36.0 0.1 copy-done.3
  36.2 0.1 fusion.106
  36.3 0.1 fusion.99
  36.3 0.1 fusion.93
  36.5 0.1 bitcast_dynamic-update-slice_fusion.1
  36.6 1.0 copy-done.4
  37.5 0.2 multiply_add_fusion.1
  37.7 0.1 fusion.125
  37.8 1.0 fusion.126
  38.8 2.3 %copy.84 = f32[5,16,16,3]{2,1,3,0:T(8,128)} copy(f32[5,16,16,3]{3,2,1,0:T(8,128)} %get-tuple-element.10) | data formatting | bytes 30720 | tf_op jit(solution)/shard_map/slice | solution.py:19
  41.1 1.3 %collective-permute-start.10 = (f32[5,16,16,3]{2,1,3,0:T(8,128)}, f32[5,16,16,3]{2,1,3,0:T(8,128)}, u32[]{:S(2)}, u32[]{:S(2)}) collective-permute-start(f32[5,16,16,3]{2,1,3,0:T(8,128)} %copy.84), channel_id=1, source_target_pairs={{1,0},{3,2},{5,4},{7,6},{9,8},{11,10},{13,12},{15,14},{17,16},{19,... | collective-permute-start | bytes 46088 | tf_op jit(solution)/shard_map/ppermute | solution.py:25
  42.4 1.2 %copy.86 = f32[5,16,16,3]{2,1,3,0:T(8,128)} copy(f32[5,16,16,3]{3,2,1,0:T(8,128)S(1)} %get-tuple-element.11) | data formatting | bytes 30720 | tf_op jit(solution)/shard_map/slice | solution.py:20
  43.7 4.3 %collective-permute-start.11 = (f32[5,16,16,3]{2,1,3,0:T(8,128)}, f32[5,16,16,3]{2,1,3,0:T(8,128)}, u32[]{:S(2)}, u32[]{:S(2)}) collective-permute-start(f32[5,16,16,3]{2,1,3,0:T(8,128)} %copy.86), channel_id=1, source_target_pairs={{0,1},{2,3},{4,5},{6,7},{8,9},{10,11},{12,13},{14,15},{16,17},{18,... | collective-permute-start | bytes 46088 | tf_op jit(solution)/shard_map/ppermute | solution.py:23
  48.0 0.7 fusion.124
  48.7 0.7 copy.80
  49.3 1.3 %collective-permute-start.8 = (f32[5,16,3,128]{3,1,2,0:T(8,128)}, f32[5,16,3,128]{3,1,2,0:T(8,128)S(1)}, u32[]{:S(2)}, u32[]{:S(2)}) collective-permute-start(f32[5,16,3,128]{3,1,2,0:T(8,128)} %copy.80), channel_id=1, source_target_pairs={{2,0},{3,1},{6,4},{7,5},{10,8},{11,9},{14,12},{15,13},{18,16},{19,... | collective-permute-start | bytes 368648 | tf_op jit(solution)/shard_map/ppermute | solution.py:25
  50.6 0.7 copy.82
  51.3 5.2 %collective-permute-start.9 = (f32[5,16,3,128]{3,1,2,0:T(8,128)}, f32[5,16,3,128]{3,1,2,0:T(8,128)}, u32[]{:S(2)}, u32[]{:S(2)}) collective-permute-start(f32[5,16,3,128]{3,1,2,0:T(8,128)} %copy.82), channel_id=1, source_target_pairs={{0,2},{1,3},{4,6},{5,7},{8,10},{9,11},{12,14},{13,15},{16,18},{17,... | collective-permute-start | bytes 368648 | tf_op jit(solution)/shard_map/ppermute | solution.py:23
  56.5 1.3 %collective-permute-start.6 = (f32[5,3,16,128]{3,2,1,0:T(8,128)}, f32[5,3,16,128]{3,2,1,0:T(8,128)S(1)}, u32[]{:S(2)}, u32[]{:S(2)}) collective-permute-start(f32[5,3,16,128]{3,2,1,0:T(8,128)} %get-tuple-element.6), channel_id=1, source_target_pairs={{4,0},{8,4},{12,8},{16,12},{20,16},{24,20},{28,24},{5,1},{9,5},{13... | collective-permute-start | bytes 368648 | tf_op jit(solution)/shard_map/ppermute | solution.py:25
  57.8 5.7 %collective-permute-start.7 = (f32[5,3,16,128]{3,2,1,0:T(8,128)}, f32[5,3,16,128]{3,2,1,0:T(8,128)}, u32[]{:S(2)}, u32[]{:S(2)}) collective-permute-start(f32[5,3,16,128]{3,2,1,0:T(8,128)} %get-tuple-element.7), channel_id=1, source_target_pairs={{0,4},{4,8},{8,12},{12,16},{16,20},{20,24},{24,28},{1,5},{5,9},{9,... | collective-permute-start | bytes 368648 | tf_op jit(solution)/shard_map/ppermute | solution.py:23
  63.5 1.4 %copy.85 = f32[5,16,16,3]{3,2,1,0:T(8,128)S(1)} copy(f32[5,16,16,3]{2,1,3,0:T(8,128)} %collective-permute-done.10) | data formatting | bytes 30720 | tf_op jit(solution)/shard_map/ppermute | solution.py:25
  64.9 2.3 %copy.87 = f32[5,16,16,3]{3,2,1,0:T(8,128)} copy(f32[5,16,16,3]{2,1,3,0:T(8,128)} %collective-permute-done.11) | data formatting | bytes 30720 | tf_op jit(solution)/shard_map/ppermute | solution.py:23
  67.2 3.6 %fusion.32 = f32[5,16,16,128]{3,2,1,0:T(8,128)S(1)} fusion(f32[5,16,16,3]{3,2,1,0:T(8,128)} %copy.87, f32[5,16,16,128]{3,2,1,0:T(8,128)S(1)} %multiply_add_fusion.1, f32[5,16,16,3]{3,2,1,0:T(8,128)S(1)} %copy.85), kind=kLoop, calls=%fused_computation.69 | loop fusion | flops 2293760 | bytes 1341440 | tf_op jit(solution)/shard_map/add | solution.py:38
  70.8 0.1 copy.81
  70.9 1.0 copy.83
  71.9 1.8 %fusion.4 = (f32[5,16,16,128]{3,2,1,0:T(8,128)S(1)}, f32[5,16,16,128]{3,2,1,0:T(8,128)S(1)}) fusion(f32[5,16,16,128]{3,2,1,0:T(8,128)S(1)} %multiply_add_fusion.1, f32[5,3,16,128]{3,2,1,0:T(8,128)} %collective-permute-done.7, f32[5,3,16,128]{3,2,1,0:T(8,128)S(1)} %collective-permute-done.6, f32[5,16,3,128]{3,2,1,0:T(4,128)S(1)} %copy.83, ...), kind=kLoop, calls=%fused_computation.41 | loop fusion | flops 4587520 | bytes 2457600 | tf_op jit(solution)/shard_map/add | solution.py:38
  73.8 0.1 fusion.82
  73.8 0.1 fusion.75
  73.9 0.1 fusion.69
  74.0 0.1 bitcast_dynamic-update-slice_fusion
  74.1 1.0 copy-done.5
  75.1 0.2 multiply_add_fusion
  75.5 0.3 fusion.119
  75.7 13.0 %all_to_all.5 = f32[8,8,640]{2,1,0:T(8,128)S(1)} all-to-all(f32[8,8,640]{2,1,0:T(8,128)S(1)} %fusion.119), channel_id=1, replica_groups=mesh['ax'=8,'ty'=2,'tz'=2] {'ax'}, dimensions={0} | all-to-all | bytes 327680 | tf_op jit(solution)/shard_map/all_to_all | solution.py:92
  88.7 0.3 convolution_reduce_fusion
  89.1 0.3 copy.90
  89.3 0.8 bitcast_reduce_fusion
  90.2 16.6 %reduce-scatter.4.cloned.1.call-done = f32[32,5]{1,0:T(8,128)} async-done(((f32[128,5]{1,0:T(8,128)}), f32[32,5]{1,0:T(8,128)}) %reduce-scatter.4.cloned.1.call-update) | async-done | bytes 656
  106.8 0.8 reshape_bitcast_fusion
  107.6 0.7 copy.91
  (41 shorter events, 0.4 us)
Async XLA Ops:
  7.2 81.6 %copy-start = (f32[1,128,128]{2,1,0:T(8,128)S(1)}, f32[1,128,128]{2,1,0:T(8,128)}, u32[]{:S(2)}) copy-start(f32[1,128,128]{2,1,0:T(8,128)} %param.12) | copy-start | bytes 196612
  7.2 2.6 %copy-start.2 = (f32[5,16,16,128]{3,2,1,0:T(8,128)S(1)}, f32[5,16,16,128]{3,2,1,0:T(8,128)}, u32[]{:S(2)}) copy-start(f32[5,16,16,128]{3,2,1,0:T(8,128)} %param.7) | copy-start | bytes 1966084
  7.2 99.6 %reduce-scatter.4.cloned.1.call-start = ((), (), s32[]{:S(2)}) async-start(), calls=%async_computation.2 | async-start | bytes 81920
  8.4 23.8 %collective-permute-start.2 = (f32[5,16,3,128]{3,1,2,0:T(8,128)S(1)}, f32[5,16,3,128]{3,1,2,0:T(8,128)S(1)}, u32[]{:S(2)}, u32[]{:S(2)}) collective-permute-start(f32[5,16,3,128]{3,1,2,0:T(8,128)S(1)} %copy.92), channel_id=1, source_target_pairs={{2,0},{3,1},{6,4},{7,5},{10,8},{11,9},{14,12},{15,13},{18,16},{19,... | collective-permute-start | bytes 368648 | tf_op jit(solution)/shard_map/ppermute | solution.py:25
  10.0 17.6 %copy-start.9 = (s32[1,1,1,32,1]{3,4,2,1,0:T(1,128)S(1)}, s32[1,1,1,32,1]{3,4,2,1,0:T(1,128)}, u32[]{:S(2)}) copy-start(s32[1,1,1,32,1]{3,4,2,1,0:T(1,128)} %param.13) | copy-start | bytes 388
  10.6 17.4 %collective-permute-start.4 = (f32[5,16,16,3]{2,1,3,0:T(8,128)S(1)}, f32[5,16,16,3]{2,1,3,0:T(8,128)S(1)}, u32[]{:S(2)}, u32[]{:S(2)}) collective-permute-start(f32[5,16,16,3]{2,1,3,0:T(8,128)S(1)} %copy.94), channel_id=1, source_target_pairs={{1,0},{3,2},{5,4},{7,6},{9,8},{11,10},{13,12},{15,14},{17,16},{19,... | collective-permute-start | bytes 46088 | tf_op jit(solution)/shard_map/ppermute | solution.py:25
  12.5 17.4 %collective-permute-start.5 = (f32[5,16,16,3]{2,1,3,0:T(8,128)S(1)}, f32[5,16,16,3]{2,1,3,0:T(8,128)}, u32[]{:S(2)}, u32[]{:S(2)}) collective-permute-start(f32[5,16,16,3]{2,1,3,0:T(8,128)S(1)} %copy.95), channel_id=1, source_target_pairs={{0,1},{2,3},{4,5},{6,7},{8,9},{10,11},{12,13},{14,15},{16,17},{18,... | collective-permute-start | bytes 46088 | tf_op jit(solution)/shard_map/ppermute | solution.py:23
  16.9 15.4 %collective-permute-start.1 = (f32[5,3,16,128]{3,2,1,0:T(8,128)}, f32[5,3,16,128]{3,2,1,0:T(8,128)S(1)}, u32[]{:S(2)}, u32[]{:S(2)}) collective-permute-start(f32[5,3,16,128]{3,2,1,0:T(8,128)} %get-tuple-element.13), channel_id=1, source_target_pairs={{0,4},{4,8},{8,12},{12,16},{16,20},{20,24},{24,28},{1,5},{5,9},{9,... | collective-permute-start | bytes 368648 | tf_op jit(solution)/shard_map/ppermute | solution.py:23
  22.4 8.9 %collective-permute-start.3 = (f32[5,16,3,128]{3,1,2,0:T(8,128)}, f32[5,16,3,128]{3,1,2,0:T(8,128)}, u32[]{:S(2)}, u32[]{:S(2)}) collective-permute-start(f32[5,16,3,128]{3,1,2,0:T(8,128)} %copy.93), channel_id=1, source_target_pairs={{0,2},{1,3},{4,6},{5,7},{8,10},{9,11},{12,14},{13,15},{16,18},{17,... | collective-permute-start | bytes 368648 | tf_op jit(solution)/shard_map/ppermute | solution.py:23
  28.0 7.0 %collective-permute-start = (f32[5,3,16,128]{3,2,1,0:T(8,128)}, f32[5,3,16,128]{3,2,1,0:T(8,128)S(1)}, u32[]{:S(2)}, u32[]{:S(2)}) collective-permute-start(f32[5,3,16,128]{3,2,1,0:T(8,128)} %get-tuple-element.12), channel_id=1, source_target_pairs={{4,0},{8,4},{12,8},{16,12},{20,16},{24,20},{28,24},{5,1},{9,5},{13... | collective-permute-start | bytes 368648 | tf_op jit(solution)/shard_map/ppermute | solution.py:25
  35.0 1.0 copy-start.1
  35.2 0.9 copy-start.3
  36.4 1.1 copy-start.4
  36.4 1.1 copy-start.7
  41.1 16.6 %collective-permute-start.10 = (f32[5,16,16,3]{2,1,3,0:T(8,128)}, f32[5,16,16,3]{2,1,3,0:T(8,128)}, u32[]{:S(2)}, u32[]{:S(2)}) collective-permute-start(f32[5,16,16,3]{2,1,3,0:T(8,128)} %copy.84), channel_id=1, source_target_pairs={{1,0},{3,2},{5,4},{7,6},{9,8},{11,10},{13,12},{15,14},{17,16},{19,... | collective-permute-start | bytes 46088 | tf_op jit(solution)/shard_map/ppermute | solution.py:25
  43.7 21.3 %collective-permute-start.11 = (f32[5,16,16,3]{2,1,3,0:T(8,128)}, f32[5,16,16,3]{2,1,3,0:T(8,128)}, u32[]{:S(2)}, u32[]{:S(2)}) collective-permute-start(f32[5,16,16,3]{2,1,3,0:T(8,128)} %copy.86), channel_id=1, source_target_pairs={{0,1},{2,3},{4,5},{6,7},{8,9},{10,11},{12,13},{14,15},{16,17},{18,... | collective-permute-start | bytes 46088 | tf_op jit(solution)/shard_map/ppermute | solution.py:23
  49.3 21.5 %collective-permute-start.8 = (f32[5,16,3,128]{3,1,2,0:T(8,128)}, f32[5,16,3,128]{3,1,2,0:T(8,128)S(1)}, u32[]{:S(2)}, u32[]{:S(2)}) collective-permute-start(f32[5,16,3,128]{3,1,2,0:T(8,128)} %copy.80), channel_id=1, source_target_pairs={{2,0},{3,1},{6,4},{7,5},{10,8},{11,9},{14,12},{15,13},{18,16},{19,... | collective-permute-start | bytes 368648 | tf_op jit(solution)/shard_map/ppermute | solution.py:25
  51.3 19.6 %collective-permute-start.9 = (f32[5,16,3,128]{3,1,2,0:T(8,128)}, f32[5,16,3,128]{3,1,2,0:T(8,128)}, u32[]{:S(2)}, u32[]{:S(2)}) collective-permute-start(f32[5,16,3,128]{3,1,2,0:T(8,128)} %copy.82), channel_id=1, source_target_pairs={{0,2},{1,3},{4,6},{5,7},{8,10},{9,11},{12,14},{13,15},{16,18},{17,... | collective-permute-start | bytes 368648 | tf_op jit(solution)/shard_map/ppermute | solution.py:23
  56.5 15.4 %collective-permute-start.6 = (f32[5,3,16,128]{3,2,1,0:T(8,128)}, f32[5,3,16,128]{3,2,1,0:T(8,128)S(1)}, u32[]{:S(2)}, u32[]{:S(2)}) collective-permute-start(f32[5,3,16,128]{3,2,1,0:T(8,128)} %get-tuple-element.6), channel_id=1, source_target_pairs={{4,0},{8,4},{12,8},{16,12},{20,16},{24,20},{28,24},{5,1},{9,5},{13... | collective-permute-start | bytes 368648 | tf_op jit(solution)/shard_map/ppermute | solution.py:25
  57.8 14.1 %collective-permute-start.7 = (f32[5,3,16,128]{3,2,1,0:T(8,128)}, f32[5,3,16,128]{3,2,1,0:T(8,128)}, u32[]{:S(2)}, u32[]{:S(2)}) collective-permute-start(f32[5,3,16,128]{3,2,1,0:T(8,128)} %get-tuple-element.7), channel_id=1, source_target_pairs={{0,4},{4,8},{8,12},{12,16},{16,20},{20,24},{24,28},{1,5},{5,9},{9,... | collective-permute-start | bytes 368648 | tf_op jit(solution)/shard_map/ppermute | solution.py:23
  74.0 1.1 copy-start.5
  74.0 1.1 copy-start.8
  75.3 14.8 %copy-start.6 = (f32[5,16,16,128]{3,2,1,0:T(8,128)}, f32[5,16,16,128]{3,2,1,0:T(8,128)S(1)}, u32[]{:S(2)}) copy-start(f32[5,16,16,128]{3,2,1,0:T(8,128)S(1)} %multiply_add_fusion) | copy-start | bytes 1966084
Sparse Core Ops, SparseCore 0:
  90.3 16.4 reduce-scatter.3
where the time goes:
time: 116 us; the launch traced here: 115 us
  starting transfers between devices  36.7 us (32%)
  local copies, waits for them, and re-layouts  24 us (21%)
  waiting for transfers between devices  16.8 us (14%)
  between operations  14.4 us (12%)
  blocking collectives  13 us (11%)
  other arithmetic  9.65 us (8%)
    ppermute x6, starting transfers between devices, padded_2(): lax.ppermute(tail, axis, [(i, (i + 1) % count) for i in range(ends)])  29 us
    unnamed x2, waiting for transfers between devices  16.6 us
    all_to_all x1, blocking collectives, on_device(): lax.all_to_all(outgoing, 'ax', split_axis=0, concat_axis=0, tiled=True)  13 us
    ppermute x6, starting transfers between devices, padded_2(): lax.ppermute(head, axis, [((i + 1) % count, i) for i in range(ends)])  7.72 us
    unnamed x30, local copies, waits for them, and re-layouts  7.33 us
    slice x8, local copies, waits for them, and re-layouts, padded_2(): head = lax.slice_in_dim(cells, 0, width, axis=dim)  6.91 us
    ppermute x4, local copies, waits for them, and re-layouts, padded_2(): lax.ppermute(tail, axis, [(i, (i + 1) % count) for i in range(ends)])  5.65 us
    add x3, other arithmetic, difference(): summed = contrib if summed is None else summed + contrib  5.65 us
  transfers between devices with their start and end apart: 13, of which 2 were waited for; matrix products, arithmetic and copies ran while one was open for 18% of the time, Pallas kernels for 0%

commit v1 on v0

v1 whole, which is shorter than its diff:
```python
import functools
import math

import jax
import jax.numpy as jnp
import numpy as np
from jax import lax
from jax.experimental import pallas as pl
from jax.experimental.pallas import tpu as pltpu
from jax.sharding import PartitionSpec as P

FACE_PLANES = 2
TIME_STEP = 0.6
HALO = 3
WEIGHTS = {1: 45.0, 2: -9.0, 3: 1.0}
F32, BF16 = jnp.float32, jnp.bfloat16
VMEM = pl.BlockSpec(memory_space=pltpu.VMEM)
ANY = pl.BlockSpec(memory_space=pl.ANY)


def weight_of(offset):
    size = np.abs(offset)
    table = np.zeros(offset.shape, np.float32)
    for s, w in WEIGHTS.items():
        table = np.where(size == s, np.sign(offset) * w, table)
    return table


def tables(nx, ny, nz):
    y, z, layer, x = np.arange(ny), np.arange(nz), np.arange(HALO), np.eye(nx, dtype=np.float32)
    along_y = np.kron(x, weight_of(y[None, :] - y[:, None]))
    along_z = weight_of(z[:, None] - z[None, :])

    def from_rows(places):
        w = weight_of(places[None, :] - y[:, None])
        m = np.einsum("xp,yl->xylp", x, w)
        return m.reshape(nx * ny, HALO * nx)

    y_halo = np.stack([from_rows(ny + layer), from_rows(layer - HALO), np.zeros((nx * ny, HALO * nx))])
    z_halo = np.stack(
        [weight_of(z[:, None] + nz - z[None, :]), weight_of(z[:, None] - nz - z[None, :]), np.zeros((nz, nz))]
    )
    twice = lambda m, axis: np.concatenate([m, m], axis=axis)
    return [
        jnp.asarray(m, BF16)
        for m in (along_y, twice(along_z, 0), twice(y_halo, 2), twice(z_halo, 1))
    ]


def halves(v):
    high = v.astype(BF16)
    return high, (v - high.astype(F32)).astype(BF16)


def dot(a, b):
    return jnp.dot(a, b, preferred_element_type=F32)


def couple(acc, u, c, d, grad):
    acc = [acc[k] + u * grad[k] for k in range(5)]
    acc[1 + d] = acc[1 + d] + c * grad[4]
    acc[4] = acc[4] + c * grad[1 + d]
    return acc


def pack(v_ref, xlo_ref, xhi_ref, y_refs, position, count):
    nx, ny = v_ref.shape[1:3]
    xlo_ref[...] = v_ref[:, :HALO]
    xhi_ref[...] = v_ref[:, nx - HALO :]

    def rows(ref, start):
        for k in range(5):
            for l in range(HALO):
                ref[k, l] = v_ref[k, :, start + l, :]

    if count == 2:

        @pl.when(position == 0)
        def _():
            rows(y_refs[0], ny - HALO)

        @pl.when(position != 0)
        def _():
            rows(y_refs[0], 0)
    else:
        rows(y_refs[0], 0)
        rows(y_refs[1], ny - HALO)


def pack_kernel(count, v_ref, xlo_ref, xhi_ref, *y_refs):
    pack(v_ref, xlo_ref, xhi_ref, y_refs, lax.axis_index("ty"), count)


def local_kernel(scale, second, *refs):
    if second:
        _, adj_ref, v_ref, vel_ref, c_ref, sponge_ref, source_ref, ay_ref, bz_ref, out_ref, dy, dz = refs
    else:
        _, v_ref, vel_ref, c_ref, sponge_ref, source_ref, ay_ref, bz_ref, out_ref, dy, dz = refs
        adj_ref = None
    nx, ny, nz = v_ref.shape[1:]
    for k in range(5):
        high, low = halves(v_ref[k].reshape(nx * ny, nz))
        dz[k] = dot(jnp.concatenate([high, low], axis=1), bz_ref[...]).reshape(nx, ny, nz)
        dy[k] = (dot(ay_ref[...], high) + dot(ay_ref[...], low)).reshape(nx, ny, nz)
    part = scale / 60.0
    for x in range(nx):
        c = c_ref[x] * part
        u = [vel_ref[d, x] * part for d in range(3)]
        damp = sponge_ref[x] * scale
        acc, gx, gy, gz = [], [], [], []
        for k in range(5):
            cur = v_ref[k, x]
            base = cur if adj_ref is None else 0.5 * (adj_ref[k, x] + cur)
            acc.append(base + (scale * source_ref[k, x] - damp * cur))
            total = None
            for s, w in WEIGHTS.items():
                diff = None
                if x + s < nx and x - s >= 0:
                    diff = v_ref[k, x + s] - v_ref[k, x - s]
                elif x + s < nx:
                    diff = v_ref[k, x + s]
                elif x - s >= 0:
                    diff = -v_ref[k, x - s]
                if diff is not None:
                    diff = diff if w == 1.0 else w * diff
                    total = diff if total is None else total + diff
            gx.append(total)
            gy.append(dy[k, x])
            gz.append(dz[k, x])
        for d, g in enumerate((gx, gy, gz)):
            acc = couple(acc, u[d], c, d, g)
        for k in range(5):
            out_ref[k, x] = acc[k]


def edge_flags():
    at, count = lax.axis_index("ax"), lax.axis_size("ax")
    return (at > 0).astype(F32), (at < count - 1).astype(F32)


def side_of(axis):
    at, count = lax.axis_index(axis), lax.axis_size(axis)
    if count == 2:
        return [at]
    return [jnp.where(at > 0, 1, 2), jnp.where(at < count - 1, 0, 2)]


def add_halos(scale, part_ref, vel_ref, c_ref, from_lo, from_hi, y_blocks, z_blocks, py_ref, wz_ref, dy, dz, out_ref):
    nx, ny, nz = part_ref.shape[1:]
    y_sides, z_sides = side_of("ty"), side_of("tz")
    has_lo, has_hi = edge_flags()
    for k in range(5):
        total = None
        for ref, side in zip(y_blocks, y_sides):
            high, low = halves(ref[k].reshape(HALO * nx, nz))
            term = dot(py_ref[side], jnp.concatenate([high, low], axis=0))
            total = term if total is None else total + term
        dy[k] = total.reshape(nx, ny, nz)
        total = None
        for ref, side in zip(z_blocks, z_sides):
            high, low = halves(ref[k].reshape(nx * ny, nz))
            term = dot(jnp.concatenate([high, low], axis=1), wz_ref[side])
            total = term if total is None else total + term
        dz[k] = total.reshape(nx, ny, nz)
    part = scale / 60.0
    for x in range(nx):
        c = c_ref[x] * part
        acc = [part_ref[k, x] for k in range(5)]
        for ref, has, places in ((from_lo, has_lo, range(-HALO, 0)), (from_hi, has_hi, range(nx, nx + HALO))):
            near = [(l, p - x) for l, p in enumerate(places) if abs(p - x) <= HALO]
            if near:
                grad = []
                for k in range(5):
                    total = None
                    for l, off in near:
                        w = WEIGHTS[abs(off)] * (1.0 if off > 0 else -1.0)
                        term = ref[k, l] * w
                        total = term if total is None else total + term
                    grad.append(total)
                keep = part * has
                acc = couple(acc, vel_ref[0, x] * keep, c_ref[x] * keep, 0, grad)
        acc = couple(acc, vel_ref[1, x] * part, c, 1, [dy[k, x] for k in range(5)])
        acc = couple(acc, vel_ref[2, x] * part, c, 2, [dz[k, x] for k in range(5)])
        for k in range(5):
            out_ref[k, x] = acc[k]


def halo_kernel(scale, ny_blocks, nz_blocks, last, *refs):
    refs = list(refs)
    part_ref, vel_ref, c_ref, from_lo, from_hi = refs[:5]
    y_blocks, refs = refs[5 : 5 + ny_blocks], refs[5 + ny_blocks :]
    z_blocks, refs = refs[:nz_blocks], refs[nz_blocks:]
    if last:
        py_ref, wz_ref, owner_ref, out_ref, sums_ref, dy, dz = refs
    else:
        py_ref, wz_ref, out_ref, xlo_ref, xhi_ref = refs[:5]
        y_refs, (dy, dz) = refs[5:-2], refs[-2:]
    add_halos(scale, part_ref, vel_ref, c_ref, from_lo, from_hi, y_blocks, z_blocks, py_ref, wz_ref, dy, dz, out_ref)
    if not last:
        pack(out_ref, xlo_ref, xhi_ref, y_refs, lax.axis_index("ty"), lax.axis_size("ty"))
        return
    ny, nz = out_ref.shape[2:]
    devices = sums_ref.shape[0]
    each = devices // lax.axis_size("ax")
    blocks = FACE_PLANES * ny
    place = lax.broadcasted_iota(jnp.int32, (blocks, devices), 1) // each
    choose = (owner_ref[...] == place).astype(F32)
    sums_ref[...] = jnp.zeros(sums_ref.shape, F32)
    for k in range(5):
        rows = out_ref[k, :FACE_PLANES].reshape(blocks, nz)
        sums_ref[:, k, :] = lax.dot_general(
            choose, rows, (((0,), (0,)), ((), ())), precision=lax.Precision.HIGHEST, preferred_element_type=F32
        )


def modes_kernel(scale, sums_ref, basis_ref, out_ref):
    share = out_ref.shape[2]
    total = sums_ref[0]
    for i in range(1, sums_ref.shape[0]):
        total = total + sums_ref[i]
    modes = lax.dot_general(
        total, basis_ref[0], (((1,), (0,)), ((), ())), precision=lax.Precision.HIGHEST, preferred_element_type=F32
    )
    mine = lax.axis_index("ty") * lax.axis_size("tz") + lax.axis_index("tz")
    width = modes.shape[1]
    modes = pltpu.roll(modes * scale, lax.rem(width - mine * share, width), 1)
    out_ref[0] = modes[:5, :share]


def ring(v, axis, step):
    count = lax.axis_size(axis)
    return lax.ppermute(v, axis, [(i, (i + step) % count) for i in range(count)])


def exchange(v, xlo, xhi, ys):
    below, above = ring(xhi, "ax", 1), ring(xlo, "ax", -1)
    if lax.axis_size("ty") == 2:
        y_blocks = [ring(ys[0], "ty", 1)]
    else:
        y_blocks = [ring(ys[1], "ty", 1), ring(ys[0], "ty", -1)]
    if lax.axis_size("tz") == 2:
        z_blocks = [ring(v, "tz", 1)]
    else:
        z_blocks = [ring(v, "tz", 1), ring(v, "tz", -1)]
    return below, above, y_blocks, z_blocks


def call(kernel, args, outs, scratch=(), specs=None, flops=0):
    moved = sum(4 * math.prod(a.shape) for a in (*args, *outs))
    return pl.pallas_call(
        kernel,
        out_shape=list(outs),
        in_specs=specs or [VMEM] * len(args),
        out_specs=[VMEM] * len(outs),
        scratch_shapes=list(scratch),
        cost_estimate=pl.CostEstimate(flops=flops, bytes_accessed=moved, transcendentals=0),
        compiler_params=pltpu.CompilerParams(vmem_limit_bytes=48 << 20),
    )(*args)


def on_device(adjoint, velocity, sound_speed, sponge, source, mode_basis, block_owner):
    nx, ny, nz = adjoint.shape[1:]
    n_ax, n_ty, n_tz = (lax.axis_size(a) for a in ("ax", "ty", "tz"))
    ay, bz, py, wz = tables(nx, ny, nz)
    shape = lambda *s: jax.ShapeDtypeStruct(s, F32)
    brick = shape(5, nx, ny, nz)
    side_x, side_y = shape(5, HALO, ny, nz), shape(5, HALO, nx, nz)
    sides = [side_x, side_x] + [side_y] * (1 if n_ty == 2 else 2)
    grads = [pltpu.VMEM((5, nx, ny, nz), F32)] * 2
    work = 5 * nx * ny * nz * 800

    xlo, xhi, *ys = call(functools.partial(pack_kernel, n_ty), [adjoint], sides)
    below, above, y_blocks, z_blocks = exchange(adjoint, xlo, xhi, ys)
    rest = [velocity, sound_speed, sponge, source, ay, bz]
    args = [xlo, adjoint, *rest]
    (part,) = call(
        functools.partial(local_kernel, TIME_STEP, False), args, [brick], grads, [ANY] + [VMEM] * (len(args) - 1), work
    )
    args = [part, velocity, sound_speed, below, above, *y_blocks, *z_blocks, py, wz]
    mid, xlo, xhi, *ys = call(
        functools.partial(halo_kernel, TIME_STEP, len(y_blocks), len(z_blocks), False),
        args,
        [brick, *sides],
        grads,
        flops=work // 2,
    )
    below, above, y_blocks, z_blocks = exchange(mid, xlo, xhi, ys)
    args = [xlo, adjoint, mid, *rest]
    (part,) = call(
        functools.partial(local_kernel, 0.5 * TIME_STEP, True), args, [brick], grads, [ANY] + [VMEM] * (len(args) - 1), work
    )
    devices = n_ax * n_ty * n_tz
    owners = block_owner.reshape(FACE_PLANES * ny, 1)
    args = [part, velocity, sound_speed, below, above, *y_blocks, *z_blocks, py, wz, owners]
    adjoint_out, sums = call(
        functools.partial(halo_kernel, 0.5 * TIME_STEP, len(y_blocks), len(z_blocks), True),
        args,
        [brick, shape(devices, 8, nz)],
        grads,
        flops=work // 2,
    )
    sums = lax.all_to_all(sums, ("ax", "ty", "tz"), split_axis=0, concat_axis=0, tiled=True)
    share = mode_basis.shape[2] // (n_ty * n_tz)
    scale = 1.0 / math.sqrt(FACE_PLANES * ny * n_ty * n_tz)
    (sensitivity,) = call(functools.partial(modes_kernel, scale), [sums, mode_basis], [shape(1, 5, share)])
    return (adjoint_out, sensitivity)


def solution(mesh):
    return jax.shard_map(
        on_device,
        mesh=mesh,
        in_specs=(
            P(None, "ax", "ty", "tz"),
            P(None, "ax", "ty", "tz"),
            P("ax", "ty", "tz"),
            P("ax", "ty", "tz"),
            P(None, "ax", "ty", "tz"),
            P("ax", None, None),
            P("ax", "ty", "tz", None, None),
        ),
        out_specs=(P(None, "ax", "ty", "tz"), P("ax", None, ("ty", "tz"))),
        check_vma=False,
    )
```

time: 116 us -> 42.3 us (0.36)
  starting transfers between devices: 36.7 us -> 11.2 us
  local copies, waits for them, and re-layouts: 24 us -> 7.92 us
  between operations: 14.4 us -> 0.74 us
  waiting for transfers between devices: 16.8 us -> 5.47 us
  other arithmetic: 9.65 us -> 0 us
  Pallas kernels: 0 us -> 5.75 us
  blocking collectives: 13 us -> 10.9 us
    ppermute x12 -> x8, starting transfers between devices: 36.7 us -> 11.2 us  [ring(): lax.ppermute(v, axis, [(i, (i + step) % count) for i in range(count)])]
    unnamed x2 -> x0, waiting for transfers between devices: 16.6 us -> none
    slice x10 -> x0, local copies, waits for them, and re-layouts: 8.8 us -> none  [the longest x8 6.91 us: padded_2(): head = lax.slice_in_dim(cells, 0, width, axis=dim)]
    ppermute x7 -> x0, local copies, waits for them, and re-layouts: 7.69 us -> none  [the longest x4 5.65 us: padded_2(): lax.ppermute(tail, axis, [(i, (i + 1) % count) for i in range(ends)])]
    add x6 -> x0, other arithmetic: 6.09 us -> none  [the longest x3 5.65 us: difference(): summed = contrib if summed is None else summed + contrib]
    pallas_call x0 -> x6, Pallas kernels: none -> 5.75 us  [call(): pl.pallas_call(kernel, out_shape=list(outs), in_specs=specs or [VMEM] * l...]
    ppermute x12 -> x8, waiting for transfers between devices: 0.15 us -> 5.47 us  [ring(): lax.ppermute(v, axis, [(i, (i + step) % count) for i in range(count)])]
    unnamed x9 -> x0, other arithmetic: 3.05 us -> none
  transfers between devices with their start and end apart: 13 -> 8, of which waited for: 2 -> 2; matrix products, arithmetic and copies ran while one was open for 18% -> 2% of each run, Pallas kernels for 0% -> 4%
where the time goes in v1:
time: 42.3 us; the launch traced here: 41.9 us
  starting transfers between devices  11.2 us (26%)
  blocking collectives  10.9 us (26%)
  local copies, waits for them, and re-layouts  7.92 us (19%)
  Pallas kernels  5.75 us (14%)
  waiting for transfers between devices  5.47 us (13%)
  between operations  0.74 us (2%)
    ppermute x8, starting transfers between devices, ring(): lax.ppermute(v, axis, [(i, (i + step) % count) for i in range(count)])  11.2 us
    all_to_all x1, blocking collectives, on_device(): lax.all_to_all(sums, ('ax', 'ty', 'tz'), split_axis=0, concat_axis=0, til...  10.9 us
    unnamed x31, local copies, waits for them, and re-layouts  7.19 us
    pallas_call x6, Pallas kernels, call(): pl.pallas_call(kernel, out_shape=list(outs), in_specs=specs or [VMEM] * l...  5.75 us
    ppermute x8, waiting for transfers between devices, ring(): lax.ppermute(v, axis, [(i, (i + step) % count) for i in range(count)])  5.47 us
  transfers between devices with their start and end apart: 8, of which 2 were waited for; matrix products, arithmetic and copies ran while one was open for 2% of the time, Pallas kernels for 4%

profile of v1, /device:TPU:0, one launch (start us, length us, event | category | flops | bytes accessed | tf_op | source)
XLA Modules:
  0.0 41.9 jit_solution(14650360912014435476)
XLA Ops:
  0.6 0.0 copy-start
  0.6 0.5 %collective-permute-start.3 = (f32[5,16,16,128]{3,2,1,0:T(8,128)}, f32[5,16,16,128]{3,2,1,0:T(8,128)S(1)}, u32[]{:S(2)}, u32[]{:S(2)}) collective-permute-start(f32[5,16,16,128]{3,2,1,0:T(8,128)} %refs_1_.6), channel_id=1, source_target_pairs={{0,1},{1,0},{2,3},{3,2},{4,5},{5,4},{6,7},{7,6},{8,9},{9,8},{10,11... | collective-permute-start | bytes 1966088 | tf_op jit(solution)/shard_map/ppermute | solution.py:232
  1.2 0.0 copy-start.1
  1.2 1.1 %copy-done.1 = f32[5,16,16,128]{3,2,1,0:T(8,128)S(1)} copy-done((f32[5,16,16,128]{3,2,1,0:T(8,128)S(1)}, f32[5,16,16,128]{3,2,1,0:T(8,128)}, u32[]{:S(2)}) %copy-start.1) | copy-done | bytes 655384
  2.2 0.0 copy-start.5
  2.2 0.0 copy-start.8
  2.2 0.1 shard_map.122
  2.3 5.7 %collective-permute-start.1 = (f32[5,3,16,128]{3,2,1,0:T(8,128)S(1)}, f32[5,3,16,128]{3,2,1,0:T(8,128)S(1)}, u32[]{:S(2)}, u32[]{:S(2)}) collective-permute-start(f32[5,3,16,128]{3,2,1,0:T(8,128)S(1)} %get-tuple-element.11.refs_0_), channel_id=1, source_target_pairs={{0,28},{4,0},{8,4},{12,8},{16,12},{20,16},{24,20},{28,24},{1,29},{... | collective-permute-start | bytes 368648 | tf_op jit(solution)/shard_map/ppermute | solution.py:232
  8.0 0.0 collective-permute-start
  8.0 1.5 %collective-permute-start.2 = (f32[5,3,16,128]{3,2,1,0:T(8,128)S(1)}, f32[5,3,16,128]{3,2,1,0:T(8,128)S(1)}, u32[]{:S(2)}, u32[]{:S(2)}) collective-permute-start(f32[5,3,16,128]{3,2,1,0:T(8,128)S(1)} %get-tuple-element.13), channel_id=1, source_target_pairs={{0,2},{2,0},{1,3},{3,1},{4,6},{6,4},{5,7},{7,5},{8,10},{10,8},{9,1... | collective-permute-start | bytes 368648 | tf_op jit(solution)/shard_map/ppermute | solution.py:232
  9.5 0.0 copy-done
  9.5 0.0 copy-done.5
  9.5 0.0 copy-done.8
  9.5 0.0 copy-start.3
  9.5 1.1 %copy-done.3 = f32[5,16,16,128]{3,2,1,0:T(8,128)S(1)} copy-done((f32[5,16,16,128]{3,2,1,0:T(8,128)S(1)}, f32[5,16,16,128]{3,2,1,0:T(8,128)}, u32[]{:S(2)}) %copy-start.3) | copy-done | bytes 655384
  10.6 0.0 copy-start.10
  10.6 0.9 %copy-done.10 = bf16[256,256]{1,0:T(8,128)(2,1)S(1)} copy-done((bf16[256,256]{1,0:T(8,128)(2,1)S(1)}, bf16[256,256]{1,0:T(8,128)(2,1)}, u32[]{:S(2)}) %copy-start.10) | copy-done | bytes 131096
  11.5 0.0 copy-start.12
  11.5 0.8 %copy-done.12 = bf16[256,128]{1,0:T(8,128)(2,1)S(1)} copy-done((bf16[256,128]{1,0:T(8,128)(2,1)S(1)}, bf16[256,128]{1,0:T(8,128)(2,1)}, u32[]{:S(2)}) %copy-start.12) | copy-done | bytes 65560
  12.3 0.0 copy-start.6
  12.3 0.0 copy-start.7
  12.3 0.9 %shard_map.123.refs_0_ = f32[5,16,16,128]{3,2,1,0:T(8,128)S(1)} custom-call(f32[5,3,16,128]{3,2,1,0:T(8,128)S(1)} %get-tuple-element.11.refs_0_, f32[5,16,16,128]{3,2,1,0:T(8,128)S(1)} %copy-done.1, f32[3,16,16,128]{3,2,1,0:T(8,128)S(1)} %copy-done, f32[16,16,128]{2,1,0:T(8,128)S(1)} %copy-done.5, f32[16,16,128]{2,1,0:T(8,128)S(1)} %copy-done.8, ...), custom_call_target="tpu_custom_call" | custom-call | flops 131072000 | bytes 3137536 | tf_op jit(solution)/shard_map/pallas_call | solution.py:250
  13.2 0.0 copy-start.2
  13.2 0.0 copy-start.4
  13.3 0.0 collective-permute-done.1.refs_4_
  13.3 2.8 %collective-permute-done.refs_3_ = f32[5,3,16,128]{3,2,1,0:T(8,128)S(1)} collective-permute-done((f32[5,3,16,128]{3,2,1,0:T(8,128)S(1)}, f32[5,3,16,128]{3,2,1,0:T(8,128)S(1)}, u32[]{:S(2)}, u32[]{:S(2)}) %collective-permute-start) | collective-permute-done | bytes 122912 | tf_op jit(solution)/shard_map/ppermute | solution.py:232
  16.1 0.0 collective-permute-done.2.refs_5_
  16.1 0.0 collective-permute-done.3.refs_6_
  16.1 0.0 copy-done.6
  16.1 0.0 copy-done.7
  16.1 1.3 %shard_map.124 = (f32[5,16,16,128]{3,2,1,0:T(8,128)S(1)}, f32[5,3,16,128]{3,2,1,0:T(8,128)}, f32[5,3,16,128]{3,2,1,0:T(8,128)}, f32[5,3,16,128]{3,2,1,0:T(8,128)}) custom-call(f32[5,16,16,128]{3,2,1,0:T(8,128)S(1)} %shard_map.123.refs_0_, f32[3,16,16,128]{3,2,1,0:T(8,128)S(1)} %copy-done, f32[16,16,128]{2,1,0:T(8,128)S(1)} %copy-done.5, ...), custom_call_target="tpu_custom_call" | custom-call | flops 65536000 | bytes 3915776 | tf_op jit(solution)/shard_map/pallas_call | solution.py:250
  17.4 0.0 collective-permute-start.7
  17.4 1.9 %collective-permute-start.5 = (f32[5,3,16,128]{3,2,1,0:T(8,128)}, f32[5,3,16,128]{3,2,1,0:T(8,128)}, u32[]{:S(2)}, u32[]{:S(2)}) collective-permute-start(f32[5,3,16,128]{3,2,1,0:T(8,128)} %get-tuple-element.14.refs_0_), channel_id=1, source_target_pairs={{0,28},{4,0},{8,4},{12,8},{16,12},{20,16},{24,20},{28,24},{1,29},{... | collective-permute-start | bytes 368648 | tf_op jit(solution)/shard_map/ppermute | solution.py:232
  19.3 0.1 collective-permute-start.4
  19.4 1.5 %collective-permute-start.6 = (f32[5,3,16,128]{3,2,1,0:T(8,128)}, f32[5,3,16,128]{3,2,1,0:T(8,128)}, u32[]{:S(2)}, u32[]{:S(2)}) collective-permute-start(f32[5,3,16,128]{3,2,1,0:T(8,128)} %get-tuple-element.17), channel_id=1, source_target_pairs={{0,2},{2,0},{1,3},{3,1},{4,6},{6,4},{5,7},{7,5},{8,10},{10,8},{9,1... | collective-permute-start | bytes 368648 | tf_op jit(solution)/shard_map/ppermute | solution.py:232
  20.9 0.7 %copy.13.refs_9_ = s32[32,1]{1,0:T(8,128)S(1)} copy(s32[32,1]{0,1:T(1,128)} %bitcast.1) | data formatting | bytes 256 | tf_op jit(solution)/shard_map/reshape | solution.py:293
  21.7 0.0 copy-done.2
  21.7 0.0 copy-done.4
  21.7 0.0 copy-start.9
  21.7 0.9 %copy-done.9 = f32[16,16,128]{2,1,0:T(8,128)S(1)} copy-done((f32[16,16,128]{2,1,0:T(8,128)S(1)}, f32[16,16,128]{2,1,0:T(8,128)}, u32[]{:S(2)}) %copy-start.9) | copy-done | bytes 131096
  22.6 0.0 copy-start.11
  22.6 0.9 %copy-done.11 = bf16[256,256]{1,0:T(8,128)(2,1)S(1)} copy-done((bf16[256,256]{1,0:T(8,128)(2,1)S(1)}, bf16[256,256]{1,0:T(8,128)(2,1)}, u32[]{:S(2)}) %copy-start.11) | copy-done | bytes 131096
  23.5 0.0 copy-start.13
  23.5 0.8 %copy-done.13 = bf16[256,128]{1,0:T(8,128)(2,1)S(1)} copy-done((bf16[256,128]{1,0:T(8,128)(2,1)S(1)}, bf16[256,128]{1,0:T(8,128)(2,1)}, u32[]{:S(2)}) %copy-start.13) | copy-done | bytes 65560
  24.3 0.9 %shard_map.125.refs_0_ = f32[5,16,16,128]{3,2,1,0:T(8,128)S(1)} custom-call(f32[5,3,16,128]{3,2,1,0:T(8,128)} %get-tuple-element.14.refs_0_, f32[5,16,16,128]{3,2,1,0:T(8,128)S(1)} %copy-done.2, f32[5,16,16,128]{3,2,1,0:T(8,128)S(1)} %get-tuple-element.15.refs_2_, f32[3,16,16,128]{3,2,1,0:T(8,128)S(1)} %copy-done, f32[16,16,128]{2,1,0:T(8,128)S(1)} %copy-done.5, ...), custom_call_target="tpu_custom_call" | custom-call | flops 131072000 | bytes 3792896 | tf_op jit(solution)/shard_map/pallas_call | solution.py:250
  25.2 0.0 collective-permute-done.5.refs_4_
  25.2 2.6 %collective-permute-done.4.refs_3_ = f32[5,3,16,128]{3,2,1,0:T(8,128)} collective-permute-done((f32[5,3,16,128]{3,2,1,0:T(8,128)}, f32[5,3,16,128]{3,2,1,0:T(8,128)}, u32[]{:S(2)}, u32[]{:S(2)}) %collective-permute-start.4) | collective-permute-done | bytes 122912 | tf_op jit(solution)/shard_map/ppermute | solution.py:232
  27.8 0.0 collective-permute-done.6.refs_5_
  27.8 0.0 collective-permute-done.7.refs_6_
  27.8 2.4 %shard_map.126 = (f32[5,16,16,128]{3,2,1,0:T(8,128)}, f32[32,8,128]{2,1,0:T(8,128)S(1)}) custom-call(f32[5,16,16,128]{3,2,1,0:T(8,128)S(1)} %shard_map.125.refs_0_, f32[3,16,16,128]{3,2,1,0:T(8,128)S(1)} %copy-done, f32[16,16,128]{2,1,0:T(8,128)S(1)} %copy-done.5, f32[5,3,16,128]{3,2,1,0:T(8,128)} %collective-permute-done.4.refs_3_, ...), custom_call_target="tpu_custom_call" | custom-call | flops 65536000 | bytes 3678336 | tf_op jit(solution)/shard_map/pallas_call | solution.py:250
  30.2 0.0 copy-start.14
  30.2 10.9 %all_to_all.5.sums_ref = f32[32,8,128]{2,1,0:T(8,128)S(1)} all-to-all(f32[32,8,128]{2,1,0:T(8,128)S(1)} %get-tuple-element.19), channel_id=1, replica_groups=mesh['ax'=8,'ty'=2,'tz'=2] {'ax','ty','tz'}, dimensions={0} | all-to-all | bytes 262144 | tf_op jit(solution)/shard_map/all_to_all | solution.py:302
  41.1 0.0 copy-done.14
  41.1 0.2 shard_map.127
  41.3 0.6 %copy.14 = f32[1,5,32]{2,0,1:T(1,128)} copy(f32[1,5,32]{2,1,0:T(8,128)S(1)} %shard_map.127) | data formatting | bytes 1280
Async XLA Ops:
  0.6 8.9 %copy-start = (f32[3,16,16,128]{3,2,1,0:T(8,128)S(1)}, f32[3,16,16,128]{3,2,1,0:T(8,128)}, u32[]{:S(2)}) copy-start(f32[3,16,16,128]{3,2,1,0:T(8,128)} %refs_1_.7) | copy-start | bytes 1179652
  0.6 15.5 %collective-permute-start.3 = (f32[5,16,16,128]{3,2,1,0:T(8,128)}, f32[5,16,16,128]{3,2,1,0:T(8,128)S(1)}, u32[]{:S(2)}, u32[]{:S(2)}) collective-permute-start(f32[5,16,16,128]{3,2,1,0:T(8,128)} %refs_1_.6), channel_id=1, source_target_pairs={{0,1},{1,0},{2,3},{3,2},{4,5},{5,4},{6,7},{7,6},{8,9},{9,8},{10,11... | collective-permute-start | bytes 1966088 | tf_op jit(solution)/shard_map/ppermute | solution.py:232
  1.2 1.1 %copy-start.1 = (f32[5,16,16,128]{3,2,1,0:T(8,128)S(1)}, f32[5,16,16,128]{3,2,1,0:T(8,128)}, u32[]{:S(2)}) copy-start(f32[5,16,16,128]{3,2,1,0:T(8,128)} %refs_1_.6) | copy-start | bytes 1966084
  2.2 7.2 %copy-start.5 = (f32[16,16,128]{2,1,0:T(8,128)S(1)}, f32[16,16,128]{2,1,0:T(8,128)}, u32[]{:S(2)}) copy-start(f32[16,16,128]{2,1,0:T(8,128)} %refs_2_.5) | copy-start | bytes 393220
  2.2 7.2 %copy-start.8 = (f32[16,16,128]{2,1,0:T(8,128)S(1)}, f32[16,16,128]{2,1,0:T(8,128)}, u32[]{:S(2)}) copy-start(f32[16,16,128]{2,1,0:T(8,128)} %refs_5_.3) | copy-start | bytes 393220
  2.3 10.9 %collective-permute-start.1 = (f32[5,3,16,128]{3,2,1,0:T(8,128)S(1)}, f32[5,3,16,128]{3,2,1,0:T(8,128)S(1)}, u32[]{:S(2)}, u32[]{:S(2)}) collective-permute-start(f32[5,3,16,128]{3,2,1,0:T(8,128)S(1)} %get-tuple-element.11.refs_0_), channel_id=1, source_target_pairs={{0,28},{4,0},{8,4},{12,8},{16,12},{20,16},{24,20},{28,24},{1,29},{... | collective-permute-start | bytes 368648 | tf_op jit(solution)/shard_map/ppermute | solution.py:232
  8.0 8.1 %collective-permute-start = (f32[5,3,16,128]{3,2,1,0:T(8,128)S(1)}, f32[5,3,16,128]{3,2,1,0:T(8,128)S(1)}, u32[]{:S(2)}, u32[]{:S(2)}) collective-permute-start(f32[5,3,16,128]{3,2,1,0:T(8,128)S(1)} %get-tuple-element.12), channel_id=1, source_target_pairs={{0,4},{4,8},{8,12},{12,16},{16,20},{20,24},{24,28},{28,0},{1,5},{5... | collective-permute-start | bytes 368648 | tf_op jit(solution)/shard_map/ppermute | solution.py:232
  8.0 8.1 %collective-permute-start.2 = (f32[5,3,16,128]{3,2,1,0:T(8,128)S(1)}, f32[5,3,16,128]{3,2,1,0:T(8,128)S(1)}, u32[]{:S(2)}, u32[]{:S(2)}) collective-permute-start(f32[5,3,16,128]{3,2,1,0:T(8,128)S(1)} %get-tuple-element.13), channel_id=1, source_target_pairs={{0,2},{2,0},{1,3},{3,1},{4,6},{6,4},{5,7},{7,5},{8,10},{10,8},{9,1... | collective-permute-start | bytes 368648 | tf_op jit(solution)/shard_map/ppermute | solution.py:232
  9.5 1.1 %copy-start.3 = (f32[5,16,16,128]{3,2,1,0:T(8,128)S(1)}, f32[5,16,16,128]{3,2,1,0:T(8,128)}, u32[]{:S(2)}) copy-start(f32[5,16,16,128]{3,2,1,0:T(8,128)} %refs_6_.2) | copy-start | bytes 1966084
  10.6 0.9 %copy-start.10 = (bf16[256,256]{1,0:T(8,128)(2,1)S(1)}, bf16[256,256]{1,0:T(8,128)(2,1)}, u32[]{:S(2)}) copy-start(bf16[256,256]{1,0:T(8,128)(2,1)} %constant.8.clone.refs_6_.refs_7_) | copy-start | bytes 393220
  11.5 0.8 %copy-start.12 = (bf16[256,128]{1,0:T(8,128)(2,1)S(1)}, bf16[256,128]{1,0:T(8,128)(2,1)}, u32[]{:S(2)}) copy-start(bf16[256,128]{1,0:T(8,128)(2,1)} %constant.9.clone.refs_7_.refs_8_) | copy-start | bytes 196612
  12.3 3.8 %copy-start.6 = (bf16[3,256,96]{2,1,0:T(8,128)(2,1)S(1)}, bf16[3,256,96]{2,1,0:T(8,128)(2,1)}, u32[]{:S(2)}) copy-start(bf16[3,256,96]{2,1,0:T(8,128)(2,1)} %constant.10.clone.refs_7_) | copy-start | bytes 442372
  12.3 3.8 %copy-start.7 = (bf16[3,256,128]{2,1,0:T(8,128)(2,1)S(1)}, bf16[3,256,128]{2,1,0:T(8,128)(2,1)}, u32[]{:S(2)}) copy-start(bf16[3,256,128]{2,1,0:T(8,128)(2,1)} %constant.11.clone.refs_8_) | copy-start | bytes 589828
  13.2 8.4 %copy-start.2 = (f32[5,16,16,128]{3,2,1,0:T(8,128)S(1)}, f32[5,16,16,128]{3,2,1,0:T(8,128)}, u32[]{:S(2)}) copy-start(f32[5,16,16,128]{3,2,1,0:T(8,128)} %refs_1_.6) | copy-start | bytes 1966084
  13.2 8.4 %copy-start.4 = (f32[5,16,16,128]{3,2,1,0:T(8,128)S(1)}, f32[5,16,16,128]{3,2,1,0:T(8,128)}, u32[]{:S(2)}) copy-start(f32[5,16,16,128]{3,2,1,0:T(8,128)} %refs_6_.2) | copy-start | bytes 1966084
  17.4 10.4 %collective-permute-start.7 = (f32[5,16,16,128]{3,2,1,0:T(8,128)S(1)}, f32[5,16,16,128]{3,2,1,0:T(8,128)S(1)}, u32[]{:S(2)}, u32[]{:S(2)}) collective-permute-start(f32[5,16,16,128]{3,2,1,0:T(8,128)S(1)} %get-tuple-element.15.refs_2_), channel_id=1, source_target_pairs={{0,1},{1,0},{2,3},{3,2},{4,5},{5,4},{6,7},{7,6},{8,9},{9,8},{10,11... | collective-permute-start | bytes 1966088 | tf_op jit(solution)/shard_map/ppermute | solution.py:232
  17.4 7.8 %collective-permute-start.5 = (f32[5,3,16,128]{3,2,1,0:T(8,128)}, f32[5,3,16,128]{3,2,1,0:T(8,128)}, u32[]{:S(2)}, u32[]{:S(2)}) collective-permute-start(f32[5,3,16,128]{3,2,1,0:T(8,128)} %get-tuple-element.14.refs_0_), channel_id=1, source_target_pairs={{0,28},{4,0},{8,4},{12,8},{16,12},{20,16},{24,20},{28,24},{1,29},{... | collective-permute-start | bytes 368648 | tf_op jit(solution)/shard_map/ppermute | solution.py:232
  19.3 8.5 %collective-permute-start.4 = (f32[5,3,16,128]{3,2,1,0:T(8,128)}, f32[5,3,16,128]{3,2,1,0:T(8,128)}, u32[]{:S(2)}, u32[]{:S(2)}) collective-permute-start(f32[5,3,16,128]{3,2,1,0:T(8,128)} %get-tuple-element.16), channel_id=1, source_target_pairs={{0,4},{4,8},{8,12},{12,16},{16,20},{20,24},{24,28},{28,0},{1,5},{5... | collective-permute-start | bytes 368648 | tf_op jit(solution)/shard_map/ppermute | solution.py:232
  19.4 8.4 %collective-permute-start.6 = (f32[5,3,16,128]{3,2,1,0:T(8,128)}, f32[5,3,16,128]{3,2,1,0:T(8,128)}, u32[]{:S(2)}, u32[]{:S(2)}) collective-permute-start(f32[5,3,16,128]{3,2,1,0:T(8,128)} %get-tuple-element.17), channel_id=1, source_target_pairs={{0,2},{2,0},{1,3},{3,1},{4,6},{6,4},{5,7},{7,5},{8,10},{10,8},{9,1... | collective-permute-start | bytes 368648 | tf_op jit(solution)/shard_map/ppermute | solution.py:232
  21.7 0.9 %copy-start.9 = (f32[16,16,128]{2,1,0:T(8,128)S(1)}, f32[16,16,128]{2,1,0:T(8,128)}, u32[]{:S(2)}) copy-start(f32[16,16,128]{2,1,0:T(8,128)} %refs_5_.3) | copy-start | bytes 393220
  22.6 0.9 %copy-start.11 = (bf16[256,256]{1,0:T(8,128)(2,1)S(1)}, bf16[256,256]{1,0:T(8,128)(2,1)}, u32[]{:S(2)}) copy-start(bf16[256,256]{1,0:T(8,128)(2,1)} %constant.8.clone.refs_6_.refs_7_) | copy-start | bytes 393220
  23.5 0.8 %copy-start.13 = (bf16[256,128]{1,0:T(8,128)(2,1)S(1)}, bf16[256,128]{1,0:T(8,128)(2,1)}, u32[]{:S(2)}) copy-start(bf16[256,128]{1,0:T(8,128)(2,1)} %constant.9.clone.refs_7_.refs_8_) | copy-start | bytes 196612
  30.2 10.9 %copy-start.14 = (f32[1,128,128]{2,1,0:T(8,128)S(1)}, f32[1,128,128]{2,1,0:T(8,128)}, u32[]{:S(2)}) copy-start(f32[1,128,128]{2,1,0:T(8,128)} %basis_ref.1) | copy-start | bytes 196612

commit v2 on v0

v2 whole, which is shorter than its diff:
```python
import functools
import math

import jax
import jax.numpy as jnp
import numpy as np
from jax import lax
from jax.experimental import pallas as pl
from jax.experimental.pallas import tpu as pltpu
from jax.sharding import PartitionSpec as P

FACE_PLANES = 2
TIME_STEP = 0.6
HALO = 3
WEIGHTS = {1: 45.0, 2: -9.0, 3: 1.0}
F32, BF16 = jnp.float32, jnp.bfloat16
VMEM = pl.BlockSpec(memory_space=pltpu.VMEM)
ANY = pl.BlockSpec(memory_space=pl.ANY)
HBM = pl.BlockSpec(memory_space=pltpu.HBM)
ABOVE, BELOW, NONE = 0, 1, 2


def weight_of(offset):
    size = np.abs(offset)
    table = np.zeros(offset.shape, np.float32)
    for s, w in WEIGHTS.items():
        table = np.where(size == s, np.sign(offset) * w, table)
    return table


def tables(nx, ny, nz):
    y, z, layer, x = np.arange(ny), np.arange(nz), np.arange(HALO), np.eye(nx, dtype=np.float32)
    face = np.eye(FACE_PLANES, dtype=np.float32)
    band = weight_of(y[None, :] - y[:, None])
    along_z = weight_of(z[:, None] - z[None, :])

    def from_rows(places):
        w = weight_of(places[None, :] - y[:, None])
        return np.einsum("xp,yl->xylp", x, w).reshape(nx * ny, HALO * nx)

    y_halo = np.stack([from_rows(ny + layer), from_rows(layer - HALO), np.zeros((nx * ny, HALO * nx))])
    y_face = np.stack(
        [np.kron(face, weight_of(y[None, :] + o - y[:, None])) for o in (ny, -ny)]
        + [np.zeros((FACE_PLANES * ny, FACE_PLANES * ny))]
    )
    z_halo = np.stack([weight_of(z[:, None] + o - z[None, :]) for o in (nz, -nz)] + [np.zeros((nz, nz))])
    twice = lambda m, axis: np.concatenate([m, m], axis=axis)
    return dict(
        ay=jnp.asarray(np.kron(x, band), BF16),
        bz=jnp.asarray(twice(along_z, 0), BF16),
        py=jnp.asarray(twice(y_halo, 2), BF16),
        wz=jnp.asarray(twice(z_halo, 1), BF16),
        fy=jnp.asarray(np.concatenate([twice(np.kron(face, band), 1)[None], twice(y_face, 2)]), BF16),
    )


def halves(v):
    high = v.astype(BF16)
    return high, (v - high.astype(F32)).astype(BF16)


def stacked(v, axis):
    return jnp.concatenate(halves(v), axis=axis)


def dot(a, b):
    return jnp.dot(a, b, preferred_element_type=F32)


def couple(acc, u, c, d, grad):
    acc = [u * grad[k] if acc is None else acc[k] + u * grad[k] for k in range(5)]
    acc[1 + d] = acc[1 + d] + c * grad[4]
    acc[4] = acc[4] + c * grad[1 + d]
    return acc


def pairs_of(count):
    return count % 2 == 0


def x_sides():
    at, count = lax.axis_index("ax"), lax.axis_size("ax")
    has_lo, has_hi = at > 0, at < count - 1
    if not pairs_of(count):
        return [(False, has_lo), (True, has_hi)]
    even = lax.rem(at, 2) == 0
    return [(even, jnp.where(even, has_hi, has_lo)), (jnp.logical_not(even), jnp.where(even, has_lo, has_hi))]


def sides_of(axis):
    at, count = lax.axis_index(axis), lax.axis_size(axis)
    if count == 2:
        return [at]
    return [jnp.where(at > 0, BELOW, NONE), jnp.where(at < count - 1, ABOVE, NONE)]


def turned(side):
    if isinstance(side, int):
        return (BELOW, ABOVE, NONE)[side]
    return jnp.where(side == NONE, NONE, 1 - side)


def start_of(from_above_next, size):
    if isinstance(from_above_next, bool):
        return size - HALO if from_above_next else 0
    return jnp.where(from_above_next, size - HALO, 0)


def pack_first(adj, vel, c, owner_ref, *refs):
    n_y = len(sides_of("ty"))
    x_msgs, y_msgs, (aux, token, rows, sems) = refs[:2], refs[2 : 2 + n_y], refs[2 + n_y :]
    token[...] = jnp.zeros(token.shape, F32)
    nx, ny, nz = adj.shape[1:]
    half = rows.shape[3]
    at = lax.axis_index("ty")
    copies = []

    def copy(src, dst):
        copies.append(pltpu.make_async_copy(src, dst, sems.at[len(copies)]))
        copies[-1].start()

    if n_y == 1:
        tops = [at == 0]
    else:
        tops = [True, False]
    for i, top in enumerate(tops):
        first = (ny - half if top else 0) if isinstance(top, bool) else pl.multiple_of(jnp.where(top, ny - half, 0), 8)
        copy(adj.at[:, :, pl.ds(first, half), :], rows.at[i])
    for ref, (above, _) in zip(x_msgs, x_sides()):
        up = above if pairs_of(lax.axis_size("ax")) else not above
        copy(adj.at[:, pl.ds(start_of(up, nx), HALO)], ref.at[:5])
    for d, msgs in enumerate((x_msgs, y_msgs, (aux,))):
        for ref in msgs:
            n = ref.shape[0]
            copy(vel.at[d, :FACE_PLANES], ref.at[n - 2, :2])
            copy(c.at[0], ref.at[n - 2, 2])
            copy(c.at[1], ref.at[n - 1, 0])
    blocks = owner_ref.shape[1]
    eye = lax.broadcasted_iota(jnp.int32, (blocks, blocks), 0) == lax.broadcasted_iota(jnp.int32, (blocks, blocks), 1)
    column = jnp.sum(jnp.where(eye, owner_ref[...].astype(F32), 0.0), axis=1, keepdims=True)
    owners = jnp.broadcast_to(column, (blocks, nz)).reshape(FACE_PLANES, ny, nz)
    for ref in (*x_msgs, *y_msgs, aux):
        ref[ref.shape[0] - 1, 1:] = owners
    for one in copies:
        one.wait()
    for i, (ref, top) in enumerate(zip(y_msgs, tops)):

        def put(r, ref=ref, i=i):
            for k in range(5):
                for l in range(HALO):
                    ref[k, l] = rows[i, k, :, r + l, :]

        if isinstance(top, bool):
            put(half - HALO if top else 0)
        else:
            pl.when(top)(functools.partial(put, half - HALO))
            pl.when(jnp.logical_not(top))(functools.partial(put, 0))


def pack_second(v_ref, x_msgs, y_msgs):
    nx, ny = v_ref.shape[1:3]
    for ref, (above, _) in zip(x_msgs, x_sides()):
        up = above if pairs_of(lax.axis_size("ax")) else not above
        ref[...] = v_ref[:, pl.ds(start_of(up, nx), HALO)]

    def put(ref, start):
        for k in range(5):
            for l in range(HALO):
                ref[k, l] = v_ref[k, :, start + l, :]

    if len(y_msgs) == 1:
        at = lax.axis_index("ty")
        pl.when(at == 0)(functools.partial(put, y_msgs[0], ny - HALO))
        pl.when(at != 0)(functools.partial(put, y_msgs[0], 0))
    else:
        put(y_msgs[0], ny - HALO)
        put(y_msgs[1], 0)


def x_difference(v_ref, k, x):
    nx, total = v_ref.shape[1], None
    for s, w in WEIGHTS.items():
        diff = None
        if x + s < nx:
            diff = v_ref[k, x + s]
        if x - s >= 0:
            diff = -v_ref[k, x - s] if diff is None else diff - v_ref[k, x - s]
        if diff is not None:
            diff = diff if w == 1.0 else w * diff
            total = diff if total is None else total + diff
    return total


def own_rate(scale, x, v_ref, adj_ref, vel_ref, c_ref, sponge_ref, source_ref, gy, gz):
    part = scale / 60.0
    c, damp = c_ref[x] * part, sponge_ref[x] * scale
    acc = []
    for k in range(5):
        cur = v_ref[k, x]
        base = cur if adj_ref is None else 0.5 * (adj_ref[k, x] + cur)
        acc.append(base + (scale * source_ref[k, x] - damp * cur))
    gx = [x_difference(v_ref, k, x) for k in range(5)]
    for d, g in enumerate((gx, gy, gz)):
        acc = couple(acc, vel_ref[d, x] * part, c, d, g)
    return acc


def own_differences(v_ref, ay_ref, bz_ref, k):
    nx, ny, nz = v_ref.shape[1:]
    high, low = halves(v_ref[k].reshape(nx * ny, nz))
    along_z = dot(jnp.concatenate([high, low], axis=1), bz_ref[...])
    return dot(ay_ref[...], high) + dot(ay_ref[...], low), along_z


def halo_differences(k, shape, y_blocks, z_blocks, py_ref, wz_ref, along_y=None, along_z=None):
    nx, ny, nz = shape
    for ref, side in zip(y_blocks, sides_of("ty")):
        term = dot(py_ref[side], stacked(ref[k].reshape(HALO * nx, nz), 0))
        along_y = term if along_y is None else along_y + term
    for ref, side in zip(z_blocks, sides_of("tz")):
        term = dot(stacked(ref[k].reshape(nx * ny, nz), 1), wz_ref[side])
        along_z = term if along_z is None else along_z + term
    return along_y, along_z


def add_x_blocks(scale, out_ref, vel_ref, c_ref, x_blocks):
    nx = out_ref.shape[1]
    for ref, (above, present) in zip(x_blocks, x_sides()):
        keep = jnp.where(present, jnp.where(above, scale / 60.0, -scale / 60.0), 0.0)
        for e in range(HALO):
            x = jnp.where(above, nx - 1 - e, e)
            grad = []
            for k in range(5):
                total = None
                for m in range(HALO - e):
                    w = WEIGHTS[m + 1 + e]
                    term = ref[k, jnp.where(above, m, HALO - 1 - m)]
                    term = term if w == 1.0 else w * term
                    total = term if total is None else total + term
                grad.append(total)
            acc = couple([out_ref[k, x] for k in range(5)], vel_ref[0, x] * keep, c_ref[x] * keep, 0, grad)
            for k in range(5):
                out_ref[k, x] = acc[k]


def local_kernel(scale, v_ref, vel_ref, c_ref, sponge_ref, source_ref, ay_ref, bz_ref, _, out_ref, dy, dz):
    nx, ny, nz = v_ref.shape[1:]
    for k in range(5):
        along_y, along_z = own_differences(v_ref, ay_ref, bz_ref, k)
        dy[k], dz[k] = along_y.reshape(nx, ny, nz), along_z.reshape(nx, ny, nz)
    for x in range(nx):
        gy, gz = [dy[k, x] for k in range(5)], [dz[k, x] for k in range(5)]
        acc = own_rate(scale, x, v_ref, None, vel_ref, c_ref, sponge_ref, source_ref, gy, gz)
        for k in range(5):
            out_ref[k, x] = acc[k]


def face_sums(scale, mid, adj, vel, c, sponge, source, x_blocks, y_blocks, auxes, owner_ref, bz, wz, fy, sums_ref):
    nx, ny, nz = mid.shape[1:]
    rows = FACE_PLANES * ny
    part = scale / 60.0
    flat = lambda v: v.reshape(rows, nz)
    tall, wide = [], []
    for k in range(5):
        high, low = halves(flat(mid[k, :FACE_PLANES]))
        tall.append(jnp.concatenate([high, low], axis=0))
        wide.append(jnp.concatenate([high, low], axis=1))
    groups, owners = [], []
    gy = [dot(fy[0], tall[k]).reshape(FACE_PLANES, ny, nz) for k in range(5)]
    gz = [dot(wide[k], bz[...]).reshape(FACE_PLANES, ny, nz) for k in range(5)]
    planes = [
        own_rate(scale, p, mid, adj, vel, c, sponge, source, [g[p] for g in gy], [g[p] for g in gz])
        for p in range(FACE_PLANES)
    ]
    groups.append([jnp.concatenate([planes[p][k] for p in range(FACE_PLANES)], axis=0) for k in range(5)])
    owners.append(owner_ref[...].astype(F32))

    def neighbour(ref, d, keep, grad):
        n = ref.shape[0]
        u = flat(ref[n - 2, :2])
        speed = jnp.concatenate([ref[n - 2, 2], ref[n - 1, 0]], axis=0)
        groups.append(couple(None, u * keep, speed * keep, d, grad))
        owners.append(flat(ref[n - 1, 1:])[:, :1])

    grad = []
    for k in range(5):
        at_plane = []
        for p in range(FACE_PLANES):
            total = None
            for l in range(p, HALO):
                w = WEIGHTS[HALO + p - l]
                term = mid[k, nx - HALO + l]
                term = term if w == 1.0 else w * term
                total = term if total is None else total + term
            at_plane.append(total)
        grad.append(jnp.concatenate(at_plane, axis=0))
    for ref, (above, present) in zip(x_blocks, x_sides()):
        keep = jnp.where(jnp.logical_and(above, present), -part, 0.0)
        neighbour(ref, 0, keep, grad)
    for ref, side in zip(y_blocks, sides_of("ty")):
        neighbour(ref, 1, part, [dot(fy[1 + turned(side)], tall[k]) for k in range(5)])
    for ref, side in zip(auxes, sides_of("tz")):
        neighbour(ref, 2, part, [dot(wide[k], wz[turned(side)]) for k in range(5)])

    devices = sums_ref.shape[0]
    each = devices // lax.axis_size("ax")
    blocks = owner_ref.shape[1]
    eye = lax.broadcasted_iota(jnp.int32, (blocks, blocks), 0) == lax.broadcasted_iota(jnp.int32, (blocks, blocks), 1)
    owners[0] = jnp.sum(jnp.where(eye, owners[0], 0.0), axis=1, keepdims=True)
    total = rows * len(groups)
    place = (lax.broadcasted_iota(jnp.int32, (total, devices), 1) // each).astype(F32)
    choose = (jnp.concatenate(owners, axis=0) == place).astype(F32).astype(BF16)
    choose = jnp.concatenate([choose, choose], axis=0)
    sums_ref[:, 5:, :] = jnp.zeros((devices, sums_ref.shape[1] - 5, nz), F32)
    for k in range(5):
        values = stacked(jnp.concatenate([g[k] for g in groups], axis=0), 0)
        sums_ref[:, k, :] = lax.dot_general(choose, values, (((0,), (0,)), ((), ())), preferred_element_type=F32)


def mid_kernel(*refs):
    refs = list(refs)
    n_y, n_z = len(sides_of("ty")), len(sides_of("tz"))
    part_ref, adj, vel, c, sponge, source, owner_ref, bz, py, wz, fy = refs[:11]
    x_blocks, refs = refs[11:13], refs[13:]
    y_blocks, z_blocks, auxes, refs = refs[:n_y], refs[n_y : n_y + n_z], refs[n_y + n_z : n_y + 2 * n_z], refs[n_y + 2 * n_z :]
    out_ref, sums_ref, x_msgs, y_msgs, dy, dz = refs[0], refs[1], refs[2:4], refs[4 : 4 + n_y], refs[-2], refs[-1]
    shape = nx, ny, nz = out_ref.shape[1:]
    for k in range(5):
        along_y, along_z = halo_differences(k, shape, y_blocks, z_blocks, py, wz)
        dy[k], dz[k] = along_y.reshape(shape), along_z.reshape(shape)
    part = TIME_STEP / 60.0
    for x in range(nx):
        acc, speed = [part_ref[k, x] for k in range(5)], c[x] * part
        acc = couple(acc, vel[1, x] * part, speed, 1, [dy[k, x] for k in range(5)])
        acc = couple(acc, vel[2, x] * part, speed, 2, [dz[k, x] for k in range(5)])
        for k in range(5):
            out_ref[k, x] = acc[k]
    add_x_blocks(TIME_STEP, out_ref, vel, c, x_blocks)
    pack_second(out_ref, x_msgs, y_msgs)
    face_sums(
        0.5 * TIME_STEP, out_ref, adj, vel, c, sponge, source, x_blocks, y_blocks, auxes, owner_ref, bz, wz, fy, sums_ref
    )


def final_kernel(*refs):
    refs = list(refs)
    n_y, n_z = len(sides_of("ty")), len(sides_of("tz"))
    adj, mid, vel, c, sponge, source, ay, bz, py, wz, _ = refs[:11]
    x_blocks, refs = refs[11:13], refs[13:]
    y_blocks, z_blocks, (out_ref, dy, dz) = refs[:n_y], refs[n_y : n_y + n_z], refs[n_y + n_z :]
    shape = nx, ny, nz = out_ref.shape[1:]
    for k in range(5):
        own = own_differences(mid, ay, bz, k)
        along_y, along_z = halo_differences(k, shape, y_blocks, z_blocks, py, wz, *own)
        dy[k], dz[k] = along_y.reshape(shape), along_z.reshape(shape)
    scale = 0.5 * TIME_STEP
    for x in range(nx):
        gy, gz = [dy[k, x] for k in range(5)], [dz[k, x] for k in range(5)]
        acc = own_rate(scale, x, mid, adj, vel, c, sponge, source, gy, gz)
        for k in range(5):
            out_ref[k, x] = acc[k]
    add_x_blocks(scale, out_ref, vel, c, x_blocks)


def modes_kernel(scale, sums_ref, basis_ref, out_ref):
    share = out_ref.shape[2]
    total = sums_ref[0]
    for i in range(1, sums_ref.shape[0]):
        total = total + sums_ref[i]
    modes = lax.dot_general(
        total, basis_ref[0], (((1,), (0,)), ((), ())), precision=lax.Precision.HIGHEST, preferred_element_type=F32
    )
    mine = lax.axis_index("ty") * lax.axis_size("tz") + lax.axis_index("tz")
    width = modes.shape[1]
    modes = pltpu.roll(modes * scale, lax.rem(width - mine * share, width), 1)
    for k in range(5):
        out_ref[k] = modes[k : k + 1, :share]


def swap_x(first, second):
    count, cores = lax.axis_size("ax"), lax.axis_size("tz")
    if not pairs_of(count):
        return [ring(first, "ax", 1), ring(second, "ax", -1)]
    near = lax.ppermute(first, "ax", [(i, i ^ 1) for i in range(count)])
    pairs = []
    for i in range(count):
        for u in range(cores):
            if i in (0, count - 1):
                pairs.append((i * cores + u, i * cores + (u + 1) % cores))
            else:
                j = i - 1 if i % 2 == 0 else i + 1
                pairs.append((i * cores + u, j * cores + u))
    return [near, lax.ppermute(second, ("ax", "tz"), pairs)]


def ring(v, axis, step):
    count = lax.axis_size(axis)
    return lax.ppermute(v, axis, [(i, (i + step) % count) for i in range(count)])


def from_sides(axis, to_above, to_below):
    if lax.axis_size(axis) == 2:
        return [ring(to_above, axis, 1)]
    return [ring(to_above, axis, 1), ring(to_below, axis, -1)]


def call(kernel, args, outs, scratch=(), away={}, flops=0, grant=12):
    moved = sum(4 * math.prod(a.shape) for a in (*args, *outs))
    return pl.pallas_call(
        kernel,
        out_shape=list(outs),
        in_specs=[away.get(i, VMEM) for i in range(len(args))],
        out_specs=[VMEM] * len(outs),
        scratch_shapes=list(scratch),
        cost_estimate=pl.CostEstimate(flops=flops, bytes_accessed=moved, transcendentals=0),
        compiler_params=pltpu.CompilerParams(vmem_limit_bytes=grant << 20),
    )(*args)


def on_device(adjoint, velocity, sound_speed, sponge, source, mode_basis, block_owner):
    nx, ny, nz = adjoint.shape[1:]
    n_ax, n_ty, n_tz = (lax.axis_size(a) for a in ("ax", "ty", "tz"))
    n_y = 1 if n_ty == 2 else 2
    t = tables(nx, ny, nz)
    shape = lambda *s: jax.ShapeDtypeStruct(s, F32)
    brick = shape(5, nx, ny, nz)
    grads = [pltpu.VMEM((5, nx, ny, nz), F32)] * 2
    work = 5 * nx * ny * nz * 800
    owners = block_owner.reshape(1, FACE_PLANES * ny)
    devices = n_ax * n_ty * n_tz

    *msgs, aux, token = call(
        pack_first,
        [adjoint, velocity, sound_speed, owners],
        [shape(7, HALO, ny, nz)] * 2 + [shape(7, HALO, nx, nz)] * n_y + [shape(2, HALO, ny, nz), shape(8, nz)],
        [pltpu.VMEM((n_y, 5, nx, 8, nz), F32), pltpu.SemaphoreType.DMA((32,))],
        away={0: HBM, 1: HBM, 2: HBM},
        grant=62,
    )
    z_blocks = from_sides("tz", adjoint, adjoint)
    auxes = from_sides("tz", aux, aux)
    y_blocks = from_sides("ty", msgs[2], msgs[-1])
    x_blocks = swap_x(msgs[0], msgs[1])
    fields = [velocity, sound_speed, sponge, source]
    (part,) = call(
        functools.partial(local_kernel, TIME_STEP),
        [adjoint, *fields, t["ay"], t["bz"], token],
        [brick],
        grads,
        away={7: ANY},
        flops=work,
    )
    mid, sums, *msgs = call(
        mid_kernel,
        [part, adjoint, *fields, owners, t["bz"], t["py"], t["wz"], t["fy"], *x_blocks, *y_blocks, *z_blocks, *auxes],
        [brick, shape(devices, 8, nz)] + [shape(5, HALO, ny, nz)] * 2 + [shape(5, HALO, nx, nz)] * n_y,
        grads,
        flops=work // 2,
        grant=8,
    )
    z_blocks = from_sides("tz", mid, mid)
    y_blocks = from_sides("ty", msgs[2], msgs[-1])
    x_blocks = swap_x(msgs[0], msgs[1])
    sums = lax.all_to_all(sums, ("ax", "ty", "tz"), split_axis=0, concat_axis=0, tiled=True)
    share = mode_basis.shape[2] // (n_ty * n_tz)
    scale = 1.0 / math.sqrt(FACE_PLANES * ny * n_ty * n_tz)
    (modes,) = call(functools.partial(modes_kernel, scale), [sums, mode_basis], [shape(5, 1, share)], grant=2)
    (adjoint_out,) = call(
        final_kernel,
        [adjoint, mid, *fields, t["ay"], t["bz"], t["py"], t["wz"], sums, *x_blocks, *y_blocks, *z_blocks],
        [brick],
        grads,
        away={10: ANY},
        flops=work,
        grant=6,
    )
    return (adjoint_out, jnp.transpose(modes, (1, 0, 2)))


def solution(mesh):
    return jax.shard_map(
        on_device,
        mesh=mesh,
        in_specs=(
            P(None, "ax", "ty", "tz"),
            P(None, "ax", "ty", "tz"),
            P("ax", "ty", "tz"),
            P("ax", "ty", "tz"),
            P(None, "ax", "ty", "tz"),
            P("ax", None, None),
            P("ax", "ty", "tz", None, None),
        ),
        out_specs=(P(None, "ax", "ty", "tz"), P("ax", None, ("ty", "tz"))),
        check_vma=False,
    )
```

time: 116 us -> 36.8 us (0.32)
  starting transfers between devices: 36.7 us -> 14 us
  local copies, waits for them, and re-layouts: 24 us -> 3.78 us
  between operations: 14.4 us -> 0.8 us
  blocking collectives: 13 us -> 0 us
  Pallas kernels: 0 us -> 11 us
  waiting for transfers between devices: 16.8 us -> 6.84 us
  other arithmetic: 9.65 us -> 0 us
    ppermute x12 -> x9, starting transfers between devices: 36.7 us -> 8.15 us  [the longest x2 4.46 us: swap_x(): near = lax.ppermute(first, 'ax', [(i, i ^ 1) for i in range(count)])]
    unnamed x2 -> x0, waiting for transfers between devices: 16.6 us -> none
    all_to_all x1 -> x0, blocking collectives: 13 us -> none  [on_device(): lax.all_to_all(outgoing, 'ax', split_axis=0, concat_axis=0, tiled=True)]
    pallas_call x0 -> x5, Pallas kernels: none -> 11 us  [call(): pl.pallas_call(kernel, out_shape=list(outs), in_specs=[away.get(i, VMEM)...]
    slice x10 -> x0, local copies, waits for them, and re-layouts: 8.8 us -> none  [the longest x8 6.91 us: padded_2(): head = lax.slice_in_dim(cells, 0, width, axis=dim)]
    ppermute x7 -> x0, local copies, waits for them, and re-layouts: 7.69 us -> none  [the longest x4 5.65 us: padded_2(): lax.ppermute(tail, axis, [(i, (i + 1) % count) for i in range(ends)])]
    add x6 -> x0, other arithmetic: 6.09 us -> none  [the longest x3 5.65 us: difference(): summed = contrib if summed is None else summed + contrib]
    all_to_all x0 -> x1, starting transfers between devices: none -> 5.84 us  [on_device(): lax.all_to_all(sums, ('ax', 'ty', 'tz'), split_axis=0, concat_axis=0, til...]
  transfers between devices with their start and end apart: 13 -> 10, of which waited for: 2 -> 2; matrix products, arithmetic and copies ran while one was open for 18% -> 0% of each run, Pallas kernels for 0% -> 13%
where the time goes in v2:
time: 36.8 us; the launch traced here: 36.4 us
  starting transfers between devices  14 us (38%)
  Pallas kernels  11 us (30%)
  waiting for transfers between devices  6.84 us (19%)
  local copies, waits for them, and re-layouts  3.78 us (10%)
  between operations  0.8 us (2%)
    pallas_call x5, Pallas kernels, call(): pl.pallas_call(kernel, out_shape=list(outs), in_specs=[away.get(i, VMEM)...  11 us
    all_to_all x1, starting transfers between devices, on_device(): lax.all_to_all(sums, ('ax', 'ty', 'tz'), split_axis=0, concat_axis=0, til...  5.84 us
    all_to_all x1, waiting for transfers between devices, on_device(): lax.all_to_all(sums, ('ax', 'ty', 'tz'), split_axis=0, concat_axis=0, til...  4.92 us
    ppermute x2, starting transfers between devices, swap_x(): near = lax.ppermute(first, 'ax', [(i, i ^ 1) for i in range(count)])  4.46 us
    unnamed x32, local copies, waits for them, and re-layouts  3.78 us
    ppermute x5, starting transfers between devices, ring(): lax.ppermute(v, axis, [(i, (i + step) % count) for i in range(count)])  3.51 us
    ppermute x2, waiting for transfers between devices, swap_x(): near = lax.ppermute(first, 'ax', [(i, i ^ 1) for i in range(count)])  1.91 us
  transfers between devices with their start and end apart: 10, of which 2 were waited for; matrix products, arithmetic and copies ran while one was open for 0% of the time, Pallas kernels for 13%

profile of v2, /device:TPU:0, one launch (start us, length us, event | category | flops | bytes accessed | tf_op | source)
XLA Modules:
  0.0 36.4 jit_solution(15120264224071833014)
XLA Ops:
  0.6 0.0 copy-start
  0.6 0.5 %collective-permute-start.3 = (f32[5,16,16,128]{3,2,1,0:T(8,128)}, f32[5,16,16,128]{3,2,1,0:T(8,128)}, u32[]{:S(2)}, u32[]{:S(2)}) collective-permute-start(f32[5,16,16,128]{3,2,1,0:T(8,128)} %refs_0_.1), channel_id=1, source_target_pairs={{0,1},{1,0},{2,3},{3,2},{4,5},{5,4},{6,7},{7,6},{8,9},{9,8},{10,11... | collective-permute-start | bytes 1966088 | tf_op jit(solution)/shard_map/ppermute | solution.py:398
  1.2 0.0 copy-start.1
  1.2 0.0 copy-start.4
  1.2 3.0 %shard_map.131 = (f32[7,3,16,128]{3,2,1,0:T(8,128)}, f32[7,3,16,128]{3,2,1,0:T(8,128)}, f32[7,3,16,128]{3,2,1,0:T(8,128)}, f32[2,3,16,128]{3,2,1,0:T(8,128)}, f32[8,128]{1,0:T(8,128)}) custom-call(f32[5,16,16,128]{3,2,1,0:T(8,128)} %refs_0_.1, f32[3,16,16,128]{3,2,1,0:T(8,128)} %refs_2_.3, f32[16,16,128]{2,1,0:T(8,128)} %refs_3_.3, s32[1,32]{1,0:T(1,128)} %bitcast.2), custom_call_target="tpu_custom_call" | custom-call | bytes 1749120 | tf_op jit(solution)/shard_map/pallas_call | solution.py:409
  4.1 0.0 copy-start.14
  4.2 2.6 %collective-permute-start = (f32[7,3,16,128]{3,2,1,0:T(8,128)}, f32[7,3,16,128]{3,2,1,0:T(8,128)S(1)}, u32[]{:S(2)}, u32[]{:S(2)}) collective-permute-start(f32[7,3,16,128]{3,2,1,0:T(8,128)} %get-tuple-element.13), channel_id=1, source_target_pairs={{0,4},{4,0},{8,12},{12,8},{16,20},{20,16},{24,28},{28,24},{1,5},{5... | collective-permute-start | bytes 516104 | tf_op jit(solution)/shard_map/ppermute | solution.py:384
  6.8 0.2 collective-permute-start.1
  7.0 1.5 %collective-permute-start.2 = (f32[7,3,16,128]{3,2,1,0:T(8,128)}, f32[7,3,16,128]{3,2,1,0:T(8,128)S(1)}, u32[]{:S(2)}, u32[]{:S(2)}) collective-permute-start(f32[7,3,16,128]{3,2,1,0:T(8,128)} %get-tuple-element.15), channel_id=1, source_target_pairs={{0,2},{2,0},{1,3},{3,1},{4,6},{6,4},{5,7},{7,5},{8,10},{10,8},{9,1... | collective-permute-start | bytes 516104 | tf_op jit(solution)/shard_map/ppermute | solution.py:398
  8.4 0.1 collective-permute-start.4
  8.5 0.0 copy-done
  8.5 0.0 copy-done.1
  8.5 0.0 copy-done.4
  8.5 0.0 copy-done.14
  8.5 0.0 copy-start.2
  8.5 1.1 %copy-done.2 = f32[5,16,16,128]{3,2,1,0:T(8,128)S(1)} copy-done((f32[5,16,16,128]{3,2,1,0:T(8,128)S(1)}, f32[5,16,16,128]{3,2,1,0:T(8,128)}, u32[]{:S(2)}) %copy-start.2) | copy-done | bytes 655384
  9.6 0.0 copy-start.5
  9.6 0.9 %copy-done.5 = f32[16,16,128]{2,1,0:T(8,128)S(1)} copy-done((f32[16,16,128]{2,1,0:T(8,128)S(1)}, f32[16,16,128]{2,1,0:T(8,128)}, u32[]{:S(2)}) %copy-start.5) | copy-done | bytes 131096
  10.5 0.0 copy-start.9
  10.5 0.8 %copy-done.9 = bf16[256,128]{1,0:T(8,128)(2,1)S(1)} copy-done((bf16[256,128]{1,0:T(8,128)(2,1)S(1)}, bf16[256,128]{1,0:T(8,128)(2,1)}, u32[]{:S(2)}) %copy-start.9) | copy-done | bytes 65560
  11.3 0.0 copy-start.10
  11.3 0.9 %copy-done.10 = bf16[256,256]{1,0:T(8,128)(2,1)S(1)} copy-done((bf16[256,256]{1,0:T(8,128)(2,1)S(1)}, bf16[256,256]{1,0:T(8,128)(2,1)}, u32[]{:S(2)}) %copy-start.10) | copy-done | bytes 131096
  12.2 0.0 copy-start.6
  12.2 0.0 copy-start.7
  12.2 0.0 copy-start.8
  12.2 0.0 copy-start.13
  12.3 0.0 copy-start.15
  12.3 0.9 %shard_map.132.refs_0_ = f32[5,16,16,128]{3,2,1,0:T(8,128)S(1)} custom-call(f32[5,16,16,128]{3,2,1,0:T(8,128)S(1)} %copy-done, f32[3,16,16,128]{3,2,1,0:T(8,128)S(1)} %copy-done.1, f32[16,16,128]{2,1,0:T(8,128)S(1)} %copy-done.4, f32[16,16,128]{2,1,0:T(8,128)S(1)} %copy-done.5, f32[5,16,16,128]{3,2,1,0:T(8,128)S(1)} %copy-done.2, ...), custom_call_target="tpu_custom_call" | custom-call | flops 131072000 | bytes 3018752 | tf_op jit(solution)/shard_map/pallas_call | solution.py:409
  13.1 0.0 collective-permute-done.4.refs_15_
  13.1 1.9 %collective-permute-done.refs_11_ = f32[7,3,16,128]{3,2,1,0:T(8,128)S(1)} collective-permute-done((f32[7,3,16,128]{3,2,1,0:T(8,128)}, f32[7,3,16,128]{3,2,1,0:T(8,128)S(1)}, u32[]{:S(2)}, u32[]{:S(2)}) %collective-permute-start) | collective-permute-done | bytes 172064 | tf_op jit(solution)/shard_map/ppermute | solution.py:384
  15.0 0.0 collective-permute-done.1.refs_12_
  15.0 0.0 collective-permute-done.2.refs_13_
  15.1 0.0 collective-permute-done.3.refs_14_
  15.1 0.0 copy-done.6
  15.1 0.0 copy-done.7
  15.1 0.0 copy-done.8
  15.1 0.0 copy-done.13
  15.1 0.0 copy-done.15
  15.1 0.0 copy-start.3
  15.1 3.0 %shard_map.133 = (f32[5,16,16,128]{3,2,1,0:T(8,128)}, f32[32,8,128]{2,1,0:T(8,128)}, f32[5,3,16,128]{3,2,1,0:T(8,128)S(1)}, f32[5,3,16,128]{3,2,1,0:T(8,128)S(1)}, f32[5,3,16,128]{3,2,1,0:T(8,128)S(1)}) custom-call(f32[5,16,16,128]{3,2,1,0:T(8,128)S(1)} %shard_map.132.refs_0_, f32[5,16,16,128]{3,2,1,0:T(8,128)S(1)} %copy-done, ...), custom_call_target="tpu_custom_call" | custom-call | flops 65536000 | bytes 5849216 | tf_op jit(solution)/shard_map/pallas_call | solution.py:409
  18.1 0.0 collective-permute-start.8
  18.1 0.0 copy-start.12
  18.1 5.8 %all-to-all-start = ((f32[32,8,128]{2,1,0:T(8,128)}), f32[32,8,128]{2,1,0:T(8,128)S(1)}, u32[]{:S(2)}, u32[]{:S(2)}) async-start(f32[32,8,128]{2,1,0:T(8,128)} %get-tuple-element.18), calls=%async_computation | async-start | bytes 262144 | tf_op jit(solution)/shard_map/all_to_all | solution.py:464
  24.0 0.0 copy-start.11
  24.0 1.8 %collective-permute-start.5 = (f32[5,3,16,128]{3,2,1,0:T(8,128)S(1)}, f32[5,3,16,128]{3,2,1,0:T(8,128)S(1)}, u32[]{:S(2)}, u32[]{:S(2)}) collective-permute-start(f32[5,3,16,128]{3,2,1,0:T(8,128)S(1)} %get-tuple-element.19), channel_id=1, source_target_pairs={{0,4},{4,0},{8,12},{12,8},{16,20},{20,16},{24,28},{28,24},{1,5},{5... | collective-permute-start | bytes 368648 | tf_op jit(solution)/shard_map/ppermute | solution.py:384
  25.8 0.0 collective-permute-start.6
  25.8 1.5 %collective-permute-start.7 = (f32[5,3,16,128]{3,2,1,0:T(8,128)S(1)}, f32[5,3,16,128]{3,2,1,0:T(8,128)S(1)}, u32[]{:S(2)}, u32[]{:S(2)}) collective-permute-start(f32[5,3,16,128]{3,2,1,0:T(8,128)S(1)} %get-tuple-element.21), channel_id=1, source_target_pairs={{0,2},{2,0},{1,3},{3,1},{4,6},{6,4},{5,7},{7,5},{8,10},{10,8},{9,1... | collective-permute-start | bytes 368648 | tf_op jit(solution)/shard_map/ppermute | solution.py:398
  27.3 4.9 %all-to-all-done.refs_10_.sums_ref = f32[32,8,128]{2,1,0:T(8,128)S(1)} async-done(((f32[32,8,128]{2,1,0:T(8,128)}), f32[32,8,128]{2,1,0:T(8,128)S(1)}, u32[]{:S(2)}, u32[]{:S(2)}) %all-to-all-start) | async-done | bytes 131104 | tf_op jit(solution)/shard_map/all_to_all | solution.py:464
  32.2 0.0 copy-done.12
  32.2 0.8 %shard_map.135 = f32[5,1,32]{2,1,0:T(1,128)} custom-call(f32[32,8,128]{2,1,0:T(8,128)S(1)} %all-to-all-done.refs_10_.sums_ref, f32[1,128,128]{2,1,0:T(8,128)S(1)} %copy-done.12), custom_call_target="tpu_custom_call" | custom-call | bytes 197248 | tf_op jit(solution)/shard_map/pallas_call | solution.py:409
  33.1 0.0 collective-permute-done.5.refs_11_
  33.1 0.0 collective-permute-done.6.refs_12_
  33.1 0.0 collective-permute-done.7.refs_13_
  33.1 0.0 collective-permute-done.8.refs_14_
  33.1 0.0 copy-done.3
  33.1 0.0 copy-done.11
  33.1 3.3 %shard_map.134 = f32[5,16,16,128]{3,2,1,0:T(8,128)} custom-call(f32[5,16,16,128]{3,2,1,0:T(8,128)S(1)} %copy-done, f32[5,16,16,128]{3,2,1,0:T(8,128)} %get-tuple-element.17.refs_1_, f32[3,16,16,128]{3,2,1,0:T(8,128)S(1)} %copy-done.1, f32[16,16,128]{2,1,0:T(8,128)S(1)} %copy-done.4, f32[16,16,128]{2,1,0:T(8,128)S(1)} %copy-done.6, ...), custom_call_target="tpu_custom_call" | custom-call | flops 131072000 | bytes 5513216 | tf_op jit(solution)/shard_map/pallas_call | solution.py:409
Async XLA Ops:
  0.6 7.9 %copy-start = (f32[5,16,16,128]{3,2,1,0:T(8,128)S(1)}, f32[5,16,16,128]{3,2,1,0:T(8,128)}, u32[]{:S(2)}) copy-start(f32[5,16,16,128]{3,2,1,0:T(8,128)} %refs_0_.1) | copy-start | bytes 1966084
  0.6 14.4 %collective-permute-start.3 = (f32[5,16,16,128]{3,2,1,0:T(8,128)}, f32[5,16,16,128]{3,2,1,0:T(8,128)}, u32[]{:S(2)}, u32[]{:S(2)}) collective-permute-start(f32[5,16,16,128]{3,2,1,0:T(8,128)} %refs_0_.1), channel_id=1, source_target_pairs={{0,1},{1,0},{2,3},{3,2},{4,5},{5,4},{6,7},{7,6},{8,9},{9,8},{10,11... | collective-permute-start | bytes 1966088 | tf_op jit(solution)/shard_map/ppermute | solution.py:398
  1.2 7.3 %copy-start.1 = (f32[3,16,16,128]{3,2,1,0:T(8,128)S(1)}, f32[3,16,16,128]{3,2,1,0:T(8,128)}, u32[]{:S(2)}) copy-start(f32[3,16,16,128]{3,2,1,0:T(8,128)} %refs_2_.3) | copy-start | bytes 1179652
  1.2 7.3 %copy-start.4 = (f32[16,16,128]{2,1,0:T(8,128)S(1)}, f32[16,16,128]{2,1,0:T(8,128)}, u32[]{:S(2)}) copy-start(f32[16,16,128]{2,1,0:T(8,128)} %refs_3_.3) | copy-start | bytes 393220
  4.1 4.4 %copy-start.14 = (f32[8,128]{1,0:T(8,128)S(1)}, f32[8,128]{1,0:T(8,128)}, u32[]{:S(2)}) copy-start(f32[8,128]{1,0:T(8,128)} %get-tuple-element.12._) | copy-start | bytes 12292
  4.2 10.9 %collective-permute-start = (f32[7,3,16,128]{3,2,1,0:T(8,128)}, f32[7,3,16,128]{3,2,1,0:T(8,128)S(1)}, u32[]{:S(2)}, u32[]{:S(2)}) collective-permute-start(f32[7,3,16,128]{3,2,1,0:T(8,128)} %get-tuple-element.13), channel_id=1, source_target_pairs={{0,4},{4,0},{8,12},{12,8},{16,20},{20,16},{24,28},{28,24},{1,5},{5... | collective-permute-start | bytes 516104 | tf_op jit(solution)/shard_map/ppermute | solution.py:384
  6.8 8.3 %collective-permute-start.1 = (f32[7,3,16,128]{3,2,1,0:T(8,128)}, f32[7,3,16,128]{3,2,1,0:T(8,128)S(1)}, u32[]{:S(2)}, u32[]{:S(2)}) collective-permute-start(f32[7,3,16,128]{3,2,1,0:T(8,128)} %get-tuple-element.14), channel_id=1, source_target_pairs={{0,1},{1,0},{4,8},{5,9},{8,4},{9,5},{12,16},{13,17},{16,12},{17,13... | collective-permute-start | bytes 516104 | tf_op jit(solution)/shard_map/ppermute | solution.py:393
  7.0 8.1 %collective-permute-start.2 = (f32[7,3,16,128]{3,2,1,0:T(8,128)}, f32[7,3,16,128]{3,2,1,0:T(8,128)S(1)}, u32[]{:S(2)}, u32[]{:S(2)}) collective-permute-start(f32[7,3,16,128]{3,2,1,0:T(8,128)} %get-tuple-element.15), channel_id=1, source_target_pairs={{0,2},{2,0},{1,3},{3,1},{4,6},{6,4},{5,7},{7,5},{8,10},{10,8},{9,1... | collective-permute-start | bytes 516104 | tf_op jit(solution)/shard_map/ppermute | solution.py:398
  8.4 4.7 %collective-permute-start.4 = (f32[2,3,16,128]{3,2,1,0:T(8,128)}, f32[2,3,16,128]{3,2,1,0:T(8,128)S(1)}, u32[]{:S(2)}, u32[]{:S(2)}) collective-permute-start(f32[2,3,16,128]{3,2,1,0:T(8,128)} %get-tuple-element.16), channel_id=1, source_target_pairs={{0,1},{1,0},{2,3},{3,2},{4,5},{5,4},{6,7},{7,6},{8,9},{9,8},{10,11... | collective-permute-start | bytes 147464 | tf_op jit(solution)/shard_map/ppermute | solution.py:398
  8.5 1.1 %copy-start.2 = (f32[5,16,16,128]{3,2,1,0:T(8,128)S(1)}, f32[5,16,16,128]{3,2,1,0:T(8,128)}, u32[]{:S(2)}) copy-start(f32[5,16,16,128]{3,2,1,0:T(8,128)} %refs_5_.3) | copy-start | bytes 1966084
  9.6 0.9 %copy-start.5 = (f32[16,16,128]{2,1,0:T(8,128)S(1)}, f32[16,16,128]{2,1,0:T(8,128)}, u32[]{:S(2)}) copy-start(f32[16,16,128]{2,1,0:T(8,128)} %refs_4_.3) | copy-start | bytes 393220
  10.5 0.8 %copy-start.9 = (bf16[256,128]{1,0:T(8,128)(2,1)S(1)}, bf16[256,128]{1,0:T(8,128)(2,1)}, u32[]{:S(2)}) copy-start(bf16[256,128]{1,0:T(8,128)(2,1)} %constant.11.clone.bz_ref.refs_7_) | copy-start | bytes 196612
  11.3 0.9 %copy-start.10 = (bf16[256,256]{1,0:T(8,128)(2,1)S(1)}, bf16[256,256]{1,0:T(8,128)(2,1)}, u32[]{:S(2)}) copy-start(bf16[256,256]{1,0:T(8,128)(2,1)} %constant.10.clone.ay_ref.refs_6_) | copy-start | bytes 393220
  12.2 2.8 %copy-start.6 = (f32[16,16,128]{2,1,0:T(8,128)S(1)}, f32[16,16,128]{2,1,0:T(8,128)}, u32[]{:S(2)}) copy-start(f32[16,16,128]{2,1,0:T(8,128)} %refs_4_.3) | copy-start | bytes 393220
  12.2 2.8 %copy-start.7 = (bf16[3,256,128]{2,1,0:T(8,128)(2,1)S(1)}, bf16[3,256,128]{2,1,0:T(8,128)(2,1)}, u32[]{:S(2)}) copy-start(bf16[3,256,128]{2,1,0:T(8,128)(2,1)} %constant.13.clone.refs_9_) | copy-start | bytes 589828
  12.2 2.8 %copy-start.8 = (bf16[3,256,96]{2,1,0:T(8,128)(2,1)S(1)}, bf16[3,256,96]{2,1,0:T(8,128)(2,1)}, u32[]{:S(2)}) copy-start(bf16[3,256,96]{2,1,0:T(8,128)(2,1)} %constant.12.clone.refs_8_) | copy-start | bytes 442372
  12.2 2.8 %copy-start.13 = (bf16[4,32,64]{2,1,0:T(8,128)(2,1)S(1)}, bf16[4,32,64]{2,1,0:T(8,128)(2,1)}, u32[]{:S(2)}) copy-start(bf16[4,32,64]{2,1,0:T(8,128)(2,1)} %constant.14.clone.refs_10_) | copy-start | bytes 49156
  12.3 2.8 %copy-start.15 = (s32[1,1,1,32,1]{3,4,2,1,0:T(1,128)S(1)}, s32[1,1,1,32,1]{3,4,2,1,0:T(1,128)}, u32[]{:S(2)}) copy-start(s32[1,1,1,32,1]{3,4,2,1,0:T(1,128)} %param.18) | copy-start | bytes 388
  15.1 18.0 %copy-start.3 = (f32[5,16,16,128]{3,2,1,0:T(8,128)S(1)}, f32[5,16,16,128]{3,2,1,0:T(8,128)}, u32[]{:S(2)}) copy-start(f32[5,16,16,128]{3,2,1,0:T(8,128)} %refs_5_.3) | copy-start | bytes 1966084
  18.1 14.9 %collective-permute-start.8 = (f32[5,16,16,128]{3,2,1,0:T(8,128)}, f32[5,16,16,128]{3,2,1,0:T(8,128)}, u32[]{:S(2)}, u32[]{:S(2)}) collective-permute-start(f32[5,16,16,128]{3,2,1,0:T(8,128)} %get-tuple-element.17.refs_1_), channel_id=1, source_target_pairs={{0,1},{1,0},{2,3},{3,2},{4,5},{5,4},{6,7},{7,6},{8,9},{9,8},{10,11... | collective-permute-start | bytes 1966088 | tf_op jit(solution)/shard_map/ppermute | solution.py:398
  18.1 14.1 %copy-start.12 = (f32[1,128,128]{2,1,0:T(8,128)S(1)}, f32[1,128,128]{2,1,0:T(8,128)}, u32[]{:S(2)}) copy-start(f32[1,128,128]{2,1,0:T(8,128)} %basis_ref.1) | copy-start | bytes 196612
  18.1 14.1 %all-to-all-start = ((f32[32,8,128]{2,1,0:T(8,128)}), f32[32,8,128]{2,1,0:T(8,128)S(1)}, u32[]{:S(2)}, u32[]{:S(2)}) async-start(f32[32,8,128]{2,1,0:T(8,128)} %get-tuple-element.18), calls=%async_computation | async-start | bytes 262144 | tf_op jit(solution)/shard_map/all_to_all | solution.py:464
  24.0 9.1 %copy-start.11 = (bf16[256,256]{1,0:T(8,128)(2,1)S(1)}, bf16[256,256]{1,0:T(8,128)(2,1)}, u32[]{:S(2)}) copy-start(bf16[256,256]{1,0:T(8,128)(2,1)} %constant.10.clone.ay_ref.refs_6_) | copy-start | bytes 393220
  24.0 9.1 %collective-permute-start.5 = (f32[5,3,16,128]{3,2,1,0:T(8,128)S(1)}, f32[5,3,16,128]{3,2,1,0:T(8,128)S(1)}, u32[]{:S(2)}, u32[]{:S(2)}) collective-permute-start(f32[5,3,16,128]{3,2,1,0:T(8,128)S(1)} %get-tuple-element.19), channel_id=1, source_target_pairs={{0,4},{4,0},{8,12},{12,8},{16,20},{20,16},{24,28},{28,24},{1,5},{5... | collective-permute-start | bytes 368648 | tf_op jit(solution)/shard_map/ppermute | solution.py:384
  25.8 7.2 %collective-permute-start.6 = (f32[5,3,16,128]{3,2,1,0:T(8,128)S(1)}, f32[5,3,16,128]{3,2,1,0:T(8,128)S(1)}, u32[]{:S(2)}, u32[]{:S(2)}) collective-permute-start(f32[5,3,16,128]{3,2,1,0:T(8,128)S(1)} %get-tuple-element.20), channel_id=1, source_target_pairs={{0,1},{1,0},{4,8},{5,9},{8,4},{9,5},{12,16},{13,17},{16,12},{17,13... | collective-permute-start | bytes 368648 | tf_op jit(solution)/shard_map/ppermute | solution.py:393
  25.8 7.2 %collective-permute-start.7 = (f32[5,3,16,128]{3,2,1,0:T(8,128)S(1)}, f32[5,3,16,128]{3,2,1,0:T(8,128)S(1)}, u32[]{:S(2)}, u32[]{:S(2)}) collective-permute-start(f32[5,3,16,128]{3,2,1,0:T(8,128)S(1)} %get-tuple-element.21), channel_id=1, source_target_pairs={{0,2},{2,0},{1,3},{3,1},{4,6},{6,4},{5,7},{7,5},{8,10},{10,8},{9,1... | collective-permute-start | bytes 368648 | tf_op jit(solution)/shard_map/ppermute | solution.py:398

commit v3 on v2

v3 whole, which is shorter than its diff:
```python
import functools
import math

import jax
import jax.numpy as jnp
import numpy as np
from jax import lax
from jax.experimental import pallas as pl
from jax.experimental.pallas import tpu as pltpu
from jax.sharding import PartitionSpec as P

FACE_PLANES = 2
TIME_STEP = 0.6
HALO = 3
EDGE = 8
WEIGHTS = {1: 45.0, 2: -9.0, 3: 1.0}
F32, BF16 = jnp.float32, jnp.bfloat16
VMEM = pl.BlockSpec(memory_space=pltpu.VMEM)
ANY = pl.BlockSpec(memory_space=pl.ANY)
HBM = pl.BlockSpec(memory_space=pltpu.HBM)
ABOVE, BELOW, NONE = 0, 1, 2


def weight_of(offset):
    size = np.abs(offset)
    table = np.zeros(offset.shape, np.float32)
    for s, w in WEIGHTS.items():
        table = np.where(size == s, np.sign(offset) * w, table)
    return table


def tables(nx, ny, nz):
    y, z, layer, x = np.arange(ny), np.arange(nz), np.arange(HALO), np.eye(nx, dtype=np.float32)
    face = np.eye(FACE_PLANES, dtype=np.float32)
    band = weight_of(y[None, :] - y[:, None])
    along_z = weight_of(z[:, None] - z[None, :])

    def from_rows(places, rows):
        w = weight_of(places[None, :] - rows[:, None])
        return np.einsum("xp,yl->xylp", x, w).reshape(nx * EDGE, HALO * nx)

    y_halo = [from_rows(ny + layer, y[ny - EDGE :]), from_rows(layer - HALO, y[:EDGE])]
    y_halo = np.stack(y_halo + [np.zeros((nx * EDGE, HALO * nx))])
    y_face = np.stack(
        [np.kron(face, weight_of(y[None, :] + o - y[:, None])) for o in (ny, -ny)]
        + [np.zeros((FACE_PLANES * ny, FACE_PLANES * ny))]
    )
    z_halo = np.stack([weight_of(z[:, None] + o - z[None, :]) for o in (nz, -nz)] + [np.zeros((nz, nz))])
    twice = lambda m, axis: np.concatenate([m, m], axis=axis)
    columns = lambda m: np.pad(m, [(0, 0)] * (m.ndim - 1) + [(0, -m.shape[-1] % nz)])
    parts = dict(
        ay=np.concatenate(np.split(np.kron(x, band), nx * ny // nz, axis=1)),
        bz=twice(along_z, 0),
        wz=twice(z_halo, 1).reshape(-1, nz),
        py=columns(twice(y_halo, 2)).reshape(-1, nz),
        fy=columns(np.concatenate([twice(np.kron(face, band), 1)[None], twice(y_face, 2)])).reshape(-1, nz),
    )
    places, at = {}, 0
    for name, m in parts.items():
        places[name], at = at, at + m.shape[0]
    return jnp.asarray(np.concatenate(list(parts.values())), BF16), places


class Bands:
    def __init__(self, ref, shape):
        self.ref, (self.nx, self.ny, self.nz) = ref, shape
        self.places = tables(*shape)[1]

    def block(self, name, rows, i=0, width=None):
        at = self.places[name]
        start = at + i * rows if isinstance(i, int) else pl.multiple_of(at + i * rows, 16)
        return self.ref[pl.ds(start, rows), : self.nz if width is None else width]

    def along_y(self):
        rows = self.nx * self.ny
        return jnp.concatenate([self.block("ay", rows, i) for i in range(rows // self.nz)], axis=1)

    def along_z(self):
        return self.block("bz", 2 * self.nz)

    def from_z(self, side):
        return self.block("wz", 2 * self.nz, side)

    def from_y(self, side):
        return self.block("py", self.nx * EDGE, side, 2 * HALO * self.nx)

    def face_y(self, i):
        return self.block("fy", FACE_PLANES * self.ny, i, 2 * FACE_PLANES * self.ny)


def halves(v):
    high = v.astype(BF16)
    return high, (v - high.astype(F32)).astype(BF16)


def stacked(v, axis):
    return jnp.concatenate(halves(v), axis=axis)


def dot(a, b):
    return jnp.dot(a, b, preferred_element_type=F32)


def couple(acc, u, c, d, grad):
    acc = [u * grad[k] if acc is None else acc[k] + u * grad[k] for k in range(5)]
    acc[1 + d] = acc[1 + d] + c * grad[4]
    acc[4] = acc[4] + c * grad[1 + d]
    return acc


def pairs_of(count):
    return count % 2 == 0


def x_sides():
    at, count = lax.axis_index("ax"), lax.axis_size("ax")
    has_lo, has_hi = at > 0, at < count - 1
    if not pairs_of(count):
        return [(False, has_lo), (True, has_hi)]
    even = lax.rem(at, 2) == 0
    return [(even, jnp.where(even, has_hi, has_lo)), (jnp.logical_not(even), jnp.where(even, has_lo, has_hi))]


def sides_of(axis):
    at, count = lax.axis_index(axis), lax.axis_size(axis)
    if count == 2:
        return [at]
    return [jnp.where(at > 0, BELOW, NONE), jnp.where(at < count - 1, ABOVE, NONE)]


def turned(side):
    if isinstance(side, int):
        return (BELOW, ABOVE, NONE)[side]
    return jnp.where(side == NONE, NONE, 1 - side)


def start_of(from_above_next, size):
    if isinstance(from_above_next, bool):
        return size - HALO if from_above_next else 0
    return jnp.where(from_above_next, size - HALO, 0)


def pack_first(adj, vel, c, owner_ref, *refs):
    n_y = len(sides_of("ty"))
    x_msgs, y_msgs, (aux, token, rows, speeds, sems) = refs[:2], refs[2 : 2 + n_y], refs[2 + n_y :]
    nx, ny, nz = adj.shape[1:]
    half = rows.shape[3]
    at = lax.axis_index("ty")
    copies = []

    def copy(src, dst):
        copies.append(pltpu.make_async_copy(src, dst, sems.at[len(copies)]))
        copies[-1].start()

    if n_y == 1:
        tops = [at == 0]
    else:
        tops = [True, False]
    for i, top in enumerate(tops):
        first = (ny - half if top else 0) if isinstance(top, bool) else pl.multiple_of(jnp.where(top, ny - half, 0), 8)
        copy(adj.at[:, :, pl.ds(first, half), :], rows.at[i])
    for ref, (above, _) in zip(x_msgs, x_sides()):
        up = above if pairs_of(lax.axis_size("ax")) else not above
        copy(adj.at[:, pl.ds(start_of(up, nx), HALO)], ref.at[:5])
    copy(vel.at[:, :FACE_PLANES], speeds.at[:3])
    copy(c.at[:FACE_PLANES], speeds.at[3])
    token[...] = jnp.zeros(token.shape, F32)
    blocks = owner_ref.shape[1]
    eye = lax.broadcasted_iota(jnp.int32, (blocks, blocks), 0) == lax.broadcasted_iota(jnp.int32, (blocks, blocks), 1)
    column = jnp.sum(jnp.where(eye, owner_ref[...].astype(F32), 0.0), axis=1, keepdims=True)
    owners = jnp.broadcast_to(column, (blocks, nz)).reshape(FACE_PLANES, ny, nz)
    for one in copies:
        one.wait()
    for d, msgs in enumerate((x_msgs, y_msgs, (aux,))):
        for ref in msgs:
            n = ref.shape[0]
            ref[n - 2, :2] = speeds[d]
            ref[n - 1, :2] = speeds[3]
            ref[n - 2, 2] = owners[0]
            ref[n - 1, 2] = owners[1]
    for i, (ref, top) in enumerate(zip(y_msgs, tops)):

        def put(r, ref=ref, i=i):
            for k in range(5):
                for l in range(HALO):
                    ref[k, l] = rows[i, k, :, r + l, :]

        if isinstance(top, bool):
            put(half - HALO if top else 0)
        else:
            pl.when(top)(functools.partial(put, half - HALO))
            pl.when(jnp.logical_not(top))(functools.partial(put, 0))


def pack_second(v_ref, x_msgs, y_msgs):
    nx, ny = v_ref.shape[1:3]
    for ref, (above, _) in zip(x_msgs, x_sides()):
        up = above if pairs_of(lax.axis_size("ax")) else not above
        ref[...] = v_ref[:, pl.ds(start_of(up, nx), HALO)]

    def put(ref, start):
        for k in range(5):
            for l in range(HALO):
                ref[k, l] = v_ref[k, :, start + l, :]

    if len(y_msgs) == 1:
        at = lax.axis_index("ty")
        pl.when(at == 0)(functools.partial(put, y_msgs[0], ny - HALO))
        pl.when(at != 0)(functools.partial(put, y_msgs[0], 0))
    else:
        put(y_msgs[0], ny - HALO)
        put(y_msgs[1], 0)


def x_difference(v_ref, k, x):
    nx, total = v_ref.shape[1], None
    for s, w in WEIGHTS.items():
        diff = None
        if x + s < nx:
            diff = v_ref[k, x + s]
        if x - s >= 0:
            diff = -v_ref[k, x - s] if diff is None else diff - v_ref[k, x - s]
        if diff is not None:
            diff = diff if w == 1.0 else w * diff
            total = diff if total is None else total + diff
    return total


def own_rate(scale, x, v_ref, adj_ref, vel_ref, c_ref, sponge_ref, source_ref, gy, gz):
    part = scale / 60.0
    c, damp = c_ref[x] * part, sponge_ref[x] * scale
    acc = []
    for k in range(5):
        cur = v_ref[k, x]
        base = cur if adj_ref is None else 0.5 * (adj_ref[k, x] + cur)
        acc.append(base + (scale * source_ref[k, x] - damp * cur))
    gx = [x_difference(v_ref, k, x) for k in range(5)]
    for d, g in enumerate((gx, gy, gz)):
        acc = couple(acc, vel_ref[d, x] * part, c, d, g)
    return acc


def add_x_blocks(scale, out_ref, vel_ref, c_ref, x_blocks):
    nx = out_ref.shape[1]
    for ref, (above, present) in zip(x_blocks, x_sides()):
        keep = jnp.where(present, jnp.where(above, scale / 60.0, -scale / 60.0), 0.0)
        for e in range(HALO):
            x = jnp.where(above, nx - 1 - e, e)
            grad = []
            for k in range(5):
                total = None
                for m in range(HALO - e):
                    w = WEIGHTS[m + 1 + e]
                    term = ref[k, jnp.where(above, m, HALO - 1 - m)]
                    term = term if w == 1.0 else w * term
                    total = term if total is None else total + term
                grad.append(total)
            acc = couple([out_ref[k, x] for k in range(5)], vel_ref[0, x] * keep, c_ref[x] * keep, 0, grad)
            for k in range(5):
                out_ref[k, x] = acc[k]


def own_planes(scale, v_ref, adj_ref, vel_ref, c_ref, sponge_ref, source_ref, table_ref, z_blocks, out_ref, dy, dz):
    nx, ny, nz = v_ref.shape[1:]
    bands = Bands(table_ref, v_ref.shape[1:])
    ay, bz = bands.along_y(), bands.along_z()
    for k in range(5):
        high, low = halves(v_ref[k].reshape(nx * ny, nz))
        dy[k] = (dot(ay, high) + dot(ay, low)).reshape(nx, ny, nz)
        along_z = dot(jnp.concatenate([high, low], axis=1), bz)
        for ref, side in zip(z_blocks, sides_of("tz")):
            along_z = along_z + dot(stacked(ref[k].reshape(nx * ny, nz), 1), bands.from_z(side))
        dz[k] = along_z.reshape(nx, ny, nz)
    for x in range(nx):
        gy, gz = [dy[k, x] for k in range(5)], [dz[k, x] for k in range(5)]
        acc = own_rate(scale, x, v_ref, adj_ref, vel_ref, c_ref, sponge_ref, source_ref, gy, gz)
        for k in range(5):
            out_ref[k, x] = acc[k]


def first_kernel(adj, vel, c, sponge, source, table, _, *refs):
    n_z, refs = len(sides_of("tz")), refs[1:]
    z_blocks, (out_ref, dy, dz) = refs[:n_z], refs[n_z:]
    own_planes(TIME_STEP, adj, None, vel, c, sponge, source, table, z_blocks, out_ref, dy, dz)


def second_kernel(mid, adj, vel, c, sponge, source, table, *refs):
    n_z = len(sides_of("tz"))
    z_blocks, (out_ref, dy, dz) = refs[:n_z], refs[n_z:]
    own_planes(0.5 * TIME_STEP, mid, adj, vel, c, sponge, source, table, z_blocks, out_ref, dy, dz)


def add_y_blocks(scale, out_ref, vel_ref, c_ref, y_blocks, table_ref):
    nx, ny, nz = out_ref.shape[1:]
    bands = Bands(table_ref, out_ref.shape[1:])
    part = scale / 60.0
    for ref, side in zip(y_blocks, sides_of("ty")):
        values = [stacked(ref[k].reshape(HALO * nx, nz), 0) for k in range(5)]
        grads = dot(bands.from_y(side), jnp.concatenate(values, axis=1))
        at = pl.multiple_of(jnp.where(side == ABOVE, ny - EDGE, 0), EDGE)
        for x in range(nx):
            rows = pl.ds(at, EDGE)
            grad = [grads[x * EDGE : (x + 1) * EDGE, k * nz : (k + 1) * nz] for k in range(5)]
            acc = [out_ref[k, x, rows, :] for k in range(5)]
            acc = couple(acc, vel_ref[1, x, rows, :] * part, c_ref[x, rows, :] * part, 1, grad)
            for k in range(5):
                out_ref[k, x, rows, :] = acc[k]


def mid_kernel(part_ref, vel, c, table, *refs):
    n_y = len(sides_of("ty"))
    n_z = len(sides_of("tz"))
    x_blocks, y_blocks, (out_ref, *msgs) = refs[:2], refs[2 : 2 + n_y], refs[2 + n_y + n_z :]
    out_ref[...] = part_ref[...]
    add_y_blocks(TIME_STEP, out_ref, vel, c, y_blocks, table)
    add_x_blocks(TIME_STEP, out_ref, vel, c, x_blocks)
    pack_second(out_ref, msgs[:2], msgs[2:])


def sums_kernel(mid, adj, vel, c, sponge, source, table, owner_ref, *refs):
    n_y, n_z = len(sides_of("ty")), len(sides_of("tz"))
    x_blocks, y_blocks, auxes, sums_ref = refs[:2], refs[2 : 2 + n_y], refs[2 + n_y : 2 + n_y + n_z], refs[-1]
    nx, ny, nz = mid.shape[1:]
    rows = FACE_PLANES * ny
    bands = Bands(table, mid.shape[1:])
    scale = 0.5 * TIME_STEP
    part = scale / 60.0
    flat = lambda v: v.reshape(rows, nz)
    split = [halves(flat(mid[k, :FACE_PLANES])) for k in range(5)]
    tall = jnp.concatenate([jnp.concatenate(pair, axis=0) for pair in split], axis=1)
    wide = jnp.concatenate([jnp.concatenate(pair, axis=1) for pair in split], axis=0)
    along_y = lambda i: [g for g in jnp.split(dot(bands.face_y(i), tall), 5, axis=1)]
    along_z = lambda m: [g for g in jnp.split(dot(wide, m), 5, axis=0)]
    groups, owners = [], []
    gy = [g.reshape(FACE_PLANES, ny, nz) for g in along_y(0)]
    gz = [g.reshape(FACE_PLANES, ny, nz) for g in along_z(bands.along_z())]
    planes = [
        own_rate(scale, p, mid, adj, vel, c, sponge, source, [g[p] for g in gy], [g[p] for g in gz])
        for p in range(FACE_PLANES)
    ]
    groups.append([jnp.concatenate([planes[p][k] for p in range(FACE_PLANES)], axis=0) for k in range(5)])
    eye = lax.broadcasted_iota(jnp.int32, (rows, rows), 0) == lax.broadcasted_iota(jnp.int32, (rows, rows), 1)
    owners.append(jnp.sum(jnp.where(eye, owner_ref[...].astype(F32), 0.0), axis=1, keepdims=True))

    def neighbour(ref, d, keep, grad):
        n = ref.shape[0]
        groups.append(couple(None, flat(ref[n - 2, :2]) * keep, flat(ref[n - 1, :2]) * keep, d, grad))
        owners.append(jnp.concatenate([ref[n - 2, 2], ref[n - 1, 2]], axis=0)[:, :1])

    grad = []
    for k in range(5):
        at_plane = []
        for p in range(FACE_PLANES):
            total = None
            for l in range(p, HALO):
                w = WEIGHTS[HALO + p - l]
                term = mid[k, nx - HALO + l]
                term = term if w == 1.0 else w * term
                total = term if total is None else total + term
            at_plane.append(total)
        grad.append(jnp.concatenate(at_plane, axis=0))
    for ref, (above, present) in zip(x_blocks, x_sides()):
        neighbour(ref, 0, jnp.where(jnp.logical_and(above, present), -part, 0.0), grad)
    for ref, side in zip(y_blocks, sides_of("ty")):
        neighbour(ref, 1, part, along_y(1 + turned(side)))
    for ref, side in zip(auxes, sides_of("tz")):
        neighbour(ref, 2, part, along_z(bands.from_z(turned(side))))

    devices = sums_ref.shape[0]
    each = devices // lax.axis_size("ax")
    total = rows * len(groups)
    place = (lax.broadcasted_iota(jnp.int32, (total, devices), 1) // each).astype(F32)
    choose = (jnp.concatenate(owners, axis=0) == place).astype(F32).astype(BF16)
    choose = jnp.concatenate([choose, choose], axis=0)
    values = [stacked(jnp.concatenate([g[k] for g in groups], axis=0), 0) for k in range(5)]
    sums = lax.dot_general(
        choose, jnp.concatenate(values, axis=1), (((0,), (0,)), ((), ())), preferred_element_type=F32
    )
    sums_ref[:, 5:, :] = jnp.zeros((devices, sums_ref.shape[1] - 5, nz), F32)
    for k in range(5):
        sums_ref[:, k, :] = sums[:, k * nz : (k + 1) * nz]


def final_kernel(part_ref, vel, c, table, *refs):
    n_y = len(sides_of("ty"))
    x_blocks, y_blocks, (out_ref, token, work, sems) = refs[:2], refs[2 : 2 + n_y], refs[2 + n_y :]
    nx = part_ref.shape[1]
    token[...] = jnp.zeros(token.shape, F32)
    scale = 0.5 * TIME_STEP
    work[...] = part_ref[...]
    add_y_blocks(scale, work, vel, c, y_blocks, table)
    inner = pltpu.make_async_copy(work.at[:, HALO : nx - HALO], out_ref.at[:, HALO : nx - HALO], sems.at[0])
    inner.start()
    add_x_blocks(scale, work, vel, c, x_blocks)
    low = pltpu.make_async_copy(work.at[:, :HALO], out_ref.at[:, :HALO], sems.at[1])
    high = pltpu.make_async_copy(work.at[:, nx - HALO :], out_ref.at[:, nx - HALO :], sems.at[2])
    low.start()
    high.start()
    inner.wait()
    low.wait()
    high.wait()


def modes_kernel(scale, sums_ref, basis_ref, _, out_ref):
    share = out_ref.shape[2]
    total = sums_ref[0]
    for i in range(1, sums_ref.shape[0]):
        total = total + sums_ref[i]
    modes = lax.dot_general(
        total, basis_ref[0], (((1,), (0,)), ((), ())), precision=lax.Precision.HIGHEST, preferred_element_type=F32
    )
    mine = lax.axis_index("ty") * lax.axis_size("tz") + lax.axis_index("tz")
    width = modes.shape[1]
    modes = pltpu.roll(modes * scale, lax.rem(width - mine * share, width), 1)
    for k in range(5):
        out_ref[k] = modes[k : k + 1, :share]


def swap_x(first, second):
    count, cores = lax.axis_size("ax"), lax.axis_size("tz")
    if not pairs_of(count):
        return [ring(first, "ax", 1), ring(second, "ax", -1)]
    near = lax.ppermute(first, "ax", [(i, i ^ 1) for i in range(count)])
    pairs = []
    for i in range(count):
        for u in range(cores):
            if i in (0, count - 1):
                pairs.append((i * cores + u, i * cores + (u + 1) % cores))
            else:
                j = i - 1 if i % 2 == 0 else i + 1
                pairs.append((i * cores + u, j * cores + u))
    return [near, lax.ppermute(second, ("ax", "tz"), pairs)]


def ring(v, axis, step):
    count = lax.axis_size(axis)
    return lax.ppermute(v, axis, [(i, (i + step) % count) for i in range(count)])


def from_sides(axis, to_above, to_below):
    if lax.axis_size(axis) == 2:
        return [ring(to_above, axis, 1)]
    return [ring(to_above, axis, 1), ring(to_below, axis, -1)]


def call(kernel, args, outs, scratch=(), away={}, out_away={}, flops=0, grant=12, hint=(20, 10)):
    moved = sum(4 * math.prod(a.shape) for a in (*args, *outs))
    return pl.pallas_call(
        kernel,
        out_shape=list(outs),
        in_specs=[away.get(i, VMEM) for i in range(len(args))],
        out_specs=[out_away.get(i, VMEM) for i in range(len(outs))],
        scratch_shapes=list(scratch),
        cost_estimate=pl.CostEstimate(flops=int(flops * hint[0]), bytes_accessed=int(moved * hint[1]), transcendentals=0),
        compiler_params=pltpu.CompilerParams(vmem_limit_bytes=grant << 20),
    )(*args)


def on_device(adjoint, velocity, sound_speed, sponge, source, mode_basis, block_owner):
    nx, ny, nz = adjoint.shape[1:]
    n_ax, n_ty, n_tz = (lax.axis_size(a) for a in ("ax", "ty", "tz"))
    n_y = 1 if n_ty == 2 else 2
    table, _ = tables(nx, ny, nz)
    shape = lambda *s: jax.ShapeDtypeStruct(s, F32)
    brick = shape(5, nx, ny, nz)
    grads = [pltpu.VMEM((5, nx, ny, nz), F32)] * 2
    work = 5 * nx * ny * nz * 800
    owners = block_owner.reshape(1, FACE_PLANES * ny)
    devices = n_ax * n_ty * n_tz

    *msgs, aux, token = call(
        pack_first,
        [adjoint, velocity, sound_speed, owners],
        [shape(7, HALO, ny, nz)] * 2 + [shape(7, HALO, nx, nz)] * n_y + [shape(2, HALO, ny, nz), shape(8, nz)],
        [pltpu.VMEM((n_y, 5, nx, 8, nz), F32), pltpu.VMEM((4, FACE_PLANES, ny, nz), F32), pltpu.SemaphoreType.DMA((8,))],
        away={0: HBM, 1: HBM, 2: HBM},
        grant=60, flops=10**6,
    )
    z_blocks = from_sides("tz", adjoint, adjoint)
    auxes = from_sides("tz", aux, aux)
    y_first = from_sides("ty", msgs[2], msgs[-1])
    x_first = swap_x(msgs[0], msgs[1])
    fields = [velocity, sound_speed, sponge, source, table]
    (part,) = call(
        first_kernel, [adjoint, *fields, token, owners, *z_blocks], [brick], grads, away={6: ANY}, flops=work, grant=8
    )
    vel, c = velocity, sound_speed
    mid, *msgs = call(
        mid_kernel,
        [part, vel, c, table, *x_first, *y_first, *auxes],
        [brick] + [shape(5, HALO, ny, nz)] * 2 + [shape(5, HALO, nx, nz)] * n_y,
        flops=work // 4,
        grant=8,
    )
    z_blocks = from_sides("tz", mid, mid)
    y_blocks = from_sides("ty", msgs[2], msgs[-1])
    x_blocks = swap_x(msgs[0], msgs[1])
    (sums,) = call(
        sums_kernel,
        [mid, adjoint, vel, c, sponge, source, table, owners, *x_first, *y_first, *auxes],
        [shape(devices, 8, nz)],
        flops=work // 4,
        grant=8,
        hint=(0.02, 0.01),
    )
    sums = lax.all_to_all(sums, ("ax", "ty", "tz"), split_axis=0, concat_axis=0, tiled=True)
    (part,) = call(
        second_kernel, [mid, adjoint, *fields, *z_blocks], [brick], grads, flops=work, grant=8, hint=(0.02, 0.01)
    )
    adjoint_out, token = call(
        final_kernel,
        [part, vel, c, table, *x_blocks, *y_blocks],
        [brick, shape(8, nz)],
        [pltpu.VMEM((5, nx, ny, nz), F32), pltpu.SemaphoreType.DMA((3,))],
        out_away={0: HBM},
        flops=work // 4,
        grant=6,
        hint=(100, 10),
    )
    share = mode_basis.shape[2] // (n_ty * n_tz)
    scale = 1.0 / math.sqrt(FACE_PLANES * ny * n_ty * n_tz)
    (modes,) = call(functools.partial(modes_kernel, scale), [sums, mode_basis, token], [shape(5, 1, share)], grant=2)
    return (adjoint_out, jnp.transpose(modes, (1, 0, 2)))


def solution(mesh):
    return jax.shard_map(
        on_device,
        mesh=mesh,
        in_specs=(
            P(None, "ax", "ty", "tz"),
            P(None, "ax", "ty", "tz"),
            P("ax", "ty", "tz"),
            P("ax", "ty", "tz"),
            P(None, "ax", "ty", "tz"),
            P("ax", None, None),
            P("ax", "ty", "tz", None, None),
        ),
        out_specs=(P(None, "ax", "ty", "tz"), P("ax", None, ("ty", "tz"))),
        check_vma=False,
    )
```

time: 36.8 us -> 34.8 us (0.946)
  local copies, waits for them, and re-layouts: 3.78 us -> 3.07 us
  starting transfers between devices: 14 us -> 13.4 us
  waiting for transfers between devices: 6.84 us -> 6.4 us
    all_to_all x1, starting transfers between devices: 5.84 us -> 4.19 us  [on_device(): lax.all_to_all(sums, ('ax', 'ty', 'tz'), split_axis=0, concat_axis=0, til...]
    ppermute x2, starting transfers between devices: 4.46 us -> 5.33 us  [swap_x(): near = lax.ppermute(first, 'ax', [(i, i ^ 1) for i in range(count)])]
    all_to_all x1, waiting for transfers between devices: 4.92 us -> 4.1 us  [on_device(): lax.all_to_all(sums, ('ax', 'ty', 'tz'), split_axis=0, concat_axis=0, til...]
    unnamed x32 -> x24, local copies, waits for them, and re-layouts: 3.78 us -> 3.07 us
    ppermute x2, waiting for transfers between devices: 1.91 us -> 2.29 us  [swap_x(): near = lax.ppermute(first, 'ax', [(i, i ^ 1) for i in range(count)])]
    pallas_call x5 -> x7, Pallas kernels: 11 us -> 10.7 us  [call(): pl.pallas_call(kernel, out_shape=list(outs), in_specs=[away.get(i, VMEM)...]
  transfers between devices with their start and end apart: 10 -> 10, of which waited for: 2 -> 2; matrix products, arithmetic and copies ran while one was open for 0% -> 0% of each run, Pallas kernels for 13% -> 26%
where the time goes in v3:
time: 34.8 us; the launch traced here: 34.4 us
  starting transfers between devices  13.4 us (39%)
  Pallas kernels  10.7 us (31%)
  waiting for transfers between devices  6.4 us (18%)
  local copies, waits for them, and re-layouts  3.07 us (9%)
  between operations  0.8 us (2%)
    pallas_call x7, Pallas kernels, call(): pl.pallas_call(kernel, out_shape=list(outs), in_specs=[away.get(i, VMEM)...  10.7 us
    ppermute x2, starting transfers between devices, swap_x(): near = lax.ppermute(first, 'ax', [(i, i ^ 1) for i in range(count)])  5.33 us
    all_to_all x1, starting transfers between devices, on_device(): lax.all_to_all(sums, ('ax', 'ty', 'tz'), split_axis=0, concat_axis=0, til...  4.19 us
    all_to_all x1, waiting for transfers between devices, on_device(): lax.all_to_all(sums, ('ax', 'ty', 'tz'), split_axis=0, concat_axis=0, til...  4.1 us
    ppermute x5, starting transfers between devices, ring(): lax.ppermute(v, axis, [(i, (i + step) % count) for i in range(count)])  3.65 us
    unnamed x24, local copies, waits for them, and re-layouts  3.07 us
    ppermute x2, waiting for transfers between devices, swap_x(): near = lax.ppermute(first, 'ax', [(i, i ^ 1) for i in range(count)])  2.29 us
  transfers between devices with their start and end apart: 10, of which 2 were waited for; matrix products, arithmetic and copies ran while one was open for 0% of the time, Pallas kernels for 26%

profile of v3, /device:TPU:0, one launch (start us, length us, event | category | flops | bytes accessed | tf_op | source)
XLA Modules:
  0.0 34.4 jit_solution(15381087597742277971)
XLA Ops:
  0.6 0.0 copy-start
  0.6 0.5 %collective-permute-start = (f32[5,16,16,128]{3,2,1,0:T(8,128)}, f32[5,16,16,128]{3,2,1,0:T(8,128)S(1)}, u32[]{:S(2)}, u32[]{:S(2)}) collective-permute-start(f32[5,16,16,128]{3,2,1,0:T(8,128)} %adj.7), channel_id=1, source_target_pairs={{0,1},{1,0},{2,3},{3,2},{4,5},{5,4},{6,7},{7,6},{8,9},{9,8},{10,11... | collective-permute-start | bytes 1966088 | tf_op jit(solution)/shard_map/ppermute | solution.py:437
  1.2 0.0 copy-start.1
  1.2 0.0 copy-start.6
  1.2 2.7 %shard_map.95 = (f32[7,3,16,128]{3,2,1,0:T(8,128)}, f32[7,3,16,128]{3,2,1,0:T(8,128)}, f32[7,3,16,128]{3,2,1,0:T(8,128)}, f32[2,3,16,128]{3,2,1,0:T(8,128)}, f32[8,128]{1,0:T(8,128)}) custom-call(f32[5,16,16,128]{3,2,1,0:T(8,128)} %adj.7, f32[3,16,16,128]{3,2,1,0:T(8,128)} %vel.11, f32[16,16,128]{2,1,0:T(8,128)} %c.11, s32[1,32]{1,0:T(1,128)} %bitcast.2), custom_call_target="tpu_custom_call" | custom-call | flops 20000000 | bytes 17491200 | tf_op jit(solution)/shard_map/pallas_call | solution.py:448
  3.9 0.0 copy-start.11
  3.9 0.1 collective-permute-start.4
  4.0 3.0 %collective-permute-start.1 = (f32[7,3,16,128]{3,2,1,0:T(8,128)}, f32[7,3,16,128]{3,2,1,0:T(8,128)S(1)}, u32[]{:S(2)}, u32[]{:S(2)}) collective-permute-start(f32[7,3,16,128]{3,2,1,0:T(8,128)} %get-tuple-element.14), channel_id=1, source_target_pairs={{0,4},{4,0},{8,12},{12,8},{16,20},{20,16},{24,28},{28,24},{1,5},{5... | collective-permute-start | bytes 516104 | tf_op jit(solution)/shard_map/ppermute | solution.py:423
  7.0 0.0 collective-permute-start.2
  7.0 0.0 copy-start.10
  7.0 1.5 %collective-permute-start.3 = (f32[7,3,16,128]{3,2,1,0:T(8,128)}, f32[7,3,16,128]{3,2,1,0:T(8,128)S(1)}, u32[]{:S(2)}, u32[]{:S(2)}) collective-permute-start(f32[7,3,16,128]{3,2,1,0:T(8,128)} %get-tuple-element.16), channel_id=1, source_target_pairs={{0,2},{2,0},{1,3},{3,1},{4,6},{6,4},{5,7},{7,5},{8,10},{10,8},{9,1... | collective-permute-start | bytes 516104 | tf_op jit(solution)/shard_map/ppermute | solution.py:437
  8.5 0.0 collective-permute-done.refs_1_
  8.5 0.0 copy-done
  8.5 0.0 copy-done.1
  8.5 0.0 copy-done.6
  8.5 0.0 copy-done.11
  8.5 0.0 copy-done.10
  8.5 0.0 copy-start.2
  8.6 1.1 %copy-done.2 = f32[5,16,16,128]{3,2,1,0:T(8,128)S(1)} copy-done((f32[5,16,16,128]{3,2,1,0:T(8,128)S(1)}, f32[5,16,16,128]{3,2,1,0:T(8,128)}, u32[]{:S(2)}) %copy-start.2) | copy-done | bytes 655384
  9.6 0.0 copy-start.4
  9.6 1.0 %copy-done.4 = bf16[2048,128]{1,0:T(8,128)(2,1)S(1)} copy-done((bf16[2048,128]{1,0:T(8,128)(2,1)S(1)}, bf16[2048,128]{1,0:T(8,128)(2,1)}, u32[]{:S(2)}) %copy-start.4) | copy-done | bytes 524312
  10.7 0.0 copy-start.7
  10.7 0.9 %copy-done.7 = f32[16,16,128]{2,1,0:T(8,128)S(1)} copy-done((f32[16,16,128]{2,1,0:T(8,128)S(1)}, f32[16,16,128]{2,1,0:T(8,128)}, u32[]{:S(2)}) %copy-start.7) | copy-done | bytes 131096
  11.6 0.0 copy-start.5
  11.6 1.0 %shard_map.96.part_ref = f32[5,16,16,128]{3,2,1,0:T(8,128)S(1)} custom-call(f32[5,16,16,128]{3,2,1,0:T(8,128)S(1)} %copy-done, f32[3,16,16,128]{3,2,1,0:T(8,128)S(1)} %copy-done.1, f32[16,16,128]{2,1,0:T(8,128)S(1)} %copy-done.6, f32[16,16,128]{2,1,0:T(8,128)S(1)} %copy-done.7, f32[5,16,16,128]{3,2,1,0:T(8,128)S(1)} %copy-done.2, ...), custom_call_target="tpu_custom_call" | custom-call | flops 2621440000 | bytes 43296000 | tf_op jit(solution)/shard_map/pallas_call | solution.py:448
  12.6 0.0 copy-start.3
  12.6 0.0 copy-start.8
  12.6 0.0 collective-permute-done.4.refs_3_
  12.6 2.3 %collective-permute-done.1.refs_0_ = f32[7,3,16,128]{3,2,1,0:T(8,128)S(1)} collective-permute-done((f32[7,3,16,128]{3,2,1,0:T(8,128)}, f32[7,3,16,128]{3,2,1,0:T(8,128)S(1)}, u32[]{:S(2)}, u32[]{:S(2)}) %collective-permute-start.1) | collective-permute-done | bytes 172064 | tf_op jit(solution)/shard_map/ppermute | solution.py:423
  14.9 0.0 collective-permute-done.2.refs_1_
  14.9 0.0 collective-permute-done.3.refs_2_
  14.9 0.0 copy-done.5
  14.9 1.1 %shard_map.97 = (f32[5,16,16,128]{3,2,1,0:T(8,128)S(1)}, f32[5,3,16,128]{3,2,1,0:T(8,128)}, f32[5,3,16,128]{3,2,1,0:T(8,128)}, f32[5,3,16,128]{3,2,1,0:T(8,128)S(1)}) custom-call(f32[5,16,16,128]{3,2,1,0:T(8,128)S(1)} %shard_map.96.part_ref, f32[3,16,16,128]{3,2,1,0:T(8,128)S(1)} %copy-done.1, f32[16,16,128]{2,1,0:T(8,128)S(1)} %copy-done.6, ...), custom_call_target="tpu_custom_call" | custom-call | flops 655360000 | bytes 38174720 | tf_op jit(solution)/shard_map/pallas_call | solution.py:448
  16.0 0.0 collective-permute-start.5
  16.0 2.4 %collective-permute-start.6 = (f32[5,3,16,128]{3,2,1,0:T(8,128)}, f32[5,3,16,128]{3,2,1,0:T(8,128)S(1)}, u32[]{:S(2)}, u32[]{:S(2)}) collective-permute-start(f32[5,3,16,128]{3,2,1,0:T(8,128)} %get-tuple-element.19), channel_id=1, source_target_pairs={{0,4},{4,0},{8,12},{12,8},{16,20},{20,16},{24,28},{28,24},{1,5},{5... | collective-permute-start | bytes 368648 | tf_op jit(solution)/shard_map/ppermute | solution.py:423
  18.4 0.2 collective-permute-start.7
  18.6 1.5 %collective-permute-start.8 = (f32[5,3,16,128]{3,2,1,0:T(8,128)S(1)}, f32[5,3,16,128]{3,2,1,0:T(8,128)}, u32[]{:S(2)}, u32[]{:S(2)}) collective-permute-start(f32[5,3,16,128]{3,2,1,0:T(8,128)S(1)} %get-tuple-element.21), channel_id=1, source_target_pairs={{0,2},{2,0},{1,3},{3,1},{4,6},{6,4},{5,7},{7,5},{8,10},{10,8},{9,1... | collective-permute-start | bytes 368648 | tf_op jit(solution)/shard_map/ppermute | solution.py:437
  20.1 0.0 copy-done.3
  20.1 0.0 copy-done.8
  20.1 1.1 %shard_map.100 = f32[32,8,128]{2,1,0:T(8,128)} custom-call(f32[5,16,16,128]{3,2,1,0:T(8,128)S(1)} %get-tuple-element.18.mid, f32[5,16,16,128]{3,2,1,0:T(8,128)S(1)} %copy-done, f32[3,16,16,128]{3,2,1,0:T(8,128)S(1)} %copy-done.1, f32[16,16,128]{2,1,0:T(8,128)S(1)} %copy-done.6, f32[16,16,128]{2,1,0:T(8,128)S(1)} %copy-done.8, ...), custom_call_target="tpu_custom_call" | custom-call | flops 655360 | bytes 43664 | tf_op jit(solution)/shard_map/pallas_call | solution.py:448
  21.1 4.2 %all-to-all-start = ((f32[32,8,128]{2,1,0:T(8,128)}), f32[32,8,128]{2,1,0:T(8,128)S(1)}, u32[]{:S(2)}, u32[]{:S(2)}) async-start(f32[32,8,128]{2,1,0:T(8,128)} %shard_map.100), calls=%async_computation | async-start | bytes 262144 | tf_op jit(solution)/shard_map/all_to_all | solution.py:506
  25.3 0.0 collective-permute-done.5.refs_0_
  25.4 2.0 %shard_map.98.part_ref = f32[5,16,16,128]{3,2,1,0:T(8,128)S(1)} custom-call(f32[5,16,16,128]{3,2,1,0:T(8,128)S(1)} %get-tuple-element.18.mid, f32[5,16,16,128]{3,2,1,0:T(8,128)S(1)} %copy-done, f32[3,16,16,128]{3,2,1,0:T(8,128)S(1)} %copy-done.1, f32[16,16,128]{2,1,0:T(8,128)S(1)} %copy-done.6, f32[16,16,128]{2,1,0:T(8,128)S(1)} %copy-done.8, ...), custom_call_target="tpu_custom_call" | custom-call | flops 2621440 | bytes 49807 | tf_op jit(solution)/shard_map/pallas_call | solution.py:448
  27.4 0.0 copy-start.9
  27.4 0.0 collective-permute-done.6.refs_0_
  27.4 0.0 collective-permute-done.7.refs_1_
  27.4 0.0 collective-permute-done.8.refs_2_
  27.4 2.0 %shard_map.99 = (f32[5,16,16,128]{3,2,1,0:T(8,128)}, f32[8,128]{1,0:T(8,128)S(1)}) custom-call(f32[5,16,16,128]{3,2,1,0:T(8,128)S(1)} %shard_map.98.part_ref, f32[3,16,16,128]{3,2,1,0:T(8,128)S(1)} %copy-done.1, f32[16,16,128]{2,1,0:T(8,128)S(1)} %copy-done.6, bf16[2048,128]{1,0:T(8,128)(2,1)S(1)} %copy-done.5, ...), custom_call_target="tpu_custom_call" | custom-call | flops 3276800000 | bytes 32563200 | tf_op jit(solution)/shard_map/pallas_call | solution.py:448
  29.5 4.1 %all-to-all-done.sums_ref = f32[32,8,128]{2,1,0:T(8,128)S(1)} async-done(((f32[32,8,128]{2,1,0:T(8,128)}), f32[32,8,128]{2,1,0:T(8,128)S(1)}, u32[]{:S(2)}, u32[]{:S(2)}) %all-to-all-start) | async-done | bytes 131104 | tf_op jit(solution)/shard_map/all_to_all | solution.py:506
  33.6 0.0 copy-done.9
  33.6 0.8 %shard_map.101 = f32[5,1,32]{2,1,0:T(1,128)} custom-call(f32[32,8,128]{2,1,0:T(8,128)S(1)} %all-to-all-done.sums_ref, f32[1,128,128]{2,1,0:T(8,128)S(1)} %copy-done.9, f32[8,128]{1,0:T(8,128)S(1)} %get-tuple-element.23._), custom_call_target="tpu_custom_call" | custom-call | bytes 2013440 | tf_op jit(solution)/shard_map/pallas_call | solution.py:448
Async XLA Ops:
  0.6 7.9 %copy-start = (f32[5,16,16,128]{3,2,1,0:T(8,128)S(1)}, f32[5,16,16,128]{3,2,1,0:T(8,128)}, u32[]{:S(2)}) copy-start(f32[5,16,16,128]{3,2,1,0:T(8,128)} %adj.7) | copy-start | bytes 1966084
  0.6 7.9 %collective-permute-start = (f32[5,16,16,128]{3,2,1,0:T(8,128)}, f32[5,16,16,128]{3,2,1,0:T(8,128)S(1)}, u32[]{:S(2)}, u32[]{:S(2)}) collective-permute-start(f32[5,16,16,128]{3,2,1,0:T(8,128)} %adj.7), channel_id=1, source_target_pairs={{0,1},{1,0},{2,3},{3,2},{4,5},{5,4},{6,7},{7,6},{8,9},{9,8},{10,11... | collective-permute-start | bytes 1966088 | tf_op jit(solution)/shard_map/ppermute | solution.py:437
  1.2 7.4 %copy-start.1 = (f32[3,16,16,128]{3,2,1,0:T(8,128)S(1)}, f32[3,16,16,128]{3,2,1,0:T(8,128)}, u32[]{:S(2)}) copy-start(f32[3,16,16,128]{3,2,1,0:T(8,128)} %vel.11) | copy-start | bytes 1179652
  1.2 7.4 %copy-start.6 = (f32[16,16,128]{2,1,0:T(8,128)S(1)}, f32[16,16,128]{2,1,0:T(8,128)}, u32[]{:S(2)}) copy-start(f32[16,16,128]{2,1,0:T(8,128)} %c.11) | copy-start | bytes 393220
  3.9 4.6 %copy-start.11 = (f32[8,128]{1,0:T(8,128)S(1)}, f32[8,128]{1,0:T(8,128)}, u32[]{:S(2)}) copy-start(f32[8,128]{1,0:T(8,128)} %get-tuple-element.13._) | copy-start | bytes 12292
  3.9 8.7 %collective-permute-start.4 = (f32[2,3,16,128]{3,2,1,0:T(8,128)}, f32[2,3,16,128]{3,2,1,0:T(8,128)S(1)}, u32[]{:S(2)}, u32[]{:S(2)}) collective-permute-start(f32[2,3,16,128]{3,2,1,0:T(8,128)} %get-tuple-element.17), channel_id=1, source_target_pairs={{0,1},{1,0},{2,3},{3,2},{4,5},{5,4},{6,7},{7,6},{8,9},{9,8},{10,11... | collective-permute-start | bytes 147464 | tf_op jit(solution)/shard_map/ppermute | solution.py:437
  4.0 10.8 %collective-permute-start.1 = (f32[7,3,16,128]{3,2,1,0:T(8,128)}, f32[7,3,16,128]{3,2,1,0:T(8,128)S(1)}, u32[]{:S(2)}, u32[]{:S(2)}) collective-permute-start(f32[7,3,16,128]{3,2,1,0:T(8,128)} %get-tuple-element.14), channel_id=1, source_target_pairs={{0,4},{4,0},{8,12},{12,8},{16,20},{20,16},{24,28},{28,24},{1,5},{5... | collective-permute-start | bytes 516104 | tf_op jit(solution)/shard_map/ppermute | solution.py:423
  7.0 7.9 %collective-permute-start.2 = (f32[7,3,16,128]{3,2,1,0:T(8,128)}, f32[7,3,16,128]{3,2,1,0:T(8,128)S(1)}, u32[]{:S(2)}, u32[]{:S(2)}) collective-permute-start(f32[7,3,16,128]{3,2,1,0:T(8,128)} %get-tuple-element.15), channel_id=1, source_target_pairs={{0,1},{1,0},{4,8},{5,9},{8,4},{9,5},{12,16},{13,17},{16,12},{17,13... | collective-permute-start | bytes 516104 | tf_op jit(solution)/shard_map/ppermute | solution.py:432
  7.0 1.5 %copy-start.10 = (s32[1,1,1,32,1]{3,4,2,1,0:T(1,128)S(1)}, s32[1,1,1,32,1]{3,4,2,1,0:T(1,128)}, u32[]{:S(2)}) copy-start(s32[1,1,1,32,1]{3,4,2,1,0:T(1,128)} %param.14) | copy-start | bytes 388
  7.0 7.9 %collective-permute-start.3 = (f32[7,3,16,128]{3,2,1,0:T(8,128)}, f32[7,3,16,128]{3,2,1,0:T(8,128)S(1)}, u32[]{:S(2)}, u32[]{:S(2)}) collective-permute-start(f32[7,3,16,128]{3,2,1,0:T(8,128)} %get-tuple-element.16), channel_id=1, source_target_pairs={{0,2},{2,0},{1,3},{3,1},{4,6},{6,4},{5,7},{7,5},{8,10},{10,8},{9,1... | collective-permute-start | bytes 516104 | tf_op jit(solution)/shard_map/ppermute | solution.py:437
  8.5 1.1 %copy-start.2 = (f32[5,16,16,128]{3,2,1,0:T(8,128)S(1)}, f32[5,16,16,128]{3,2,1,0:T(8,128)}, u32[]{:S(2)}) copy-start(f32[5,16,16,128]{3,2,1,0:T(8,128)} %source.5) | copy-start | bytes 1966084
  9.6 1.0 %copy-start.4 = (bf16[2048,128]{1,0:T(8,128)(2,1)S(1)}, bf16[2048,128]{1,0:T(8,128)(2,1)}, u32[]{:S(2)}) copy-start(bf16[2048,128]{1,0:T(8,128)(2,1)} %constant.2.clone.table) | copy-start | bytes 1572868
  10.7 0.9 %copy-start.7 = (f32[16,16,128]{2,1,0:T(8,128)S(1)}, f32[16,16,128]{2,1,0:T(8,128)}, u32[]{:S(2)}) copy-start(f32[16,16,128]{2,1,0:T(8,128)} %sponge.5) | copy-start | bytes 393220
  11.6 3.3 %copy-start.5 = (bf16[2048,128]{1,0:T(8,128)(2,1)S(1)}, bf16[2048,128]{1,0:T(8,128)(2,1)}, u32[]{:S(2)}) copy-start(bf16[2048,128]{1,0:T(8,128)(2,1)} %constant.2.clone.table) | copy-start | bytes 1572868
  12.6 7.5 %copy-start.3 = (f32[5,16,16,128]{3,2,1,0:T(8,128)S(1)}, f32[5,16,16,128]{3,2,1,0:T(8,128)}, u32[]{:S(2)}) copy-start(f32[5,16,16,128]{3,2,1,0:T(8,128)} %source.5) | copy-start | bytes 1966084
  12.6 7.5 %copy-start.8 = (f32[16,16,128]{2,1,0:T(8,128)S(1)}, f32[16,16,128]{2,1,0:T(8,128)}, u32[]{:S(2)}) copy-start(f32[16,16,128]{2,1,0:T(8,128)} %sponge.5) | copy-start | bytes 393220
  16.0 9.4 %collective-permute-start.5 = (f32[5,16,16,128]{3,2,1,0:T(8,128)S(1)}, f32[5,16,16,128]{3,2,1,0:T(8,128)}, u32[]{:S(2)}, u32[]{:S(2)}) collective-permute-start(f32[5,16,16,128]{3,2,1,0:T(8,128)S(1)} %get-tuple-element.18.mid), channel_id=1, source_target_pairs={{0,1},{1,0},{2,3},{3,2},{4,5},{5,4},{6,7},{7,6},{8,9},{9,8},{10,11... | collective-permute-start | bytes 1966088 | tf_op jit(solution)/shard_map/ppermute | solution.py:437
  16.0 11.4 %collective-permute-start.6 = (f32[5,3,16,128]{3,2,1,0:T(8,128)}, f32[5,3,16,128]{3,2,1,0:T(8,128)S(1)}, u32[]{:S(2)}, u32[]{:S(2)}) collective-permute-start(f32[5,3,16,128]{3,2,1,0:T(8,128)} %get-tuple-element.19), channel_id=1, source_target_pairs={{0,4},{4,0},{8,12},{12,8},{16,20},{20,16},{24,28},{28,24},{1,5},{5... | collective-permute-start | bytes 368648 | tf_op jit(solution)/shard_map/ppermute | solution.py:423
  18.4 9.0 %collective-permute-start.7 = (f32[5,3,16,128]{3,2,1,0:T(8,128)}, f32[5,3,16,128]{3,2,1,0:T(8,128)}, u32[]{:S(2)}, u32[]{:S(2)}) collective-permute-start(f32[5,3,16,128]{3,2,1,0:T(8,128)} %get-tuple-element.20), channel_id=1, source_target_pairs={{0,1},{1,0},{4,8},{5,9},{8,4},{9,5},{12,16},{13,17},{16,12},{17,13... | collective-permute-start | bytes 368648 | tf_op jit(solution)/shard_map/ppermute | solution.py:432
  18.6 8.8 %collective-permute-start.8 = (f32[5,3,16,128]{3,2,1,0:T(8,128)S(1)}, f32[5,3,16,128]{3,2,1,0:T(8,128)}, u32[]{:S(2)}, u32[]{:S(2)}) collective-permute-start(f32[5,3,16,128]{3,2,1,0:T(8,128)S(1)} %get-tuple-element.21), channel_id=1, source_target_pairs={{0,2},{2,0},{1,3},{3,1},{4,6},{6,4},{5,7},{7,5},{8,10},{10,8},{9,1... | collective-permute-start | bytes 368648 | tf_op jit(solution)/shard_map/ppermute | solution.py:437
  21.1 12.4 %all-to-all-start = ((f32[32,8,128]{2,1,0:T(8,128)}), f32[32,8,128]{2,1,0:T(8,128)S(1)}, u32[]{:S(2)}, u32[]{:S(2)}) async-start(f32[32,8,128]{2,1,0:T(8,128)} %shard_map.100), calls=%async_computation | async-start | bytes 262144 | tf_op jit(solution)/shard_map/all_to_all | solution.py:506
  27.4 6.2 %copy-start.9 = (f32[1,128,128]{2,1,0:T(8,128)S(1)}, f32[1,128,128]{2,1,0:T(8,128)}, u32[]{:S(2)}) copy-start(f32[1,128,128]{2,1,0:T(8,128)} %basis_ref.1) | copy-start | bytes 196612

commit v4 on v3

--- a/solution.py
+++ b/solution.py
@@ -142,7 +142,7 @@
 
 def pack_first(adj, vel, c, owner_ref, *refs):
     n_y = len(sides_of("ty"))
-    x_msgs, y_msgs, (aux, token, rows, speeds, sems) = refs[:2], refs[2 : 2 + n_y], refs[2 + n_y :]
+    x_msgs, y_msgs, (aux, token, rows, speeds, names, sems) = refs[:2], refs[2 : 2 + n_y], refs[2 + n_y :]
     nx, ny, nz = adj.shape[1:]
     half = rows.shape[3]
     at = lax.axis_index("ty")
@@ -164,13 +164,14 @@
         copy(adj.at[:, pl.ds(start_of(up, nx), HALO)], ref.at[:5])
     copy(vel.at[:, :FACE_PLANES], speeds.at[:3])
     copy(c.at[:FACE_PLANES], speeds.at[3])
+    copy(owner_ref, names)
+    for one in copies[-3:]:
+        one.wait()
     token[...] = jnp.zeros(token.shape, F32)
-    blocks = owner_ref.shape[1]
+    blocks = names.shape[1]
     eye = lax.broadcasted_iota(jnp.int32, (blocks, blocks), 0) == lax.broadcasted_iota(jnp.int32, (blocks, blocks), 1)
-    column = jnp.sum(jnp.where(eye, owner_ref[...].astype(F32), 0.0), axis=1, keepdims=True)
+    column = jnp.sum(jnp.where(eye, names[...].astype(F32), 0.0), axis=1, keepdims=True)
     owners = jnp.broadcast_to(column, (blocks, nz)).reshape(FACE_PLANES, ny, nz)
-    for one in copies:
-        one.wait()
     for d, msgs in enumerate((x_msgs, y_msgs, (aux,))):
         for ref in msgs:
             n = ref.shape[0]
@@ -178,6 +179,8 @@
             ref[n - 1, :2] = speeds[3]
             ref[n - 2, 2] = owners[0]
             ref[n - 1, 2] = owners[1]
+    for one in copies[:-3]:
+        one.wait()
     for i, (ref, top) in enumerate(zip(y_msgs, tops)):
 
         def put(r, ref=ref, i=i):
@@ -472,8 +475,8 @@
         pack_first,
         [adjoint, velocity, sound_speed, owners],
         [shape(7, HALO, ny, nz)] * 2 + [shape(7, HALO, nx, nz)] * n_y + [shape(2, HALO, ny, nz), shape(8, nz)],
-        [pltpu.VMEM((n_y, 5, nx, 8, nz), F32), pltpu.VMEM((4, FACE_PLANES, ny, nz), F32), pltpu.SemaphoreType.DMA((8,))],
-        away={0: HBM, 1: HBM, 2: HBM},
+        [pltpu.VMEM((n_y, 5, nx, 8, nz), F32), pltpu.VMEM((4, FACE_PLANES, ny, nz), F32), pltpu.VMEM(owners.shape, jnp.int32), pltpu.SemaphoreType.DMA((8,))],
+        away={i: HBM for i in range(4)},
         grant=60, flops=10**6,
     )
     z_blocks = from_sides("tz", adjoint, adjoint)
@@ -501,11 +504,10 @@
         [shape(devices, 8, nz)],
         flops=work // 4,
         grant=8,
-        hint=(0.02, 0.01),
     )
     sums = lax.all_to_all(sums, ("ax", "ty", "tz"), split_axis=0, concat_axis=0, tiled=True)
     (part,) = call(
-        second_kernel, [mid, adjoint, *fields, *z_blocks], [brick], grads, flops=work, grant=8, hint=(0.02, 0.01)
+        second_kernel, [mid, adjoint, *fields, *z_blocks], [brick], grads, flops=work, grant=8
     )
     adjoint_out, token = call(
         final_kernel,
@@ -515,7 +517,6 @@
         out_away={0: HBM},
         flops=work // 4,
         grant=6,
-        hint=(100, 10),
     )
     share = mode_basis.shape[2] // (n_ty * n_tz)
     scale = 1.0 / math.sqrt(FACE_PLANES * ny * n_ty * n_tz)

time: 34.8 us -> 32.7 us (0.940)
  Pallas kernels: 10.7 us -> 8.45 us
  starting transfers between devices: 13.4 us -> 14.3 us
  waiting for transfers between devices: 6.4 us -> 5.71 us
    all_to_all x1, waiting for transfers between devices: 4.1 us -> 0.01 us  [on_device(): lax.all_to_all(sums, ('ax', 'ty', 'tz'), split_axis=0, concat_axis=0, til...]
    ppermute x2, waiting for transfers between devices: 2.29 us -> 5.69 us  [swap_x(): near = lax.ppermute(first, 'ax', [(i, i ^ 1) for i in range(count)])]
    pallas_call x7, Pallas kernels: 10.7 us -> 8.45 us  [call(): pl.pallas_call(kernel, out_shape=list(outs), in_specs=[away.get(i, VMEM)...]
    all_to_all x1, starting transfers between devices: 4.19 us -> 5.83 us  [on_device(): lax.all_to_all(sums, ('ax', 'ty', 'tz'), split_axis=0, concat_axis=0, til...]
    ppermute x2, starting transfers between devices: 5.33 us -> 4.79 us  [swap_x(): near = lax.ppermute(first, 'ax', [(i, i ^ 1) for i in range(count)])]
    unnamed x24 -> x26, local copies, waits for them, and re-layouts: 3.07 us -> 3.08 us
  transfers between devices with their start and end apart: 10 -> 10, of which waited for: 2 -> 2; matrix products, arithmetic and copies ran while one was open for 0% -> 0% of each run, Pallas kernels for 26% -> 22%
where the time goes in v4:
time: 32.7 us; the launch traced here: 32.4 us
  starting transfers between devices  14.3 us (44%)
  Pallas kernels  8.45 us (26%)
  waiting for transfers between devices  5.71 us (17%)
  local copies, waits for them, and re-layouts  3.08 us (9%)
  between operations  0.82 us (3%)
    pallas_call x7, Pallas kernels, call(): pl.pallas_call(kernel, out_shape=list(outs), in_specs=[away.get(i, VMEM)...  8.45 us
    all_to_all x1, starting transfers between devices, on_device(): lax.all_to_all(sums, ('ax', 'ty', 'tz'), split_axis=0, concat_axis=0, til...  5.83 us
    ppermute x2, waiting for transfers between devices, swap_x(): near = lax.ppermute(first, 'ax', [(i, i ^ 1) for i in range(count)])  5.69 us
    ppermute x2, starting transfers between devices, swap_x(): near = lax.ppermute(first, 'ax', [(i, i ^ 1) for i in range(count)])  4.79 us
    ppermute x5, starting transfers between devices, ring(): lax.ppermute(v, axis, [(i, (i + step) % count) for i in range(count)])  3.68 us
    unnamed x26, local copies, waits for them, and re-layouts  3.08 us
  transfers between devices with their start and end apart: 10, of which 2 were waited for; matrix products, arithmetic and copies ran while one was open for 0% of the time, Pallas kernels for 22%

profile of v4, /device:TPU:0, one launch (start us, length us, event | category | flops | bytes accessed | tf_op | source)
XLA Modules:
  0.0 32.4 jit_solution(16831892627073267798)
XLA Ops:
  0.6 0.0 copy-start
  0.6 0.5 %collective-permute-start = (f32[5,16,16,128]{3,2,1,0:T(8,128)}, f32[5,16,16,128]{3,2,1,0:T(8,128)S(1)}, u32[]{:S(2)}, u32[]{:S(2)}) collective-permute-start(f32[5,16,16,128]{3,2,1,0:T(8,128)} %adj.7), channel_id=1, source_target_pairs={{0,1},{1,0},{2,3},{3,2},{4,5},{5,4},{6,7},{7,6},{8,9},{9,8},{10,11... | collective-permute-start | bytes 1966088 | tf_op jit(solution)/shard_map/ppermute | solution.py:440
  1.2 0.0 copy-start.1
  1.2 0.0 copy-start.4
  1.2 2.1 %shard_map.95 = (f32[7,3,16,128]{3,2,1,0:T(8,128)}, f32[7,3,16,128]{3,2,1,0:T(8,128)}, f32[7,3,16,128]{3,2,1,0:T(8,128)}, f32[2,3,16,128]{3,2,1,0:T(8,128)}, f32[8,128]{1,0:T(8,128)}) custom-call(f32[5,16,16,128]{3,2,1,0:T(8,128)} %adj.7, f32[3,16,16,128]{3,2,1,0:T(8,128)} %vel.11, f32[16,16,128]{2,1,0:T(8,128)} %c.11, s32[1,32]{1,0:T(1,128)} %bitcast.2), custom_call_target="tpu_custom_call" | custom-call | flops 20000000 | bytes 17491200 | tf_op jit(solution)/shard_map/pallas_call | solution.py:451
  3.3 0.0 copy-start.12
  3.3 0.1 collective-permute-start.4
  3.4 3.0 %collective-permute-start.1 = (f32[7,3,16,128]{3,2,1,0:T(8,128)}, f32[7,3,16,128]{3,2,1,0:T(8,128)S(1)}, u32[]{:S(2)}, u32[]{:S(2)}) collective-permute-start(f32[7,3,16,128]{3,2,1,0:T(8,128)} %get-tuple-element.14), channel_id=1, source_target_pairs={{0,4},{4,0},{8,12},{12,8},{16,20},{20,16},{24,28},{28,24},{1,5},{5... | collective-permute-start | bytes 516104 | tf_op jit(solution)/shard_map/ppermute | solution.py:426
  6.4 0.0 collective-permute-start.2
  6.4 0.0 copy-start.10
  6.4 1.5 %collective-permute-start.3 = (f32[7,3,16,128]{3,2,1,0:T(8,128)}, f32[7,3,16,128]{3,2,1,0:T(8,128)S(1)}, u32[]{:S(2)}, u32[]{:S(2)}) collective-permute-start(f32[7,3,16,128]{3,2,1,0:T(8,128)} %get-tuple-element.16), channel_id=1, source_target_pairs={{0,2},{2,0},{1,3},{3,1},{4,6},{6,4},{5,7},{7,5},{8,10},{10,8},{9,1... | collective-permute-start | bytes 516104 | tf_op jit(solution)/shard_map/ppermute | solution.py:440
  7.9 0.0 collective-permute-done.refs_1_
  7.9 0.0 copy-done
  7.9 0.0 copy-done.1
  7.9 0.0 copy-done.4
  7.9 0.0 copy-done.12
  7.9 0.0 copy-done.10
  7.9 0.0 copy-start.2
  7.9 1.1 %copy-done.2 = f32[5,16,16,128]{3,2,1,0:T(8,128)S(1)} copy-done((f32[5,16,16,128]{3,2,1,0:T(8,128)S(1)}, f32[5,16,16,128]{3,2,1,0:T(8,128)}, u32[]{:S(2)}) %copy-start.2) | copy-done | bytes 655384
  9.0 0.0 copy-start.5
  9.0 1.0 %copy-done.5 = bf16[2048,128]{1,0:T(8,128)(2,1)S(1)} copy-done((bf16[2048,128]{1,0:T(8,128)(2,1)S(1)}, bf16[2048,128]{1,0:T(8,128)(2,1)}, u32[]{:S(2)}) %copy-start.5) | copy-done | bytes 524312
  10.0 0.0 copy-start.7
  10.0 0.9 %copy-done.7 = f32[16,16,128]{2,1,0:T(8,128)S(1)} copy-done((f32[16,16,128]{2,1,0:T(8,128)S(1)}, f32[16,16,128]{2,1,0:T(8,128)}, u32[]{:S(2)}) %copy-start.7) | copy-done | bytes 131096
  10.9 0.0 copy-start.6
  10.9 1.0 %shard_map.96.part_ref = f32[5,16,16,128]{3,2,1,0:T(8,128)S(1)} custom-call(f32[5,16,16,128]{3,2,1,0:T(8,128)S(1)} %copy-done, f32[3,16,16,128]{3,2,1,0:T(8,128)S(1)} %copy-done.1, f32[16,16,128]{2,1,0:T(8,128)S(1)} %copy-done.4, f32[16,16,128]{2,1,0:T(8,128)S(1)} %copy-done.7, f32[5,16,16,128]{3,2,1,0:T(8,128)S(1)} %copy-done.2, ...), custom_call_target="tpu_custom_call" | custom-call | flops 2621440000 | bytes 43296000 | tf_op jit(solution)/shard_map/pallas_call | solution.py:451
  11.9 0.0 copy-start.3
  11.9 0.0 copy-start.8
  11.9 0.0 collective-permute-done.4.refs_3_
  12.0 2.3 %collective-permute-done.1.refs_0_ = f32[7,3,16,128]{3,2,1,0:T(8,128)S(1)} collective-permute-done((f32[7,3,16,128]{3,2,1,0:T(8,128)}, f32[7,3,16,128]{3,2,1,0:T(8,128)S(1)}, u32[]{:S(2)}, u32[]{:S(2)}) %collective-permute-start.1) | collective-permute-done | bytes 172064 | tf_op jit(solution)/shard_map/ppermute | solution.py:426
  14.3 0.0 collective-permute-done.2.refs_1_
  14.3 0.0 collective-permute-done.3.refs_2_
  14.3 0.0 copy-done.6
  14.3 0.4 %shard_map.97 = (f32[5,16,16,128]{3,2,1,0:T(8,128)S(1)}, f32[5,3,16,128]{3,2,1,0:T(8,128)S(1)}, f32[5,3,16,128]{3,2,1,0:T(8,128)S(1)}, f32[5,3,16,128]{3,2,1,0:T(8,128)S(1)}) custom-call(f32[5,16,16,128]{3,2,1,0:T(8,128)S(1)} %shard_map.96.part_ref, f32[3,16,16,128]{3,2,1,0:T(8,128)S(1)} %copy-done.1, f32[16,16,128]{2,1,0:T(8,128)S(1)} %copy-done.4, ...), custom_call_target="tpu_custom_call" | custom-call | flops 655360000 | bytes 38174720 | tf_op jit(solution)/shard_map/pallas_call | solution.py:451
  14.7 0.0 copy-start.11
  14.7 0.1 collective-permute-start.5
  14.7 0.0 copy-done.3
  14.8 0.0 copy-done.8
  14.8 1.1 %shard_map.100 = f32[32,8,128]{2,1,0:T(8,128)} custom-call(f32[5,16,16,128]{3,2,1,0:T(8,128)S(1)} %get-tuple-element.18.mid, f32[5,16,16,128]{3,2,1,0:T(8,128)S(1)} %copy-done, f32[3,16,16,128]{3,2,1,0:T(8,128)S(1)} %copy-done.1, f32[16,16,128]{2,1,0:T(8,128)S(1)} %copy-done.4, f32[16,16,128]{2,1,0:T(8,128)S(1)} %copy-done.8, ...), custom_call_target="tpu_custom_call" | custom-call | flops 655360000 | bytes 43664640 | tf_op jit(solution)/shard_map/pallas_call | solution.py:451
  15.8 0.0 copy-done.11
  15.8 5.8 %all-to-all-start = ((f32[32,8,128]{2,1,0:T(8,128)}), f32[32,8,128]{2,1,0:T(8,128)S(1)}, u32[]{:S(2)}, u32[]{:S(2)}) async-start(f32[32,8,128]{2,1,0:T(8,128)} %shard_map.100), calls=%async_computation | async-start | bytes 262144 | tf_op jit(solution)/shard_map/all_to_all | solution.py:508
  21.7 1.8 %collective-permute-start.6 = (f32[5,3,16,128]{3,2,1,0:T(8,128)}, f32[5,3,16,128]{3,2,1,0:T(8,128)S(1)}, u32[]{:S(2)}, u32[]{:S(2)}) collective-permute-start(f32[5,3,16,128]{3,2,1,0:T(8,128)} %copy-done.11), channel_id=1, source_target_pairs={{0,4},{4,0},{8,12},{12,8},{16,20},{20,16},{24,28},{28,24},{1,5},{5... | collective-permute-start | bytes 368648 | tf_op jit(solution)/shard_map/ppermute | solution.py:426
  23.5 0.0 collective-permute-start.7
  23.5 1.5 %collective-permute-start.8 = (f32[5,3,16,128]{3,2,1,0:T(8,128)S(1)}, f32[5,3,16,128]{3,2,1,0:T(8,128)S(1)}, u32[]{:S(2)}, u32[]{:S(2)}) collective-permute-start(f32[5,3,16,128]{3,2,1,0:T(8,128)S(1)} %get-tuple-element.21), channel_id=1, source_target_pairs={{0,2},{2,0},{1,3},{3,1},{4,6},{6,4},{5,7},{7,5},{8,10},{10,8},{9,1... | collective-permute-start | bytes 368648 | tf_op jit(solution)/shard_map/ppermute | solution.py:440
  25.0 0.0 collective-permute-done.5.refs_0_
  25.0 2.0 %shard_map.98.part_ref = f32[5,16,16,128]{3,2,1,0:T(8,128)S(1)} custom-call(f32[5,16,16,128]{3,2,1,0:T(8,128)S(1)} %get-tuple-element.18.mid, f32[5,16,16,128]{3,2,1,0:T(8,128)S(1)} %copy-done, f32[3,16,16,128]{3,2,1,0:T(8,128)S(1)} %copy-done.1, f32[16,16,128]{2,1,0:T(8,128)S(1)} %copy-done.4, f32[16,16,128]{2,1,0:T(8,128)S(1)} %copy-done.8, ...), custom_call_target="tpu_custom_call" | custom-call | flops 2621440000 | bytes 49807360 | tf_op jit(solution)/shard_map/pallas_call | solution.py:451
  27.0 0.0 copy-start.9
  27.0 3.4 %collective-permute-done.6.refs_0_ = f32[5,3,16,128]{3,2,1,0:T(8,128)S(1)} collective-permute-done((f32[5,3,16,128]{3,2,1,0:T(8,128)}, f32[5,3,16,128]{3,2,1,0:T(8,128)S(1)}, u32[]{:S(2)}, u32[]{:S(2)}) %collective-permute-start.6) | collective-permute-done | bytes 122912 | tf_op jit(solution)/shard_map/ppermute | solution.py:426
  30.4 0.0 collective-permute-done.7.refs_1_
  30.4 0.0 collective-permute-done.8.refs_2_
  30.4 1.1 %shard_map.99 = (f32[5,16,16,128]{3,2,1,0:T(8,128)}, f32[8,128]{1,0:T(8,128)S(1)}) custom-call(f32[5,16,16,128]{3,2,1,0:T(8,128)S(1)} %shard_map.98.part_ref, f32[3,16,16,128]{3,2,1,0:T(8,128)S(1)} %copy-done.1, f32[16,16,128]{2,1,0:T(8,128)S(1)} %copy-done.4, bf16[2048,128]{1,0:T(8,128)(2,1)S(1)} %copy-done.6, ...), custom_call_target="tpu_custom_call" | custom-call | flops 655360000 | bytes 32563200 | tf_op jit(solution)/shard_map/pallas_call | solution.py:451
  31.5 0.0 all-to-all-done.sums_ref
  31.5 0.0 copy-done.9
  31.5 0.8 %shard_map.101 = f32[5,1,32]{2,1,0:T(1,128)} custom-call(f32[32,8,128]{2,1,0:T(8,128)S(1)} %all-to-all-done.sums_ref, f32[1,128,128]{2,1,0:T(8,128)S(1)} %copy-done.9, f32[8,128]{1,0:T(8,128)S(1)} %get-tuple-element.23._), custom_call_target="tpu_custom_call" | custom-call | bytes 2013440 | tf_op jit(solution)/shard_map/pallas_call | solution.py:451
Async XLA Ops:
  0.6 7.2 %copy-start = (f32[5,16,16,128]{3,2,1,0:T(8,128)S(1)}, f32[5,16,16,128]{3,2,1,0:T(8,128)}, u32[]{:S(2)}) copy-start(f32[5,16,16,128]{3,2,1,0:T(8,128)} %adj.7) | copy-start | bytes 1966084
  0.6 7.2 %collective-permute-start = (f32[5,16,16,128]{3,2,1,0:T(8,128)}, f32[5,16,16,128]{3,2,1,0:T(8,128)S(1)}, u32[]{:S(2)}, u32[]{:S(2)}) collective-permute-start(f32[5,16,16,128]{3,2,1,0:T(8,128)} %adj.7), channel_id=1, source_target_pairs={{0,1},{1,0},{2,3},{3,2},{4,5},{5,4},{6,7},{7,6},{8,9},{9,8},{10,11... | collective-permute-start | bytes 1966088 | tf_op jit(solution)/shard_map/ppermute | solution.py:440
  1.2 6.7 %copy-start.1 = (f32[3,16,16,128]{3,2,1,0:T(8,128)S(1)}, f32[3,16,16,128]{3,2,1,0:T(8,128)}, u32[]{:S(2)}) copy-start(f32[3,16,16,128]{3,2,1,0:T(8,128)} %vel.11) | copy-start | bytes 1179652
  1.2 6.7 %copy-start.4 = (f32[16,16,128]{2,1,0:T(8,128)S(1)}, f32[16,16,128]{2,1,0:T(8,128)}, u32[]{:S(2)}) copy-start(f32[16,16,128]{2,1,0:T(8,128)} %c.11) | copy-start | bytes 393220
  3.3 4.6 %copy-start.12 = (f32[8,128]{1,0:T(8,128)S(1)}, f32[8,128]{1,0:T(8,128)}, u32[]{:S(2)}) copy-start(f32[8,128]{1,0:T(8,128)} %get-tuple-element.13._) | copy-start | bytes 12292
  3.3 8.7 %collective-permute-start.4 = (f32[2,3,16,128]{3,2,1,0:T(8,128)}, f32[2,3,16,128]{3,2,1,0:T(8,128)S(1)}, u32[]{:S(2)}, u32[]{:S(2)}) collective-permute-start(f32[2,3,16,128]{3,2,1,0:T(8,128)} %get-tuple-element.17), channel_id=1, source_target_pairs={{0,1},{1,0},{2,3},{3,2},{4,5},{5,4},{6,7},{7,6},{8,9},{9,8},{10,11... | collective-permute-start | bytes 147464 | tf_op jit(solution)/shard_map/ppermute | solution.py:440
  3.4 10.8 %collective-permute-start.1 = (f32[7,3,16,128]{3,2,1,0:T(8,128)}, f32[7,3,16,128]{3,2,1,0:T(8,128)S(1)}, u32[]{:S(2)}, u32[]{:S(2)}) collective-permute-start(f32[7,3,16,128]{3,2,1,0:T(8,128)} %get-tuple-element.14), channel_id=1, source_target_pairs={{0,4},{4,0},{8,12},{12,8},{16,20},{20,16},{24,28},{28,24},{1,5},{5... | collective-permute-start | bytes 516104 | tf_op jit(solution)/shard_map/ppermute | solution.py:426
  6.4 7.9 %collective-permute-start.2 = (f32[7,3,16,128]{3,2,1,0:T(8,128)}, f32[7,3,16,128]{3,2,1,0:T(8,128)S(1)}, u32[]{:S(2)}, u32[]{:S(2)}) collective-permute-start(f32[7,3,16,128]{3,2,1,0:T(8,128)} %get-tuple-element.15), channel_id=1, source_target_pairs={{0,1},{1,0},{4,8},{5,9},{8,4},{9,5},{12,16},{13,17},{16,12},{17,13... | collective-permute-start | bytes 516104 | tf_op jit(solution)/shard_map/ppermute | solution.py:435
  6.4 1.5 %copy-start.10 = (s32[1,1,1,32,1]{3,4,2,1,0:T(1,128)S(1)}, s32[1,1,1,32,1]{3,4,2,1,0:T(1,128)}, u32[]{:S(2)}) copy-start(s32[1,1,1,32,1]{3,4,2,1,0:T(1,128)} %param.14) | copy-start | bytes 388
  6.4 7.9 %collective-permute-start.3 = (f32[7,3,16,128]{3,2,1,0:T(8,128)}, f32[7,3,16,128]{3,2,1,0:T(8,128)S(1)}, u32[]{:S(2)}, u32[]{:S(2)}) collective-permute-start(f32[7,3,16,128]{3,2,1,0:T(8,128)} %get-tuple-element.16), channel_id=1, source_target_pairs={{0,2},{2,0},{1,3},{3,1},{4,6},{6,4},{5,7},{7,5},{8,10},{10,8},{9,1... | collective-permute-start | bytes 516104 | tf_op jit(solution)/shard_map/ppermute | solution.py:440
  7.9 1.1 %copy-start.2 = (f32[5,16,16,128]{3,2,1,0:T(8,128)S(1)}, f32[5,16,16,128]{3,2,1,0:T(8,128)}, u32[]{:S(2)}) copy-start(f32[5,16,16,128]{3,2,1,0:T(8,128)} %source.5) | copy-start | bytes 1966084
  9.0 1.0 %copy-start.5 = (bf16[2048,128]{1,0:T(8,128)(2,1)S(1)}, bf16[2048,128]{1,0:T(8,128)(2,1)}, u32[]{:S(2)}) copy-start(bf16[2048,128]{1,0:T(8,128)(2,1)} %constant.2.clone.table) | copy-start | bytes 1572868
  10.0 0.9 %copy-start.7 = (f32[16,16,128]{2,1,0:T(8,128)S(1)}, f32[16,16,128]{2,1,0:T(8,128)}, u32[]{:S(2)}) copy-start(f32[16,16,128]{2,1,0:T(8,128)} %sponge.5) | copy-start | bytes 393220
  10.9 3.3 %copy-start.6 = (bf16[2048,128]{1,0:T(8,128)(2,1)S(1)}, bf16[2048,128]{1,0:T(8,128)(2,1)}, u32[]{:S(2)}) copy-start(bf16[2048,128]{1,0:T(8,128)(2,1)} %constant.2.clone.table) | copy-start | bytes 1572868
  11.9 2.8 %copy-start.3 = (f32[5,16,16,128]{3,2,1,0:T(8,128)S(1)}, f32[5,16,16,128]{3,2,1,0:T(8,128)}, u32[]{:S(2)}) copy-start(f32[5,16,16,128]{3,2,1,0:T(8,128)} %source.5) | copy-start | bytes 1966084
  11.9 2.8 %copy-start.8 = (f32[16,16,128]{2,1,0:T(8,128)S(1)}, f32[16,16,128]{2,1,0:T(8,128)}, u32[]{:S(2)}) copy-start(f32[16,16,128]{2,1,0:T(8,128)} %sponge.5) | copy-start | bytes 393220
  14.7 1.2 %copy-start.11 = (f32[5,3,16,128]{3,2,1,0:T(8,128)}, f32[5,3,16,128]{3,2,1,0:T(8,128)S(1)}, u32[]{:S(2)}) copy-start(f32[5,3,16,128]{3,2,1,0:T(8,128)S(1)} %get-tuple-element.19) | copy-start | bytes 368644
  14.7 10.3 %collective-permute-start.5 = (f32[5,16,16,128]{3,2,1,0:T(8,128)S(1)}, f32[5,16,16,128]{3,2,1,0:T(8,128)}, u32[]{:S(2)}, u32[]{:S(2)}) collective-permute-start(f32[5,16,16,128]{3,2,1,0:T(8,128)S(1)} %get-tuple-element.18.mid), channel_id=1, source_target_pairs={{0,1},{1,0},{2,3},{3,2},{4,5},{5,4},{6,7},{7,6},{8,9},{9,8},{10,11... | collective-permute-start | bytes 1966088 | tf_op jit(solution)/shard_map/ppermute | solution.py:440
  15.8 15.7 %all-to-all-start = ((f32[32,8,128]{2,1,0:T(8,128)}), f32[32,8,128]{2,1,0:T(8,128)S(1)}, u32[]{:S(2)}, u32[]{:S(2)}) async-start(f32[32,8,128]{2,1,0:T(8,128)} %shard_map.100), calls=%async_computation | async-start | bytes 262144 | tf_op jit(solution)/shard_map/all_to_all | solution.py:508
  21.7 8.7 %collective-permute-start.6 = (f32[5,3,16,128]{3,2,1,0:T(8,128)}, f32[5,3,16,128]{3,2,1,0:T(8,128)S(1)}, u32[]{:S(2)}, u32[]{:S(2)}) collective-permute-start(f32[5,3,16,128]{3,2,1,0:T(8,128)} %copy-done.11), channel_id=1, source_target_pairs={{0,4},{4,0},{8,12},{12,8},{16,20},{20,16},{24,28},{28,24},{1,5},{5... | collective-permute-start | bytes 368648 | tf_op jit(solution)/shard_map/ppermute | solution.py:426
  23.5 6.9 %collective-permute-start.7 = (f32[5,3,16,128]{3,2,1,0:T(8,128)S(1)}, f32[5,3,16,128]{3,2,1,0:T(8,128)S(1)}, u32[]{:S(2)}, u32[]{:S(2)}) collective-permute-start(f32[5,3,16,128]{3,2,1,0:T(8,128)S(1)} %get-tuple-element.20), channel_id=1, source_target_pairs={{0,1},{1,0},{4,8},{5,9},{8,4},{9,5},{12,16},{13,17},{16,12},{17,13... | collective-permute-start | bytes 368648 | tf_op jit(solution)/shard_map/ppermute | solution.py:435
  23.5 6.9 %collective-permute-start.8 = (f32[5,3,16,128]{3,2,1,0:T(8,128)S(1)}, f32[5,3,16,128]{3,2,1,0:T(8,128)S(1)}, u32[]{:S(2)}, u32[]{:S(2)}) collective-permute-start(f32[5,3,16,128]{3,2,1,0:T(8,128)S(1)} %get-tuple-element.21), channel_id=1, source_target_pairs={{0,2},{2,0},{1,3},{3,1},{4,6},{6,4},{5,7},{7,5},{8,10},{10,8},{9,1... | collective-permute-start | bytes 368648 | tf_op jit(solution)/shard_map/ppermute | solution.py:440
  27.0 4.5 %copy-start.9 = (f32[1,128,128]{2,1,0:T(8,128)S(1)}, f32[1,128,128]{2,1,0:T(8,128)}, u32[]{:S(2)}) copy-start(f32[1,128,128]{2,1,0:T(8,128)} %basis_ref.1) | copy-start | bytes 196612

commit v5 on v4

--- a/solution.py
+++ b/solution.py
@@ -30,6 +30,7 @@
 
 
 def tables(nx, ny, nz):
+    sides_y, sides_z = (2 if lax.axis_size(axis) == 2 else 3 for axis in ("ty", "tz"))
     y, z, layer, x = np.arange(ny), np.arange(nz), np.arange(HALO), np.eye(nx, dtype=np.float32)
     face = np.eye(FACE_PLANES, dtype=np.float32)
     band = weight_of(y[None, :] - y[:, None])
@@ -51,20 +52,20 @@
     parts = dict(
         ay=np.concatenate(np.split(np.kron(x, band), nx * ny // nz, axis=1)),
         bz=twice(along_z, 0),
-        wz=twice(z_halo, 1).reshape(-1, nz),
-        py=columns(twice(y_halo, 2)).reshape(-1, nz),
-        fy=columns(np.concatenate([twice(np.kron(face, band), 1)[None], twice(y_face, 2)])).reshape(-1, nz),
+        wz=twice(z_halo[:sides_z], 1).reshape(-1, nz),
+        fy=columns(np.concatenate([twice(np.kron(face, band), 1)[None], twice(y_face[:sides_y], 2)])).reshape(-1, nz),
     )
     places, at = {}, 0
     for name, m in parts.items():
         places[name], at = at, at + m.shape[0]
-    return jnp.asarray(np.concatenate(list(parts.values())), BF16), places
+    edge = columns(twice(y_halo[:sides_y], 2)).reshape(-1, nz)
+    return jnp.asarray(np.concatenate(list(parts.values())), BF16), jnp.asarray(edge, BF16), places
 
 
 class Bands:
     def __init__(self, ref, shape):
         self.ref, (self.nx, self.ny, self.nz) = ref, shape
-        self.places = tables(*shape)[1]
+        self.places = tables(*shape)[2]
 
     def block(self, name, rows, i=0, width=None):
         at = self.places[name]
@@ -80,9 +81,6 @@
 
     def from_z(self, side):
         return self.block("wz", 2 * self.nz, side)
-
-    def from_y(self, side):
-        return self.block("py", self.nx * EDGE, side, 2 * HALO * self.nx)
 
     def face_y(self, i):
         return self.block("fy", FACE_PLANES * self.ny, i, 2 * FACE_PLANES * self.ny)
@@ -229,14 +227,10 @@
     return total
 
 
-def own_rate(scale, x, v_ref, adj_ref, vel_ref, c_ref, sponge_ref, source_ref, gy, gz):
+def own_rate(scale, keep, x, v_ref, base, vel_ref, c_ref, sponge_ref, gy, gz):
     part = scale / 60.0
-    c, damp = c_ref[x] * part, sponge_ref[x] * scale
-    acc = []
-    for k in range(5):
-        cur = v_ref[k, x]
-        base = cur if adj_ref is None else 0.5 * (adj_ref[k, x] + cur)
-        acc.append(base + (scale * source_ref[k, x] - damp * cur))
+    c, held = c_ref[x] * part, keep - sponge_ref[x] * scale
+    acc = [base[k] + held * v_ref[k, x] for k in range(5)]
     gx = [x_difference(v_ref, k, x) for k in range(5)]
     for d, g in enumerate((gx, gy, gz)):
         acc = couple(acc, vel_ref[d, x] * part, c, d, g)
@@ -263,7 +257,7 @@
                 out_ref[k, x] = acc[k]
 
 
-def own_planes(scale, v_ref, adj_ref, vel_ref, c_ref, sponge_ref, source_ref, table_ref, z_blocks, out_ref, dy, dz):
+def own_planes(scale, keep, v_ref, base_of, vel_ref, c_ref, sponge_ref, table_ref, z_blocks, out_ref, dy, dz):
     nx, ny, nz = v_ref.shape[1:]
     bands = Bands(table_ref, v_ref.shape[1:])
     ay, bz = bands.along_y(), bands.along_z()
@@ -276,30 +270,38 @@
         dz[k] = along_z.reshape(nx, ny, nz)
     for x in range(nx):
         gy, gz = [dy[k, x] for k in range(5)], [dz[k, x] for k in range(5)]
-        acc = own_rate(scale, x, v_ref, adj_ref, vel_ref, c_ref, sponge_ref, source_ref, gy, gz)
+        base = [base_of(k, x) for k in range(5)]
+        acc = own_rate(scale, keep, x, v_ref, base, vel_ref, c_ref, sponge_ref, gy, gz)
         for k in range(5):
             out_ref[k, x] = acc[k]
 
 
 def first_kernel(adj, vel, c, sponge, source, table, _, *refs):
-    n_z, refs = len(sides_of("tz")), refs[1:]
-    z_blocks, (out_ref, dy, dz) = refs[:n_z], refs[n_z:]
-    own_planes(TIME_STEP, adj, None, vel, c, sponge, source, table, z_blocks, out_ref, dy, dz)
-
-
-def second_kernel(mid, adj, vel, c, sponge, source, table, *refs):
+    n_z, refs = len(sides_of("tz")), refs[2:]
+    z_blocks, (out_ref, base_ref, face_ref, dy, dz) = refs[:n_z], refs[n_z:]
+    face_ref[...] = sponge[:FACE_PLANES]
+
+    def base_of(k, x):
+        base_ref[k, x] = 0.5 * adj[k, x] + (0.5 * TIME_STEP) * source[k, x]
+        return TIME_STEP * source[k, x]
+
+    own_planes(TIME_STEP, 1.0, adj, base_of, vel, c, sponge, table, z_blocks, out_ref, dy, dz)
+
+
+def second_kernel(mid, base, vel, c, sponge, table, *refs):
     n_z = len(sides_of("tz"))
     z_blocks, (out_ref, dy, dz) = refs[:n_z], refs[n_z:]
-    own_planes(0.5 * TIME_STEP, mid, adj, vel, c, sponge, source, table, z_blocks, out_ref, dy, dz)
-
-
-def add_y_blocks(scale, out_ref, vel_ref, c_ref, y_blocks, table_ref):
+    base_of = lambda k, x: base[k, x]
+    own_planes(0.5 * TIME_STEP, 0.5, mid, base_of, vel, c, sponge, table, z_blocks, out_ref, dy, dz)
+
+
+def add_y_blocks(scale, out_ref, vel_ref, c_ref, y_blocks, edge_ref):
     nx, ny, nz = out_ref.shape[1:]
-    bands = Bands(table_ref, out_ref.shape[1:])
+    size = nx * EDGE
     part = scale / 60.0
     for ref, side in zip(y_blocks, sides_of("ty")):
         values = [stacked(ref[k].reshape(HALO * nx, nz), 0) for k in range(5)]
-        grads = dot(bands.from_y(side), jnp.concatenate(values, axis=1))
+        grads = dot(edge_ref[pl.ds(pl.multiple_of(side * size, 16), size), : 2 * HALO * nx], jnp.concatenate(values, axis=1))
         at = pl.multiple_of(jnp.where(side == ABOVE, ny - EDGE, 0), EDGE)
         for x in range(nx):
             rows = pl.ds(at, EDGE)
@@ -310,17 +312,17 @@
                 out_ref[k, x, rows, :] = acc[k]
 
 
-def mid_kernel(part_ref, vel, c, table, *refs):
+def mid_kernel(part_ref, vel, c, edge, *refs):
     n_y = len(sides_of("ty"))
     n_z = len(sides_of("tz"))
     x_blocks, y_blocks, (out_ref, *msgs) = refs[:2], refs[2 : 2 + n_y], refs[2 + n_y + n_z :]
     out_ref[...] = part_ref[...]
-    add_y_blocks(TIME_STEP, out_ref, vel, c, y_blocks, table)
+    add_y_blocks(TIME_STEP, out_ref, vel, c, y_blocks, edge)
     add_x_blocks(TIME_STEP, out_ref, vel, c, x_blocks)
     pack_second(out_ref, msgs[:2], msgs[2:])
 
 
-def sums_kernel(mid, adj, vel, c, sponge, source, table, owner_ref, *refs):
+def sums_kernel(mid, base, vel, c, sponge, table, owner_ref, *refs):
     n_y, n_z = len(sides_of("ty")), len(sides_of("tz"))
     x_blocks, y_blocks, auxes, sums_ref = refs[:2], refs[2 : 2 + n_y], refs[2 + n_y : 2 + n_y + n_z], refs[-1]
     nx, ny, nz = mid.shape[1:]
@@ -338,7 +340,9 @@
     gy = [g.reshape(FACE_PLANES, ny, nz) for g in along_y(0)]
     gz = [g.reshape(FACE_PLANES, ny, nz) for g in along_z(bands.along_z())]
     planes = [
-        own_rate(scale, p, mid, adj, vel, c, sponge, source, [g[p] for g in gy], [g[p] for g in gz])
+        own_rate(
+            scale, 0.5, p, mid, [base[k, p] for k in range(5)], vel, c, sponge, [g[p] for g in gy], [g[p] for g in gz]
+        )
         for p in range(FACE_PLANES)
     ]
     groups.append([jnp.concatenate([planes[p][k] for p in range(FACE_PLANES)], axis=0) for k in range(5)])
@@ -379,19 +383,17 @@
     sums = lax.dot_general(
         choose, jnp.concatenate(values, axis=1), (((0,), (0,)), ((), ())), preferred_element_type=F32
     )
-    sums_ref[:, 5:, :] = jnp.zeros((devices, sums_ref.shape[1] - 5, nz), F32)
-    for k in range(5):
-        sums_ref[:, k, :] = sums[:, k * nz : (k + 1) * nz]
-
-
-def final_kernel(part_ref, vel, c, table, *refs):
+    sums_ref[...] = sums.reshape(sums_ref.shape)
+
+
+def final_kernel(part_ref, vel, c, edge, *refs):
     n_y = len(sides_of("ty"))
     x_blocks, y_blocks, (out_ref, token, work, sems) = refs[:2], refs[2 : 2 + n_y], refs[2 + n_y :]
     nx = part_ref.shape[1]
     token[...] = jnp.zeros(token.shape, F32)
     scale = 0.5 * TIME_STEP
     work[...] = part_ref[...]
-    add_y_blocks(scale, work, vel, c, y_blocks, table)
+    add_y_blocks(scale, work, vel, c, y_blocks, edge)
     inner = pltpu.make_async_copy(work.at[:, HALO : nx - HALO], out_ref.at[:, HALO : nx - HALO], sems.at[0])
     inner.start()
     add_x_blocks(scale, work, vel, c, x_blocks)
@@ -410,7 +412,7 @@
     for i in range(1, sums_ref.shape[0]):
         total = total + sums_ref[i]
     modes = lax.dot_general(
-        total, basis_ref[0], (((1,), (0,)), ((), ())), precision=lax.Precision.HIGHEST, preferred_element_type=F32
+        jnp.concatenate(jnp.split(total, 5, axis=1), axis=0), basis_ref[0], (((1,), (0,)), ((), ())), precision=lax.Precision.HIGHEST, preferred_element_type=F32
     )
     mine = lax.axis_index("ty") * lax.axis_size("tz") + lax.axis_index("tz")
     width = modes.shape[1]
@@ -463,7 +465,7 @@
     nx, ny, nz = adjoint.shape[1:]
     n_ax, n_ty, n_tz = (lax.axis_size(a) for a in ("ax", "ty", "tz"))
     n_y = 1 if n_ty == 2 else 2
-    table, _ = tables(nx, ny, nz)
+    table, edge, _ = tables(nx, ny, nz)
     shape = lambda *s: jax.ShapeDtypeStruct(s, F32)
     brick = shape(5, nx, ny, nz)
     grads = [pltpu.VMEM((5, nx, ny, nz), F32)] * 2
@@ -484,13 +486,13 @@
     y_first = from_sides("ty", msgs[2], msgs[-1])
     x_first = swap_x(msgs[0], msgs[1])
     fields = [velocity, sound_speed, sponge, source, table]
-    (part,) = call(
-        first_kernel, [adjoint, *fields, token, owners, *z_blocks], [brick], grads, away={6: ANY}, flops=work, grant=8
+    part, base, face_sponge = call(
+        first_kernel, [adjoint, *fields, token, owners, edge, *z_blocks], [brick, brick, shape(FACE_PLANES, ny, nz)], grads, away={6: ANY}, flops=work, grant=8
     )
     vel, c = velocity, sound_speed
     mid, *msgs = call(
         mid_kernel,
-        [part, vel, c, table, *x_first, *y_first, *auxes],
+        [part, vel, c, edge, *x_first, *y_first, *auxes],
         [brick] + [shape(5, HALO, ny, nz)] * 2 + [shape(5, HALO, nx, nz)] * n_y,
         flops=work // 4,
         grant=8,
@@ -500,18 +502,18 @@
     x_blocks = swap_x(msgs[0], msgs[1])
     (sums,) = call(
         sums_kernel,
-        [mid, adjoint, vel, c, sponge, source, table, owners, *x_first, *y_first, *auxes],
-        [shape(devices, 8, nz)],
+        [mid, base, vel, c, face_sponge, table, owners, *x_first, *y_first, *auxes],
+        [shape(devices, 1, 5 * nz)],
         flops=work // 4,
         grant=8,
     )
     sums = lax.all_to_all(sums, ("ax", "ty", "tz"), split_axis=0, concat_axis=0, tiled=True)
     (part,) = call(
-        second_kernel, [mid, adjoint, *fields, *z_blocks], [brick], grads, flops=work, grant=8
+        second_kernel, [mid, base, vel, c, sponge, table, *z_blocks], [brick], grads, flops=work, grant=8
     )
     adjoint_out, token = call(
         final_kernel,
-        [part, vel, c, table, *x_blocks, *y_blocks],
+        [part, vel, c, edge, *x_blocks, *y_blocks],
         [brick, shape(8, nz)],
         [pltpu.VMEM((5, nx, ny, nz), F32), pltpu.SemaphoreType.DMA((3,))],
         out_away={0: HBM},

time: 32.7 us -> 32.4 us (level)
  local copies, waits for them, and re-layouts: 3.08 us -> 4.36 us
  Pallas kernels: 8.45 us -> 7.41 us
  waiting for transfers between devices: 5.71 us -> 5.24 us
    unnamed x26, local copies, waits for them, and re-layouts: 3.08 us -> 4.36 us
    pallas_call x7, Pallas kernels: 8.45 us -> 7.41 us  [call(): pl.pallas_call(kernel, out_shape=list(outs), in_specs=[away.get(i, VMEM)...]
    ppermute x2, waiting for transfers between devices: 5.69 us -> 5.22 us  [swap_x(): near = lax.ppermute(first, 'ax', [(i, i ^ 1) for i in range(count)])]
  transfers between devices with their start and end apart: 10 -> 10, of which waited for: 2 -> 2; matrix products, arithmetic and copies ran while one was open for 0% -> 0% of each run, Pallas kernels for 22% -> 19%
where the time goes in v5:
time: 32.4 us; the launch traced here: 32 us
  starting transfers between devices  14.2 us (44%)
  Pallas kernels  7.41 us (23%)
  waiting for transfers between devices  5.24 us (16%)
  local copies, waits for them, and re-layouts  4.36 us (13%)
  between operations  0.79 us (2%)
    pallas_call x7, Pallas kernels, call(): pl.pallas_call(kernel, out_shape=list(outs), in_specs=[away.get(i, VMEM)...  7.41 us
    all_to_all x1, starting transfers between devices, on_device(): lax.all_to_all(sums, ('ax', 'ty', 'tz'), split_axis=0, concat_axis=0, til...  5.75 us
    ppermute x2, waiting for transfers between devices, swap_x(): near = lax.ppermute(first, 'ax', [(i, i ^ 1) for i in range(count)])  5.22 us
    ppermute x2, starting transfers between devices, swap_x(): near = lax.ppermute(first, 'ax', [(i, i ^ 1) for i in range(count)])  4.79 us
    unnamed x26, local copies, waits for them, and re-layouts  4.36 us
    ppermute x5, starting transfers between devices, ring(): lax.ppermute(v, axis, [(i, (i + step) % count) for i in range(count)])  3.68 us
  transfers between devices with their start and end apart: 10, of which 2 were waited for; matrix products, arithmetic and copies ran while one was open for 0% of the time, Pallas kernels for 19%

profile of v5, /device:TPU:0, one launch (start us, length us, event | category | flops | bytes accessed | tf_op | source)
XLA Modules:
  0.0 32.0 jit_solution(4425110536747001111)
XLA Ops:
  0.6 0.0 copy-start.1
  0.6 0.5 %collective-permute-start = (f32[5,16,16,128]{3,2,1,0:T(8,128)}, f32[5,16,16,128]{3,2,1,0:T(8,128)S(1)}, u32[]{:S(2)}, u32[]{:S(2)}) collective-permute-start(f32[5,16,16,128]{3,2,1,0:T(8,128)} %adj.3), channel_id=1, source_target_pairs={{0,1},{1,0},{2,3},{3,2},{4,5},{5,4},{6,7},{7,6},{8,9},{9,8},{10,11... | collective-permute-start | bytes 1966088 | tf_op jit(solution)/shard_map/ppermute | solution.py:442
  1.2 0.0 copy-start
  1.2 0.0 copy-start.2
  1.2 2.1 %shard_map.104 = (f32[7,3,16,128]{3,2,1,0:T(8,128)}, f32[7,3,16,128]{3,2,1,0:T(8,128)}, f32[7,3,16,128]{3,2,1,0:T(8,128)}, f32[2,3,16,128]{3,2,1,0:T(8,128)}, f32[8,128]{1,0:T(8,128)}) custom-call(f32[5,16,16,128]{3,2,1,0:T(8,128)} %adj.3, f32[3,16,16,128]{3,2,1,0:T(8,128)} %vel.11, f32[16,16,128]{2,1,0:T(8,128)} %c.11, s32[1,32]{1,0:T(1,128)} %bitcast.2), custom_call_target="tpu_custom_call" | custom-call | flops 20000000 | bytes 17491200 | tf_op jit(solution)/shard_map/pallas_call | solution.py:453
  3.3 0.0 copy-start.10
  3.3 0.1 collective-permute-start.4
  3.4 3.0 %collective-permute-start.1 = (f32[7,3,16,128]{3,2,1,0:T(8,128)}, f32[7,3,16,128]{3,2,1,0:T(8,128)S(1)}, u32[]{:S(2)}, u32[]{:S(2)}) collective-permute-start(f32[7,3,16,128]{3,2,1,0:T(8,128)} %get-tuple-element.18), channel_id=1, source_target_pairs={{0,4},{4,0},{8,12},{12,8},{16,20},{20,16},{24,28},{28,24},{1,5},{5... | collective-permute-start | bytes 516104 | tf_op jit(solution)/shard_map/ppermute | solution.py:428
  6.4 0.0 collective-permute-start.2
  6.4 0.0 copy-start.6
  6.4 1.5 %collective-permute-start.3 = (f32[7,3,16,128]{3,2,1,0:T(8,128)}, f32[7,3,16,128]{3,2,1,0:T(8,128)S(1)}, u32[]{:S(2)}, u32[]{:S(2)}) collective-permute-start(f32[7,3,16,128]{3,2,1,0:T(8,128)} %get-tuple-element.20), channel_id=1, source_target_pairs={{0,2},{2,0},{1,3},{3,1},{4,6},{6,4},{5,7},{7,5},{8,10},{10,8},{9,1... | collective-permute-start | bytes 516104 | tf_op jit(solution)/shard_map/ppermute | solution.py:442
  7.9 0.0 collective-permute-done.refs_2_
  7.9 0.0 copy-done.1
  7.9 0.0 copy-done
  7.9 0.0 copy-done.2
  7.9 0.0 copy-done.10
  7.9 0.0 copy-done.6
  7.9 0.0 copy-start.3
  7.9 1.0 %copy-done.3 = bf16[1376,128]{1,0:T(8,128)(2,1)S(1)} copy-done((bf16[1376,128]{1,0:T(8,128)(2,1)S(1)}, bf16[1376,128]{1,0:T(8,128)(2,1)}, u32[]{:S(2)}) %copy-start.3) | copy-done | bytes 352280
  8.9 0.0 copy-start.7
  8.9 1.1 %copy-done.7 = f32[5,16,16,128]{3,2,1,0:T(8,128)S(1)} copy-done((f32[5,16,16,128]{3,2,1,0:T(8,128)S(1)}, f32[5,16,16,128]{3,2,1,0:T(8,128)}, u32[]{:S(2)}) %copy-start.7) | copy-done | bytes 655384
  10.0 0.0 copy-start.8
  10.0 0.9 %copy-done.8 = f32[16,16,128]{2,1,0:T(8,128)S(1)} copy-done((f32[16,16,128]{2,1,0:T(8,128)S(1)}, f32[16,16,128]{2,1,0:T(8,128)}, u32[]{:S(2)}) %copy-start.8) | copy-done | bytes 131096
  10.9 0.0 copy-start.11
  10.9 0.8 %copy-done.11 = bf16[256,128]{1,0:T(8,128)(2,1)S(1)} copy-done((bf16[256,128]{1,0:T(8,128)(2,1)S(1)}, bf16[256,128]{1,0:T(8,128)(2,1)}, u32[]{:S(2)}) %copy-start.11) | copy-done | bytes 65560
  11.7 1.0 %shard_map.105 = (f32[5,16,16,128]{3,2,1,0:T(8,128)S(1)}, f32[5,16,16,128]{3,2,1,0:T(8,128)S(1)}, f32[2,16,128]{2,1,0:T(8,128)S(1)}) custom-call(f32[5,16,16,128]{3,2,1,0:T(8,128)S(1)} %copy-done.1, f32[3,16,16,128]{3,2,1,0:T(8,128)S(1)} %copy-done, f32[16,16,128]{2,1,0:T(8,128)S(1)} %copy-done.2, f32[16,16,128]{2,1,0:T(8,128)S(1)} %copy-done.8, ...), custom_call_target="tpu_custom_call" | custom-call | flops 2621440000 | bytes 47883520 | tf_op jit(solution)/shard_map/pallas_call | solution.py:453
  12.8 0.0 collective-permute-done.4.refs_3_
  12.8 1.5 %collective-permute-done.1.refs_0_ = f32[7,3,16,128]{3,2,1,0:T(8,128)S(1)} collective-permute-done((f32[7,3,16,128]{3,2,1,0:T(8,128)}, f32[7,3,16,128]{3,2,1,0:T(8,128)S(1)}, u32[]{:S(2)}, u32[]{:S(2)}) %collective-permute-start.1) | collective-permute-done | bytes 172064 | tf_op jit(solution)/shard_map/ppermute | solution.py:428
  14.2 0.0 collective-permute-done.2.refs_1_
  14.3 0.0 collective-permute-done.3.refs_2_
  14.3 0.0 copy-start.4
  14.3 0.4 %shard_map.106 = (f32[5,16,16,128]{3,2,1,0:T(8,128)S(1)}, f32[5,3,16,128]{3,2,1,0:T(8,128)S(1)}, f32[5,3,16,128]{3,2,1,0:T(8,128)S(1)}, f32[5,3,16,128]{3,2,1,0:T(8,128)S(1)}) custom-call(f32[5,16,16,128]{3,2,1,0:T(8,128)S(1)} %get-tuple-element.17.part_ref, f32[3,16,16,128]{3,2,1,0:T(8,128)S(1)} %copy-done, f32[16,16,128]{2,1,0:T(8,128)S(1)} %copy-done.2, ...), custom_call_target="tpu_custom_call" | custom-call | flops 655360000 | bytes 28999680 | tf_op jit(solution)/shard_map/pallas_call | solution.py:453
  14.6 0.1 collective-permute-start.5
  14.7 0.5 %copy-done.4 = bf16[1376,128]{1,0:T(8,128)(2,1)S(1)} copy-done((bf16[1376,128]{1,0:T(8,128)(2,1)S(1)}, bf16[1376,128]{1,0:T(8,128)(2,1)}, u32[]{:S(2)}) %copy-start.4) | copy-done | bytes 352280
  15.2 1.0 %shard_map.109 = f32[32,1,640]{2,1,0:T(1,128)} custom-call(f32[5,16,16,128]{3,2,1,0:T(8,128)S(1)} %get-tuple-element.22.mid, f32[5,16,16,128]{3,2,1,0:T(8,128)S(1)} %get-tuple-element.23.base, f32[3,16,16,128]{3,2,1,0:T(8,128)S(1)} %copy-done, f32[16,16,128]{2,1,0:T(8,128)S(1)} %copy-done.2, f32[2,16,128]{2,1,0:T(8,128)S(1)} %get-tuple-element.28.sponge, ...), custom_call_target="tpu_custom_call" | custom-call | flops 655360000 | bytes 32032000 | tf_op jit(solution)/shard_map/pallas_call | solution.py:453
  16.3 0.0 copy-start.9
  16.3 5.7 %all-to-all-start = ((f32[32,1,640]{2,1,0:T(1,128)}), f32[32,1,640]{2,1,0:T(1,128)S(1)}, u32[]{:S(2)}, u32[]{:S(2)}) async-start(f32[32,1,640]{2,1,0:T(1,128)} %shard_map.109), calls=%async_computation | async-start | bytes 163840 | tf_op jit(solution)/shard_map/all_to_all | solution.py:510
  22.0 1.8 %collective-permute-start.6 = (f32[5,3,16,128]{3,2,1,0:T(8,128)S(1)}, f32[5,3,16,128]{3,2,1,0:T(8,128)S(1)}, u32[]{:S(2)}, u32[]{:S(2)}) collective-permute-start(f32[5,3,16,128]{3,2,1,0:T(8,128)S(1)} %get-tuple-element.24), channel_id=1, source_target_pairs={{0,4},{4,0},{8,12},{12,8},{16,20},{20,16},{24,28},{28,24},{1,5},{5... | collective-permute-start | bytes 368648 | tf_op jit(solution)/shard_map/ppermute | solution.py:428
  23.9 0.0 collective-permute-start.7
  23.9 0.0 copy-start.12
  23.9 1.5 %collective-permute-start.8 = (f32[5,3,16,128]{3,2,1,0:T(8,128)S(1)}, f32[5,3,16,128]{3,2,1,0:T(8,128)S(1)}, u32[]{:S(2)}, u32[]{:S(2)}) collective-permute-start(f32[5,3,16,128]{3,2,1,0:T(8,128)S(1)} %get-tuple-element.26), channel_id=1, source_target_pairs={{0,2},{2,0},{1,3},{3,1},{4,6},{6,4},{5,7},{7,5},{8,10},{10,8},{9,1... | collective-permute-start | bytes 368648 | tf_op jit(solution)/shard_map/ppermute | solution.py:442
  25.3 0.0 collective-permute-done.5.refs_0_
  25.3 0.0 copy-done.9
  25.3 0.9 %shard_map.107.part_ref = f32[5,16,16,128]{3,2,1,0:T(8,128)S(1)} custom-call(f32[5,16,16,128]{3,2,1,0:T(8,128)S(1)} %get-tuple-element.22.mid, f32[5,16,16,128]{3,2,1,0:T(8,128)S(1)} %get-tuple-element.23.base, f32[3,16,16,128]{3,2,1,0:T(8,128)S(1)} %copy-done, f32[16,16,128]{2,1,0:T(8,128)S(1)} %copy-done.2, f32[16,16,128]{2,1,0:T(8,128)S(1)} %copy-done.9, ...), custom_call_target="tpu_custom_call" | custom-call | flops 2621440000 | bytes 39813120 | tf_op jit(solution)/shard_map/pallas_call | solution.py:453
  26.3 0.0 copy-start.5
  26.3 3.8 %collective-permute-done.6.refs_0_ = f32[5,3,16,128]{3,2,1,0:T(8,128)S(1)} collective-permute-done((f32[5,3,16,128]{3,2,1,0:T(8,128)S(1)}, f32[5,3,16,128]{3,2,1,0:T(8,128)S(1)}, u32[]{:S(2)}, u32[]{:S(2)}) %collective-permute-start.6) | collective-permute-done | bytes 122912 | tf_op jit(solution)/shard_map/ppermute | solution.py:428
  30.0 0.0 collective-permute-done.7.refs_1_
  30.1 0.0 collective-permute-done.8.refs_2_
  30.1 0.0 copy-done.12
  30.1 1.1 %shard_map.108 = (f32[5,16,16,128]{3,2,1,0:T(8,128)}, f32[8,128]{1,0:T(8,128)S(1)}) custom-call(f32[5,16,16,128]{3,2,1,0:T(8,128)S(1)} %shard_map.107.part_ref, f32[3,16,16,128]{3,2,1,0:T(8,128)S(1)} %copy-done, f32[16,16,128]{2,1,0:T(8,128)S(1)} %copy-done.2, bf16[256,128]{1,0:T(8,128)(2,1)S(1)} %copy-done.12, ...), custom_call_target="tpu_custom_call" | custom-call | flops 655360000 | bytes 23388160 | tf_op jit(solution)/shard_map/pallas_call | solution.py:453
  31.2 0.0 all-to-all-done.sums_ref
  31.2 0.0 copy-done.5
  31.2 0.8 %shard_map.110 = f32[5,1,32]{2,1,0:T(1,128)} custom-call(f32[32,1,640]{2,1,0:T(1,128)S(1)} %all-to-all-done.sums_ref, f32[1,128,128]{2,1,0:T(8,128)S(1)} %copy-done.5, f32[8,128]{1,0:T(8,128)S(1)} %get-tuple-element.29._), custom_call_target="tpu_custom_call" | custom-call | bytes 1521920 | tf_op jit(solution)/shard_map/pallas_call | solution.py:453
Async XLA Ops:
  0.6 7.2 %copy-start.1 = (f32[5,16,16,128]{3,2,1,0:T(8,128)S(1)}, f32[5,16,16,128]{3,2,1,0:T(8,128)}, u32[]{:S(2)}) copy-start(f32[5,16,16,128]{3,2,1,0:T(8,128)} %adj.3) | copy-start | bytes 1966084
  0.6 7.2 %collective-permute-start = (f32[5,16,16,128]{3,2,1,0:T(8,128)}, f32[5,16,16,128]{3,2,1,0:T(8,128)S(1)}, u32[]{:S(2)}, u32[]{:S(2)}) collective-permute-start(f32[5,16,16,128]{3,2,1,0:T(8,128)} %adj.3), channel_id=1, source_target_pairs={{0,1},{1,0},{2,3},{3,2},{4,5},{5,4},{6,7},{7,6},{8,9},{9,8},{10,11... | collective-permute-start | bytes 1966088 | tf_op jit(solution)/shard_map/ppermute | solution.py:442
  1.2 6.7 %copy-start = (f32[3,16,16,128]{3,2,1,0:T(8,128)S(1)}, f32[3,16,16,128]{3,2,1,0:T(8,128)}, u32[]{:S(2)}) copy-start(f32[3,16,16,128]{3,2,1,0:T(8,128)} %vel.11) | copy-start | bytes 1179652
  1.2 6.7 %copy-start.2 = (f32[16,16,128]{2,1,0:T(8,128)S(1)}, f32[16,16,128]{2,1,0:T(8,128)}, u32[]{:S(2)}) copy-start(f32[16,16,128]{2,1,0:T(8,128)} %c.11) | copy-start | bytes 393220
  3.3 4.6 %copy-start.10 = (f32[8,128]{1,0:T(8,128)S(1)}, f32[8,128]{1,0:T(8,128)}, u32[]{:S(2)}) copy-start(f32[8,128]{1,0:T(8,128)} %get-tuple-element.16._) | copy-start | bytes 12292
  3.3 9.5 %collective-permute-start.4 = (f32[2,3,16,128]{3,2,1,0:T(8,128)}, f32[2,3,16,128]{3,2,1,0:T(8,128)S(1)}, u32[]{:S(2)}, u32[]{:S(2)}) collective-permute-start(f32[2,3,16,128]{3,2,1,0:T(8,128)} %get-tuple-element.21), channel_id=1, source_target_pairs={{0,1},{1,0},{2,3},{3,2},{4,5},{5,4},{6,7},{7,6},{8,9},{9,8},{10,11... | collective-permute-start | bytes 147464 | tf_op jit(solution)/shard_map/ppermute | solution.py:442
  3.4 10.8 %collective-permute-start.1 = (f32[7,3,16,128]{3,2,1,0:T(8,128)}, f32[7,3,16,128]{3,2,1,0:T(8,128)S(1)}, u32[]{:S(2)}, u32[]{:S(2)}) collective-permute-start(f32[7,3,16,128]{3,2,1,0:T(8,128)} %get-tuple-element.18), channel_id=1, source_target_pairs={{0,4},{4,0},{8,12},{12,8},{16,20},{20,16},{24,28},{28,24},{1,5},{5... | collective-permute-start | bytes 516104 | tf_op jit(solution)/shard_map/ppermute | solution.py:428
  6.4 7.9 %collective-permute-start.2 = (f32[7,3,16,128]{3,2,1,0:T(8,128)}, f32[7,3,16,128]{3,2,1,0:T(8,128)S(1)}, u32[]{:S(2)}, u32[]{:S(2)}) collective-permute-start(f32[7,3,16,128]{3,2,1,0:T(8,128)} %get-tuple-element.19), channel_id=1, source_target_pairs={{0,1},{1,0},{4,8},{5,9},{8,4},{9,5},{12,16},{13,17},{16,12},{17,13... | collective-permute-start | bytes 516104 | tf_op jit(solution)/shard_map/ppermute | solution.py:437
  6.4 1.5 %copy-start.6 = (s32[1,1,1,32,1]{3,4,2,1,0:T(1,128)S(1)}, s32[1,1,1,32,1]{3,4,2,1,0:T(1,128)}, u32[]{:S(2)}) copy-start(s32[1,1,1,32,1]{3,4,2,1,0:T(1,128)} %param.15) | copy-start | bytes 388
  6.4 7.9 %collective-permute-start.3 = (f32[7,3,16,128]{3,2,1,0:T(8,128)}, f32[7,3,16,128]{3,2,1,0:T(8,128)S(1)}, u32[]{:S(2)}, u32[]{:S(2)}) collective-permute-start(f32[7,3,16,128]{3,2,1,0:T(8,128)} %get-tuple-element.20), channel_id=1, source_target_pairs={{0,2},{2,0},{1,3},{3,1},{4,6},{6,4},{5,7},{7,5},{8,10},{10,8},{9,1... | collective-permute-start | bytes 516104 | tf_op jit(solution)/shard_map/ppermute | solution.py:442
  7.9 1.0 %copy-start.3 = (bf16[1376,128]{1,0:T(8,128)(2,1)S(1)}, bf16[1376,128]{1,0:T(8,128)(2,1)}, u32[]{:S(2)}) copy-start(bf16[1376,128]{1,0:T(8,128)(2,1)} %constant.4.clone.table) | copy-start | bytes 1056772
  8.9 1.1 %copy-start.7 = (f32[5,16,16,128]{3,2,1,0:T(8,128)S(1)}, f32[5,16,16,128]{3,2,1,0:T(8,128)}, u32[]{:S(2)}) copy-start(f32[5,16,16,128]{3,2,1,0:T(8,128)} %source.1) | copy-start | bytes 1966084
  10.0 0.9 %copy-start.8 = (f32[16,16,128]{2,1,0:T(8,128)S(1)}, f32[16,16,128]{2,1,0:T(8,128)}, u32[]{:S(2)}) copy-start(f32[16,16,128]{2,1,0:T(8,128)} %sponge.3) | copy-start | bytes 393220
  10.9 0.8 %copy-start.11 = (bf16[256,128]{1,0:T(8,128)(2,1)S(1)}, bf16[256,128]{1,0:T(8,128)(2,1)}, u32[]{:S(2)}) copy-start(bf16[256,128]{1,0:T(8,128)(2,1)} %constant.5.clone.refs_1_.edge) | copy-start | bytes 196612
  14.3 1.0 %copy-start.4 = (bf16[1376,128]{1,0:T(8,128)(2,1)S(1)}, bf16[1376,128]{1,0:T(8,128)(2,1)}, u32[]{:S(2)}) copy-start(bf16[1376,128]{1,0:T(8,128)(2,1)} %constant.4.clone.table) | copy-start | bytes 1056772
  14.6 10.7 %collective-permute-start.5 = (f32[5,16,16,128]{3,2,1,0:T(8,128)S(1)}, f32[5,16,16,128]{3,2,1,0:T(8,128)S(1)}, u32[]{:S(2)}, u32[]{:S(2)}) collective-permute-start(f32[5,16,16,128]{3,2,1,0:T(8,128)S(1)} %get-tuple-element.22.mid), channel_id=1, source_target_pairs={{0,1},{1,0},{2,3},{3,2},{4,5},{5,4},{6,7},{7,6},{8,9},{9,8},{10,11... | collective-permute-start | bytes 1966088 | tf_op jit(solution)/shard_map/ppermute | solution.py:442
  16.3 9.1 %copy-start.9 = (f32[16,16,128]{2,1,0:T(8,128)S(1)}, f32[16,16,128]{2,1,0:T(8,128)}, u32[]{:S(2)}) copy-start(f32[16,16,128]{2,1,0:T(8,128)} %sponge.3) | copy-start | bytes 393220
  16.3 14.9 %all-to-all-start = ((f32[32,1,640]{2,1,0:T(1,128)}), f32[32,1,640]{2,1,0:T(1,128)S(1)}, u32[]{:S(2)}, u32[]{:S(2)}) async-start(f32[32,1,640]{2,1,0:T(1,128)} %shard_map.109), calls=%async_computation | async-start | bytes 163840 | tf_op jit(solution)/shard_map/all_to_all | solution.py:510
  22.0 8.0 %collective-permute-start.6 = (f32[5,3,16,128]{3,2,1,0:T(8,128)S(1)}, f32[5,3,16,128]{3,2,1,0:T(8,128)S(1)}, u32[]{:S(2)}, u32[]{:S(2)}) collective-permute-start(f32[5,3,16,128]{3,2,1,0:T(8,128)S(1)} %get-tuple-element.24), channel_id=1, source_target_pairs={{0,4},{4,0},{8,12},{12,8},{16,20},{20,16},{24,28},{28,24},{1,5},{5... | collective-permute-start | bytes 368648 | tf_op jit(solution)/shard_map/ppermute | solution.py:428
  23.9 6.2 %collective-permute-start.7 = (f32[5,3,16,128]{3,2,1,0:T(8,128)S(1)}, f32[5,3,16,128]{3,2,1,0:T(8,128)S(1)}, u32[]{:S(2)}, u32[]{:S(2)}) collective-permute-start(f32[5,3,16,128]{3,2,1,0:T(8,128)S(1)} %get-tuple-element.25), channel_id=1, source_target_pairs={{0,1},{1,0},{4,8},{5,9},{8,4},{9,5},{12,16},{13,17},{16,12},{17,13... | collective-permute-start | bytes 368648 | tf_op jit(solution)/shard_map/ppermute | solution.py:437
  23.9 6.2 %copy-start.12 = (bf16[256,128]{1,0:T(8,128)(2,1)S(1)}, bf16[256,128]{1,0:T(8,128)(2,1)}, u32[]{:S(2)}) copy-start(bf16[256,128]{1,0:T(8,128)(2,1)} %constant.5.clone.refs_1_.edge) | copy-start | bytes 196612
  23.9 6.2 %collective-permute-start.8 = (f32[5,3,16,128]{3,2,1,0:T(8,128)S(1)}, f32[5,3,16,128]{3,2,1,0:T(8,128)S(1)}, u32[]{:S(2)}, u32[]{:S(2)}) collective-permute-start(f32[5,3,16,128]{3,2,1,0:T(8,128)S(1)} %get-tuple-element.26), channel_id=1, source_target_pairs={{0,2},{2,0},{1,3},{3,1},{4,6},{6,4},{5,7},{7,5},{8,10},{10,8},{9,1... | collective-permute-start | bytes 368648 | tf_op jit(solution)/shard_map/ppermute | solution.py:442
  26.3 4.9 %copy-start.5 = (f32[1,128,128]{2,1,0:T(8,128)S(1)}, f32[1,128,128]{2,1,0:T(8,128)}, u32[]{:S(2)}) copy-start(f32[1,128,128]{2,1,0:T(8,128)} %basis_ref.1) | copy-start | bytes 196612

commit v6 on v5

--- a/solution.py
+++ b/solution.py
@@ -63,12 +63,12 @@
 
 
 class Bands:
-    def __init__(self, ref, shape):
-        self.ref, (self.nx, self.ny, self.nz) = ref, shape
+    def __init__(self, ref, shape, skipped=0):
+        self.ref, self.skipped, (self.nx, self.ny, self.nz) = ref, skipped, shape
         self.places = tables(*shape)[2]
 
     def block(self, name, rows, i=0, width=None):
-        at = self.places[name]
+        at = self.places[name] - self.skipped
         start = at + i * rows if isinstance(i, int) else pl.multiple_of(at + i * rows, 16)
         return self.ref[pl.ds(start, rows), : self.nz if width is None else width]
 
@@ -278,8 +278,9 @@
 
 def first_kernel(adj, vel, c, sponge, source, table, _, *refs):
     n_z, refs = len(sides_of("tz")), refs[2:]
-    z_blocks, (out_ref, base_ref, face_ref, dy, dz) = refs[:n_z], refs[n_z:]
+    z_blocks, (out_ref, base_ref, face_ref, bands_ref, dy, dz) = refs[:n_z], refs[n_z:]
     face_ref[...] = sponge[:FACE_PLANES]
+    bands_ref[...] = table[table.shape[0] - bands_ref.shape[0] :]
 
     def base_of(k, x):
         base_ref[k, x] = 0.5 * adj[k, x] + (0.5 * TIME_STEP) * source[k, x]
@@ -327,7 +328,7 @@
     x_blocks, y_blocks, auxes, sums_ref = refs[:2], refs[2 : 2 + n_y], refs[2 + n_y : 2 + n_y + n_z], refs[-1]
     nx, ny, nz = mid.shape[1:]
     rows = FACE_PLANES * ny
-    bands = Bands(table, mid.shape[1:])
+    bands = Bands(table, mid.shape[1:], tables(*mid.shape[1:])[2]["bz"])
     scale = 0.5 * TIME_STEP
     part = scale / 60.0
     flat = lambda v: v.reshape(rows, nz)
@@ -465,7 +466,7 @@
     nx, ny, nz = adjoint.shape[1:]
     n_ax, n_ty, n_tz = (lax.axis_size(a) for a in ("ax", "ty", "tz"))
     n_y = 1 if n_ty == 2 else 2
-    table, edge, _ = tables(nx, ny, nz)
+    table, edge, places = tables(nx, ny, nz)
     shape = lambda *s: jax.ShapeDtypeStruct(s, F32)
     brick = shape(5, nx, ny, nz)
     grads = [pltpu.VMEM((5, nx, ny, nz), F32)] * 2
@@ -486,8 +487,8 @@
     y_first = from_sides("ty", msgs[2], msgs[-1])
     x_first = swap_x(msgs[0], msgs[1])
     fields = [velocity, sound_speed, sponge, source, table]
-    part, base, face_sponge = call(
-        first_kernel, [adjoint, *fields, token, owners, edge, *z_blocks], [brick, brick, shape(FACE_PLANES, ny, nz)], grads, away={6: ANY}, flops=work, grant=8
+    part, base, face_sponge, face_table = call(
+        first_kernel, [adjoint, *fields, token, owners, edge, *z_blocks], [brick, brick, shape(FACE_PLANES, ny, nz), jax.ShapeDtypeStruct((table.shape[0] - places["bz"], nz), BF16)], grads, away={6: ANY}, flops=work, grant=8
     )
     vel, c = velocity, sound_speed
     mid, *msgs = call(
@@ -502,7 +503,7 @@
     x_blocks = swap_x(msgs[0], msgs[1])
     (sums,) = call(
         sums_kernel,
-        [mid, base, vel, c, face_sponge, table, owners, *x_first, *y_first, *auxes],
+        [mid, base, vel, c, face_sponge, face_table, owners, *x_first, *y_first, *auxes],
         [shape(devices, 1, 5 * nz)],
         flops=work // 4,
         grant=8,

time: 32.4 us -> 31.9 us (0.985)
  local copies, waits for them, and re-layouts: 4.36 us -> 3.85 us
    unnamed x26, local copies, waits for them, and re-layouts: 4.36 us -> 3.85 us
  transfers between devices with their start and end apart: 10 -> 10, of which waited for: 2 -> 2; matrix products, arithmetic and copies ran while one was open for 0% -> 0% of each run, Pallas kernels for 19% -> 20%
where the time goes in v6:
time: 31.9 us; the launch traced here: 31.6 us
  starting transfers between devices  14.3 us (45%)
  Pallas kernels  7.41 us (23%)
  waiting for transfers between devices  5.24 us (16%)
  local copies, waits for them, and re-layouts  3.85 us (12%)
  between operations  0.8 us (3%)
    pallas_call x7, Pallas kernels, call(): pl.pallas_call(kernel, out_shape=list(outs), in_specs=[away.get(i, VMEM)...  7.41 us
    all_to_all x1, starting transfers between devices, on_device(): lax.all_to_all(sums, ('ax', 'ty', 'tz'), split_axis=0, concat_axis=0, til...  5.83 us
    ppermute x2, waiting for transfers between devices, swap_x(): near = lax.ppermute(first, 'ax', [(i, i ^ 1) for i in range(count)])  5.22 us
    ppermute x2, starting transfers between devices, swap_x(): near = lax.ppermute(first, 'ax', [(i, i ^ 1) for i in range(count)])  4.79 us
    unnamed x26, local copies, waits for them, and re-layouts  3.85 us
    ppermute x5, starting transfers between devices, ring(): lax.ppermute(v, axis, [(i, (i + step) % count) for i in range(count)])  3.68 us
  transfers between devices with their start and end apart: 10, of which 2 were waited for; matrix products, arithmetic and copies ran while one was open for 0% of the time, Pallas kernels for 20%

profile of v6, /device:TPU:0, one launch (start us, length us, event | category | flops | bytes accessed | tf_op | source)
XLA Modules:
  0.0 31.6 jit_solution(13007159800639668227)
XLA Ops:
  0.6 0.0 copy-start.1
  0.6 0.5 %collective-permute-start = (f32[5,16,16,128]{3,2,1,0:T(8,128)}, f32[5,16,16,128]{3,2,1,0:T(8,128)S(1)}, u32[]{:S(2)}, u32[]{:S(2)}) collective-permute-start(f32[5,16,16,128]{3,2,1,0:T(8,128)} %adj.3), channel_id=1, source_target_pairs={{0,1},{1,0},{2,3},{3,2},{4,5},{5,4},{6,7},{7,6},{8,9},{9,8},{10,11... | collective-permute-start | bytes 1966088 | tf_op jit(solution)/shard_map/ppermute | solution.py:443
  1.2 0.0 copy-start
  1.2 0.0 copy-start.2
  1.2 2.1 %shard_map.104 = (f32[7,3,16,128]{3,2,1,0:T(8,128)}, f32[7,3,16,128]{3,2,1,0:T(8,128)}, f32[7,3,16,128]{3,2,1,0:T(8,128)}, f32[2,3,16,128]{3,2,1,0:T(8,128)}, f32[8,128]{1,0:T(8,128)}) custom-call(f32[5,16,16,128]{3,2,1,0:T(8,128)} %adj.3, f32[3,16,16,128]{3,2,1,0:T(8,128)} %vel.11, f32[16,16,128]{2,1,0:T(8,128)} %c.11, s32[1,32]{1,0:T(1,128)} %bitcast.2), custom_call_target="tpu_custom_call" | custom-call | flops 20000000 | bytes 17491200 | tf_op jit(solution)/shard_map/pallas_call | solution.py:454
  3.3 0.0 copy-start.8
  3.3 0.1 collective-permute-start.4
  3.4 3.0 %collective-permute-start.1 = (f32[7,3,16,128]{3,2,1,0:T(8,128)}, f32[7,3,16,128]{3,2,1,0:T(8,128)S(1)}, u32[]{:S(2)}, u32[]{:S(2)}) collective-permute-start(f32[7,3,16,128]{3,2,1,0:T(8,128)} %get-tuple-element.19), channel_id=1, source_target_pairs={{0,4},{4,0},{8,12},{12,8},{16,20},{20,16},{24,28},{28,24},{1,5},{5... | collective-permute-start | bytes 516104 | tf_op jit(solution)/shard_map/ppermute | solution.py:429
  6.4 0.0 collective-permute-start.2
  6.4 0.0 copy-start.4
  6.4 1.5 %collective-permute-start.3 = (f32[7,3,16,128]{3,2,1,0:T(8,128)}, f32[7,3,16,128]{3,2,1,0:T(8,128)S(1)}, u32[]{:S(2)}, u32[]{:S(2)}) collective-permute-start(f32[7,3,16,128]{3,2,1,0:T(8,128)} %get-tuple-element.21), channel_id=1, source_target_pairs={{0,2},{2,0},{1,3},{3,1},{4,6},{6,4},{5,7},{7,5},{8,10},{10,8},{9,1... | collective-permute-start | bytes 516104 | tf_op jit(solution)/shard_map/ppermute | solution.py:443
  7.9 0.0 collective-permute-done.refs_2_
  7.9 0.0 copy-done.1
  7.9 0.0 copy-done
  7.9 0.0 copy-done.2
  7.9 0.0 copy-done.8
  7.9 0.0 copy-done.4
  7.9 0.0 copy-start.5
  7.9 1.1 %copy-done.5 = f32[5,16,16,128]{3,2,1,0:T(8,128)S(1)} copy-done((f32[5,16,16,128]{3,2,1,0:T(8,128)S(1)}, f32[5,16,16,128]{3,2,1,0:T(8,128)}, u32[]{:S(2)}) %copy-start.5) | copy-done | bytes 655384
  9.0 0.0 copy-start.6
  9.0 0.9 %copy-done.6 = f32[16,16,128]{2,1,0:T(8,128)S(1)} copy-done((f32[16,16,128]{2,1,0:T(8,128)S(1)}, f32[16,16,128]{2,1,0:T(8,128)}, u32[]{:S(2)}) %copy-start.6) | copy-done | bytes 131096
  9.9 0.0 copy-start.9
  9.9 1.0 %copy-done.9 = bf16[1376,128]{1,0:T(8,128)(2,1)S(1)} copy-done((bf16[1376,128]{1,0:T(8,128)(2,1)S(1)}, bf16[1376,128]{1,0:T(8,128)(2,1)}, u32[]{:S(2)}) %copy-start.9) | copy-done | bytes 352280
  10.9 0.0 copy-start.11
  10.9 0.8 %copy-done.11 = bf16[256,128]{1,0:T(8,128)(2,1)S(1)} copy-done((bf16[256,128]{1,0:T(8,128)(2,1)S(1)}, bf16[256,128]{1,0:T(8,128)(2,1)}, u32[]{:S(2)}) %copy-start.11) | copy-done | bytes 65560
  11.7 1.0 %shard_map.105 = (f32[5,16,16,128]{3,2,1,0:T(8,128)S(1)}, f32[5,16,16,128]{3,2,1,0:T(8,128)S(1)}, f32[2,16,128]{2,1,0:T(8,128)S(1)}, bf16[864,128]{1,0:T(8,128)(2,1)S(1)}) custom-call(f32[5,16,16,128]{3,2,1,0:T(8,128)S(1)} %copy-done.1, f32[3,16,16,128]{3,2,1,0:T(8,128)S(1)} %copy-done, f32[16,16,128]{2,1,0:T(8,128)S(1)} %copy-done.2, ...), custom_call_target="tpu_custom_call" | custom-call | flops 2621440000 | bytes 52307200 | tf_op jit(solution)/shard_map/pallas_call | solution.py:454
  12.8 0.0 collective-permute-done.4.refs_3_
  12.8 1.5 %collective-permute-done.1.refs_0_ = f32[7,3,16,128]{3,2,1,0:T(8,128)S(1)} collective-permute-done((f32[7,3,16,128]{3,2,1,0:T(8,128)}, f32[7,3,16,128]{3,2,1,0:T(8,128)S(1)}, u32[]{:S(2)}, u32[]{:S(2)}) %collective-permute-start.1) | collective-permute-done | bytes 172064 | tf_op jit(solution)/shard_map/ppermute | solution.py:429
  14.2 0.0 collective-permute-done.2.refs_1_
  14.3 0.0 collective-permute-done.3.refs_2_
  14.3 0.4 %shard_map.106 = (f32[5,16,16,128]{3,2,1,0:T(8,128)S(1)}, f32[5,3,16,128]{3,2,1,0:T(8,128)S(1)}, f32[5,3,16,128]{3,2,1,0:T(8,128)S(1)}, f32[5,3,16,128]{3,2,1,0:T(8,128)S(1)}) custom-call(f32[5,16,16,128]{3,2,1,0:T(8,128)S(1)} %get-tuple-element.18.part_ref, f32[3,16,16,128]{3,2,1,0:T(8,128)S(1)} %copy-done, f32[16,16,128]{2,1,0:T(8,128)S(1)} %copy-done.2, ...), custom_call_target="tpu_custom_call" | custom-call | flops 655360000 | bytes 28999680 | tf_op jit(solution)/shard_map/pallas_call | solution.py:454
  14.6 0.1 collective-permute-start.5
  14.7 0.0 copy-start.10
  14.7 1.0 %shard_map.109 = f32[32,1,640]{2,1,0:T(1,128)} custom-call(f32[5,16,16,128]{3,2,1,0:T(8,128)S(1)} %get-tuple-element.23.mid, f32[5,16,16,128]{3,2,1,0:T(8,128)S(1)} %get-tuple-element.24.base, f32[3,16,16,128]{3,2,1,0:T(8,128)S(1)} %copy-done, f32[16,16,128]{2,1,0:T(8,128)S(1)} %copy-done.2, f32[2,16,128]{2,1,0:T(8,128)S(1)} %get-tuple-element.29.sponge, ...), custom_call_target="tpu_custom_call" | custom-call | flops 655360000 | bytes 29410560 | tf_op jit(solution)/shard_map/pallas_call | solution.py:454
  15.8 0.0 copy-start.7
  15.8 5.8 %all-to-all-start = ((f32[32,1,640]{2,1,0:T(1,128)}), f32[32,1,640]{2,1,0:T(1,128)S(1)}, u32[]{:S(2)}, u32[]{:S(2)}) async-start(f32[32,1,640]{2,1,0:T(1,128)} %shard_map.109), calls=%async_computation | async-start | bytes 163840 | tf_op jit(solution)/shard_map/all_to_all | solution.py:511
  21.6 1.8 %collective-permute-start.6 = (f32[5,3,16,128]{3,2,1,0:T(8,128)S(1)}, f32[5,3,16,128]{3,2,1,0:T(8,128)S(1)}, u32[]{:S(2)}, u32[]{:S(2)}) collective-permute-start(f32[5,3,16,128]{3,2,1,0:T(8,128)S(1)} %get-tuple-element.25), channel_id=1, source_target_pairs={{0,4},{4,0},{8,12},{12,8},{16,20},{20,16},{24,28},{28,24},{1,5},{5... | collective-permute-start | bytes 368648 | tf_op jit(solution)/shard_map/ppermute | solution.py:429
  23.4 0.0 collective-permute-start.7
  23.4 0.0 copy-start.12
  23.4 1.5 %collective-permute-start.8 = (f32[5,3,16,128]{3,2,1,0:T(8,128)S(1)}, f32[5,3,16,128]{3,2,1,0:T(8,128)S(1)}, u32[]{:S(2)}, u32[]{:S(2)}) collective-permute-start(f32[5,3,16,128]{3,2,1,0:T(8,128)S(1)} %get-tuple-element.27), channel_id=1, source_target_pairs={{0,2},{2,0},{1,3},{3,1},{4,6},{6,4},{5,7},{7,5},{8,10},{10,8},{9,1... | collective-permute-start | bytes 368648 | tf_op jit(solution)/shard_map/ppermute | solution.py:443
  24.9 0.0 collective-permute-done.5.refs_0_
  24.9 0.0 copy-done.10
  24.9 0.0 copy-done.7
  24.9 0.9 %shard_map.107.part_ref = f32[5,16,16,128]{3,2,1,0:T(8,128)S(1)} custom-call(f32[5,16,16,128]{3,2,1,0:T(8,128)S(1)} %get-tuple-element.23.mid, f32[5,16,16,128]{3,2,1,0:T(8,128)S(1)} %get-tuple-element.24.base, f32[3,16,16,128]{3,2,1,0:T(8,128)S(1)} %copy-done, f32[16,16,128]{2,1,0:T(8,128)S(1)} %copy-done.2, f32[16,16,128]{2,1,0:T(8,128)S(1)} %copy-done.7, ...), custom_call_target="tpu_custom_call" | custom-call | flops 2621440000 | bytes 39813120 | tf_op jit(solution)/shard_map/pallas_call | solution.py:454
  25.9 0.0 copy-start.3
  25.9 3.8 %collective-permute-done.6.refs_0_ = f32[5,3,16,128]{3,2,1,0:T(8,128)S(1)} collective-permute-done((f32[5,3,16,128]{3,2,1,0:T(8,128)S(1)}, f32[5,3,16,128]{3,2,1,0:T(8,128)S(1)}, u32[]{:S(2)}, u32[]{:S(2)}) %collective-permute-start.6) | collective-permute-done | bytes 122912 | tf_op jit(solution)/shard_map/ppermute | solution.py:429
  29.6 0.0 collective-permute-done.7.refs_1_
  29.6 0.0 collective-permute-done.8.refs_2_
  29.6 0.0 copy-done.12
  29.6 1.1 %shard_map.108 = (f32[5,16,16,128]{3,2,1,0:T(8,128)}, f32[8,128]{1,0:T(8,128)S(1)}) custom-call(f32[5,16,16,128]{3,2,1,0:T(8,128)S(1)} %shard_map.107.part_ref, f32[3,16,16,128]{3,2,1,0:T(8,128)S(1)} %copy-done, f32[16,16,128]{2,1,0:T(8,128)S(1)} %copy-done.2, bf16[256,128]{1,0:T(8,128)(2,1)S(1)} %copy-done.12, ...), custom_call_target="tpu_custom_call" | custom-call | flops 655360000 | bytes 23388160 | tf_op jit(solution)/shard_map/pallas_call | solution.py:454
  30.7 0.0 all-to-all-done.sums_ref
  30.7 0.0 copy-done.3
  30.8 0.8 %shard_map.110 = f32[5,1,32]{2,1,0:T(1,128)} custom-call(f32[32,1,640]{2,1,0:T(1,128)S(1)} %all-to-all-done.sums_ref, f32[1,128,128]{2,1,0:T(8,128)S(1)} %copy-done.3, f32[8,128]{1,0:T(8,128)S(1)} %get-tuple-element.31._), custom_call_target="tpu_custom_call" | custom-call | bytes 1521920 | tf_op jit(solution)/shard_map/pallas_call | solution.py:454
Async XLA Ops:
  0.6 7.2 %copy-start.1 = (f32[5,16,16,128]{3,2,1,0:T(8,128)S(1)}, f32[5,16,16,128]{3,2,1,0:T(8,128)}, u32[]{:S(2)}) copy-start(f32[5,16,16,128]{3,2,1,0:T(8,128)} %adj.3) | copy-start | bytes 1966084
  0.6 7.2 %collective-permute-start = (f32[5,16,16,128]{3,2,1,0:T(8,128)}, f32[5,16,16,128]{3,2,1,0:T(8,128)S(1)}, u32[]{:S(2)}, u32[]{:S(2)}) collective-permute-start(f32[5,16,16,128]{3,2,1,0:T(8,128)} %adj.3), channel_id=1, source_target_pairs={{0,1},{1,0},{2,3},{3,2},{4,5},{5,4},{6,7},{7,6},{8,9},{9,8},{10,11... | collective-permute-start | bytes 1966088 | tf_op jit(solution)/shard_map/ppermute | solution.py:443
  1.2 6.7 %copy-start = (f32[3,16,16,128]{3,2,1,0:T(8,128)S(1)}, f32[3,16,16,128]{3,2,1,0:T(8,128)}, u32[]{:S(2)}) copy-start(f32[3,16,16,128]{3,2,1,0:T(8,128)} %vel.11) | copy-start | bytes 1179652
  1.2 6.7 %copy-start.2 = (f32[16,16,128]{2,1,0:T(8,128)S(1)}, f32[16,16,128]{2,1,0:T(8,128)}, u32[]{:S(2)}) copy-start(f32[16,16,128]{2,1,0:T(8,128)} %c.11) | copy-start | bytes 393220
  3.3 4.6 %copy-start.8 = (f32[8,128]{1,0:T(8,128)S(1)}, f32[8,128]{1,0:T(8,128)}, u32[]{:S(2)}) copy-start(f32[8,128]{1,0:T(8,128)} %get-tuple-element.17._) | copy-start | bytes 12292
  3.3 9.5 %collective-permute-start.4 = (f32[2,3,16,128]{3,2,1,0:T(8,128)}, f32[2,3,16,128]{3,2,1,0:T(8,128)S(1)}, u32[]{:S(2)}, u32[]{:S(2)}) collective-permute-start(f32[2,3,16,128]{3,2,1,0:T(8,128)} %get-tuple-element.22), channel_id=1, source_target_pairs={{0,1},{1,0},{2,3},{3,2},{4,5},{5,4},{6,7},{7,6},{8,9},{9,8},{10,11... | collective-permute-start | bytes 147464 | tf_op jit(solution)/shard_map/ppermute | solution.py:443
  3.4 10.8 %collective-permute-start.1 = (f32[7,3,16,128]{3,2,1,0:T(8,128)}, f32[7,3,16,128]{3,2,1,0:T(8,128)S(1)}, u32[]{:S(2)}, u32[]{:S(2)}) collective-permute-start(f32[7,3,16,128]{3,2,1,0:T(8,128)} %get-tuple-element.19), channel_id=1, source_target_pairs={{0,4},{4,0},{8,12},{12,8},{16,20},{20,16},{24,28},{28,24},{1,5},{5... | collective-permute-start | bytes 516104 | tf_op jit(solution)/shard_map/ppermute | solution.py:429
  6.4 7.9 %collective-permute-start.2 = (f32[7,3,16,128]{3,2,1,0:T(8,128)}, f32[7,3,16,128]{3,2,1,0:T(8,128)S(1)}, u32[]{:S(2)}, u32[]{:S(2)}) collective-permute-start(f32[7,3,16,128]{3,2,1,0:T(8,128)} %get-tuple-element.20), channel_id=1, source_target_pairs={{0,1},{1,0},{4,8},{5,9},{8,4},{9,5},{12,16},{13,17},{16,12},{17,13... | collective-permute-start | bytes 516104 | tf_op jit(solution)/shard_map/ppermute | solution.py:438
  6.4 1.5 %copy-start.4 = (s32[1,1,1,32,1]{3,4,2,1,0:T(1,128)S(1)}, s32[1,1,1,32,1]{3,4,2,1,0:T(1,128)}, u32[]{:S(2)}) copy-start(s32[1,1,1,32,1]{3,4,2,1,0:T(1,128)} %param.15) | copy-start | bytes 388
  6.4 7.9 %collective-permute-start.3 = (f32[7,3,16,128]{3,2,1,0:T(8,128)}, f32[7,3,16,128]{3,2,1,0:T(8,128)S(1)}, u32[]{:S(2)}, u32[]{:S(2)}) collective-permute-start(f32[7,3,16,128]{3,2,1,0:T(8,128)} %get-tuple-element.21), channel_id=1, source_target_pairs={{0,2},{2,0},{1,3},{3,1},{4,6},{6,4},{5,7},{7,5},{8,10},{10,8},{9,1... | collective-permute-start | bytes 516104 | tf_op jit(solution)/shard_map/ppermute | solution.py:443
  7.9 1.1 %copy-start.5 = (f32[5,16,16,128]{3,2,1,0:T(8,128)S(1)}, f32[5,16,16,128]{3,2,1,0:T(8,128)}, u32[]{:S(2)}) copy-start(f32[5,16,16,128]{3,2,1,0:T(8,128)} %source.1) | copy-start | bytes 1966084
  9.0 0.9 %copy-start.6 = (f32[16,16,128]{2,1,0:T(8,128)S(1)}, f32[16,16,128]{2,1,0:T(8,128)}, u32[]{:S(2)}) copy-start(f32[16,16,128]{2,1,0:T(8,128)} %sponge.3) | copy-start | bytes 393220
  9.9 1.0 %copy-start.9 = (bf16[1376,128]{1,0:T(8,128)(2,1)S(1)}, bf16[1376,128]{1,0:T(8,128)(2,1)}, u32[]{:S(2)}) copy-start(bf16[1376,128]{1,0:T(8,128)(2,1)} %constant.4.clone.table) | copy-start | bytes 1056772
  10.9 0.8 %copy-start.11 = (bf16[256,128]{1,0:T(8,128)(2,1)S(1)}, bf16[256,128]{1,0:T(8,128)(2,1)}, u32[]{:S(2)}) copy-start(bf16[256,128]{1,0:T(8,128)(2,1)} %constant.5.clone.refs_1_.edge) | copy-start | bytes 196612
  14.6 10.3 %collective-permute-start.5 = (f32[5,16,16,128]{3,2,1,0:T(8,128)S(1)}, f32[5,16,16,128]{3,2,1,0:T(8,128)S(1)}, u32[]{:S(2)}, u32[]{:S(2)}) collective-permute-start(f32[5,16,16,128]{3,2,1,0:T(8,128)S(1)} %get-tuple-element.23.mid), channel_id=1, source_target_pairs={{0,1},{1,0},{2,3},{3,2},{4,5},{5,4},{6,7},{7,6},{8,9},{9,8},{10,11... | collective-permute-start | bytes 1966088 | tf_op jit(solution)/shard_map/ppermute | solution.py:443
  14.7 10.2 %copy-start.10 = (bf16[1376,128]{1,0:T(8,128)(2,1)S(1)}, bf16[1376,128]{1,0:T(8,128)(2,1)}, u32[]{:S(2)}) copy-start(bf16[1376,128]{1,0:T(8,128)(2,1)} %constant.4.clone.table) | copy-start | bytes 1056772
  15.8 9.2 %copy-start.7 = (f32[16,16,128]{2,1,0:T(8,128)S(1)}, f32[16,16,128]{2,1,0:T(8,128)}, u32[]{:S(2)}) copy-start(f32[16,16,128]{2,1,0:T(8,128)} %sponge.3) | copy-start | bytes 393220
  15.8 15.0 %all-to-all-start = ((f32[32,1,640]{2,1,0:T(1,128)}), f32[32,1,640]{2,1,0:T(1,128)S(1)}, u32[]{:S(2)}, u32[]{:S(2)}) async-start(f32[32,1,640]{2,1,0:T(1,128)} %shard_map.109), calls=%async_computation | async-start | bytes 163840 | tf_op jit(solution)/shard_map/all_to_all | solution.py:511
  21.6 8.0 %collective-permute-start.6 = (f32[5,3,16,128]{3,2,1,0:T(8,128)S(1)}, f32[5,3,16,128]{3,2,1,0:T(8,128)S(1)}, u32[]{:S(2)}, u32[]{:S(2)}) collective-permute-start(f32[5,3,16,128]{3,2,1,0:T(8,128)S(1)} %get-tuple-element.25), channel_id=1, source_target_pairs={{0,4},{4,0},{8,12},{12,8},{16,20},{20,16},{24,28},{28,24},{1,5},{5... | collective-permute-start | bytes 368648 | tf_op jit(solution)/shard_map/ppermute | solution.py:429
  23.4 6.2 %collective-permute-start.7 = (f32[5,3,16,128]{3,2,1,0:T(8,128)S(1)}, f32[5,3,16,128]{3,2,1,0:T(8,128)S(1)}, u32[]{:S(2)}, u32[]{:S(2)}) collective-permute-start(f32[5,3,16,128]{3,2,1,0:T(8,128)S(1)} %get-tuple-element.26), channel_id=1, source_target_pairs={{0,1},{1,0},{4,8},{5,9},{8,4},{9,5},{12,16},{13,17},{16,12},{17,13... | collective-permute-start | bytes 368648 | tf_op jit(solution)/shard_map/ppermute | solution.py:438
  23.4 6.2 %copy-start.12 = (bf16[256,128]{1,0:T(8,128)(2,1)S(1)}, bf16[256,128]{1,0:T(8,128)(2,1)}, u32[]{:S(2)}) copy-start(bf16[256,128]{1,0:T(8,128)(2,1)} %constant.5.clone.refs_1_.edge) | copy-start | bytes 196612
  23.4 6.2 %collective-permute-start.8 = (f32[5,3,16,128]{3,2,1,0:T(8,128)S(1)}, f32[5,3,16,128]{3,2,1,0:T(8,128)S(1)}, u32[]{:S(2)}, u32[]{:S(2)}) collective-permute-start(f32[5,3,16,128]{3,2,1,0:T(8,128)S(1)} %get-tuple-element.27), channel_id=1, source_target_pairs={{0,2},{2,0},{1,3},{3,1},{4,6},{6,4},{5,7},{7,5},{8,10},{10,8},{9,1... | collective-permute-start | bytes 368648 | tf_op jit(solution)/shard_map/ppermute | solution.py:443
  25.9 4.9 %copy-start.3 = (f32[1,128,128]{2,1,0:T(8,128)S(1)}, f32[1,128,128]{2,1,0:T(8,128)}, u32[]{:S(2)}) copy-start(f32[1,128,128]{2,1,0:T(8,128)} %basis_ref.1) | copy-start | bytes 196612

commit v7 on v6

--- a/solution.py
+++ b/solution.py
@@ -317,7 +317,6 @@
     n_y = len(sides_of("ty"))
     n_z = len(sides_of("tz"))
     x_blocks, y_blocks, (out_ref, *msgs) = refs[:2], refs[2 : 2 + n_y], refs[2 + n_y + n_z :]
-    out_ref[...] = part_ref[...]
     add_y_blocks(TIME_STEP, out_ref, vel, c, y_blocks, edge)
     add_x_blocks(TIME_STEP, out_ref, vel, c, x_blocks)
     pack_second(out_ref, msgs[:2], msgs[2:])
@@ -389,11 +388,10 @@
 
 def final_kernel(part_ref, vel, c, edge, *refs):
     n_y = len(sides_of("ty"))
-    x_blocks, y_blocks, (out_ref, token, work, sems) = refs[:2], refs[2 : 2 + n_y], refs[2 + n_y :]
+    x_blocks, y_blocks, (work, out_ref, token, sems) = refs[:2], refs[2 : 2 + n_y], refs[2 + n_y :]
     nx = part_ref.shape[1]
     token[...] = jnp.zeros(token.shape, F32)
     scale = 0.5 * TIME_STEP
-    work[...] = part_ref[...]
     add_y_blocks(scale, work, vel, c, y_blocks, edge)
     inner = pltpu.make_async_copy(work.at[:, HALO : nx - HALO], out_ref.at[:, HALO : nx - HALO], sems.at[0])
     inner.start()
@@ -449,7 +447,7 @@
     return [ring(to_above, axis, 1), ring(to_below, axis, -1)]
 
 
-def call(kernel, args, outs, scratch=(), away={}, out_away={}, flops=0, grant=12, hint=(20, 10)):
+def call(kernel, args, outs, scratch=(), away={}, out_away={}, flops=0, grant=12, hint=(20, 10), same={}):
     moved = sum(4 * math.prod(a.shape) for a in (*args, *outs))
     return pl.pallas_call(
         kernel,
@@ -457,6 +455,7 @@
         in_specs=[away.get(i, VMEM) for i in range(len(args))],
         out_specs=[out_away.get(i, VMEM) for i in range(len(outs))],
         scratch_shapes=list(scratch),
+        input_output_aliases=same,
         cost_estimate=pl.CostEstimate(flops=int(flops * hint[0]), bytes_accessed=int(moved * hint[1]), transcendentals=0),
         compiler_params=pltpu.CompilerParams(vmem_limit_bytes=grant << 20),
     )(*args)
@@ -482,7 +481,8 @@
         away={i: HBM for i in range(4)},
         grant=60, flops=10**6,
     )
-    z_blocks = from_sides("tz", adjoint, adjoint)
+    whole, _ = lax.optimization_barrier((adjoint, token))
+    z_blocks = from_sides("tz", whole, whole)
     auxes = from_sides("tz", aux, aux)
     y_first = from_sides("ty", msgs[2], msgs[-1])
     x_first = swap_x(msgs[0], msgs[1])
@@ -496,6 +496,7 @@
         [part, vel, c, edge, *x_first, *y_first, *auxes],
         [brick] + [shape(5, HALO, ny, nz)] * 2 + [shape(5, HALO, nx, nz)] * n_y,
         flops=work // 4,
+        same={0: 0},
         grant=8,
     )
     z_blocks = from_sides("tz", mid, mid)
@@ -512,12 +513,13 @@
     (part,) = call(
         second_kernel, [mid, base, vel, c, sponge, table, *z_blocks], [brick], grads, flops=work, grant=8
     )
-    adjoint_out, token = call(
+    _, adjoint_out, token = call(
         final_kernel,
         [part, vel, c, edge, *x_blocks, *y_blocks],
-        [brick, shape(8, nz)],
-        [pltpu.VMEM((5, nx, ny, nz), F32), pltpu.SemaphoreType.DMA((3,))],
-        out_away={0: HBM},
+        [brick, brick, shape(8, nz)],
+        [pltpu.SemaphoreType.DMA((3,))],
+        out_away={1: HBM},
+        same={0: 0},
         flops=work // 4,
         grant=6,
     )

time: 31.9 us -> 31.9 us (level)
  transfers between devices with their start and end apart: 10 -> 10, of which waited for: 2 -> 2; matrix products, arithmetic and copies ran while one was open for 0% -> 0% of each run, Pallas kernels for 20% -> 13%
where the time goes in v7:
time: 31.9 us; the launch traced here: 31.6 us
  starting transfers between devices  14.2 us (45%)
  Pallas kernels  7.42 us (23%)
  waiting for transfers between devices  5.28 us (17%)
  local copies, waits for them, and re-layouts  3.85 us (12%)
  between operations  0.81 us (3%)
    pallas_call x7, Pallas kernels, call(): pl.pallas_call(kernel, out_shape=list(outs), in_specs=[away.get(i, VMEM)...  7.42 us
    all_to_all x1, starting transfers between devices, on_device(): lax.all_to_all(sums, ('ax', 'ty', 'tz'), split_axis=0, concat_axis=0, til...  5.83 us
    ppermute x2, waiting for transfers between devices, swap_x(): near = lax.ppermute(first, 'ax', [(i, i ^ 1) for i in range(count)])  5.26 us
    ppermute x2, starting transfers between devices, swap_x(): near = lax.ppermute(first, 'ax', [(i, i ^ 1) for i in range(count)])  4.78 us
    unnamed x26, local copies, waits for them, and re-layouts  3.85 us
    ppermute x5, starting transfers between devices, ring(): lax.ppermute(v, axis, [(i, (i + step) % count) for i in range(count)])  3.62 us
  transfers between devices with their start and end apart: 10, of which 2 were waited for; matrix products, arithmetic and copies ran while one was open for 0% of the time, Pallas kernels for 13%

profile of v7, /device:TPU:0, one launch (start us, length us, event | category | flops | bytes accessed | tf_op | source)
XLA Modules:
  0.0 31.6 jit_solution(6211390160497321086)
XLA Ops:
  0.6 0.0 copy-start.1
  0.6 0.0 copy-start
  0.6 0.0 copy-start.2
  0.7 2.1 %shard_map.104 = (f32[7,3,16,128]{3,2,1,0:T(8,128)}, f32[7,3,16,128]{3,2,1,0:T(8,128)}, f32[7,3,16,128]{3,2,1,0:T(8,128)}, f32[2,3,16,128]{3,2,1,0:T(8,128)}, f32[8,128]{1,0:T(8,128)}) custom-call(f32[5,16,16,128]{3,2,1,0:T(8,128)} %adj.3, f32[3,16,16,128]{3,2,1,0:T(8,128)} %vel.11, f32[16,16,128]{2,1,0:T(8,128)} %c.11, s32[1,32]{1,0:T(1,128)} %bitcast.2), custom_call_target="tpu_custom_call" | custom-call | flops 20000000 | bytes 17491200 | tf_op jit(solution)/shard_map/pallas_call | solution.py:452
  2.8 0.0 copy-done.1
  2.8 0.0 copy-start.8
  2.8 0.5 %collective-permute-start = (f32[5,16,16,128]{3,2,1,0:T(8,128)S(1)}, f32[5,16,16,128]{3,2,1,0:T(8,128)S(1)}, u32[]{:S(2)}, u32[]{:S(2)}) collective-permute-start(f32[5,16,16,128]{3,2,1,0:T(8,128)S(1)} %copy-done.1), channel_id=1, source_target_pairs={{0,1},{1,0},{2,3},{3,2},{4,5},{5,4},{6,7},{7,6},{8,9},{9,8},{10,11... | collective-permute-start | bytes 1966088 | tf_op jit(solution)/shard_map/ppermute | solution.py:441
  3.4 0.1 collective-permute-start.4
  3.4 2.9 %collective-permute-start.1 = (f32[7,3,16,128]{3,2,1,0:T(8,128)}, f32[7,3,16,128]{3,2,1,0:T(8,128)S(1)}, u32[]{:S(2)}, u32[]{:S(2)}) collective-permute-start(f32[7,3,16,128]{3,2,1,0:T(8,128)} %get-tuple-element.21), channel_id=1, source_target_pairs={{0,4},{4,0},{8,12},{12,8},{16,20},{20,16},{24,28},{28,24},{1,5},{5... | collective-permute-start | bytes 516104 | tf_op jit(solution)/shard_map/ppermute | solution.py:427
  6.4 0.0 copy-start.4
  6.4 0.0 collective-permute-start.2
  6.4 1.5 %collective-permute-start.3 = (f32[7,3,16,128]{3,2,1,0:T(8,128)}, f32[7,3,16,128]{3,2,1,0:T(8,128)S(1)}, u32[]{:S(2)}, u32[]{:S(2)}) collective-permute-start(f32[7,3,16,128]{3,2,1,0:T(8,128)} %get-tuple-element.23), channel_id=1, source_target_pairs={{0,2},{2,0},{1,3},{3,1},{4,6},{6,4},{5,7},{7,5},{8,10},{10,8},{9,1... | collective-permute-start | bytes 516104 | tf_op jit(solution)/shard_map/ppermute | solution.py:441
  7.9 0.0 collective-permute-done.refs_2_
  7.9 0.0 copy-done
  7.9 0.0 copy-done.2
  7.9 0.0 copy-done.8
  7.9 0.0 copy-done.4
  7.9 0.0 copy-start.5
  7.9 1.1 %copy-done.5 = f32[5,16,16,128]{3,2,1,0:T(8,128)S(1)} copy-done((f32[5,16,16,128]{3,2,1,0:T(8,128)S(1)}, f32[5,16,16,128]{3,2,1,0:T(8,128)}, u32[]{:S(2)}) %copy-start.5) | copy-done | bytes 655384
  9.0 0.0 copy-start.6
  9.0 0.9 %copy-done.6 = f32[16,16,128]{2,1,0:T(8,128)S(1)} copy-done((f32[16,16,128]{2,1,0:T(8,128)S(1)}, f32[16,16,128]{2,1,0:T(8,128)}, u32[]{:S(2)}) %copy-start.6) | copy-done | bytes 131096
  9.9 0.0 copy-start.9
  9.9 1.0 %copy-done.9 = bf16[1376,128]{1,0:T(8,128)(2,1)S(1)} copy-done((bf16[1376,128]{1,0:T(8,128)(2,1)S(1)}, bf16[1376,128]{1,0:T(8,128)(2,1)}, u32[]{:S(2)}) %copy-start.9) | copy-done | bytes 352280
  10.9 0.0 copy-start.11
  10.9 0.8 %copy-done.11 = bf16[256,128]{1,0:T(8,128)(2,1)S(1)} copy-done((bf16[256,128]{1,0:T(8,128)(2,1)S(1)}, bf16[256,128]{1,0:T(8,128)(2,1)}, u32[]{:S(2)}) %copy-start.11) | copy-done | bytes 65560
  11.7 1.0 %shard_map.105 = (f32[5,16,16,128]{3,2,1,0:T(8,128)S(1)}, f32[5,16,16,128]{3,2,1,0:T(8,128)S(1)}, f32[2,16,128]{2,1,0:T(8,128)S(1)}, bf16[864,128]{1,0:T(8,128)(2,1)S(1)}) custom-call(f32[5,16,16,128]{3,2,1,0:T(8,128)S(1)} %copy-done.1, f32[3,16,16,128]{3,2,1,0:T(8,128)S(1)} %copy-done, f32[16,16,128]{2,1,0:T(8,128)S(1)} %copy-done.2, ...), custom_call_target="tpu_custom_call" | custom-call | flops 2621440000 | bytes 52307200 | tf_op jit(solution)/shard_map/pallas_call | solution.py:452
  12.8 0.0 collective-permute-done.4.refs_3_
  12.8 1.5 %collective-permute-done.1.refs_0_ = f32[7,3,16,128]{3,2,1,0:T(8,128)S(1)} collective-permute-done((f32[7,3,16,128]{3,2,1,0:T(8,128)}, f32[7,3,16,128]{3,2,1,0:T(8,128)S(1)}, u32[]{:S(2)}, u32[]{:S(2)}) %collective-permute-start.1) | collective-permute-done | bytes 172064 | tf_op jit(solution)/shard_map/ppermute | solution.py:427
  14.3 0.0 collective-permute-done.2.refs_1_
  14.3 0.0 collective-permute-done.3.refs_2_
  14.3 0.4 %shard_map.106 = (f32[5,16,16,128]{3,2,1,0:T(8,128)S(1)}, f32[5,3,16,128]{3,2,1,0:T(8,128)S(1)}, f32[5,3,16,128]{3,2,1,0:T(8,128)S(1)}, f32[5,3,16,128]{3,2,1,0:T(8,128)S(1)}) custom-call(f32[5,16,16,128]{3,2,1,0:T(8,128)S(1)} %get-tuple-element.20.part_ref, f32[3,16,16,128]{3,2,1,0:T(8,128)S(1)} %copy-done, ...), custom_call_target="tpu_custom_call", output_to_operand_aliasing={{0}: (0, {})} | custom-call | flops 655360000 | bytes 28999680 | tf_op jit(solution)/shard_map/pallas_call | solution.py:452
  14.6 0.1 collective-permute-start.5
  14.7 0.0 copy-start.10
  14.7 1.0 %shard_map.109 = f32[32,1,640]{2,1,0:T(1,128)} custom-call(f32[5,16,16,128]{3,2,1,0:T(8,128)S(1)} %get-tuple-element.25.mid, f32[5,16,16,128]{3,2,1,0:T(8,128)S(1)} %get-tuple-element.26.base, f32[3,16,16,128]{3,2,1,0:T(8,128)S(1)} %copy-done, f32[16,16,128]{2,1,0:T(8,128)S(1)} %copy-done.2, f32[2,16,128]{2,1,0:T(8,128)S(1)} %get-tuple-element.31.sponge, ...), custom_call_target="tpu_custom_call" | custom-call | flops 655360000 | bytes 29410560 | tf_op jit(solution)/shard_map/pallas_call | solution.py:452
  15.8 0.0 copy-start.7
  15.8 5.8 %all-to-all-start = ((f32[32,1,640]{2,1,0:T(1,128)}), f32[32,1,640]{2,1,0:T(1,128)S(1)}, u32[]{:S(2)}, u32[]{:S(2)}) async-start(f32[32,1,640]{2,1,0:T(1,128)} %shard_map.109), calls=%async_computation | async-start | bytes 163840 | tf_op jit(solution)/shard_map/all_to_all | solution.py:512
  21.6 1.8 %collective-permute-start.6 = (f32[5,3,16,128]{3,2,1,0:T(8,128)S(1)}, f32[5,3,16,128]{3,2,1,0:T(8,128)S(1)}, u32[]{:S(2)}, u32[]{:S(2)}) collective-permute-start(f32[5,3,16,128]{3,2,1,0:T(8,128)S(1)} %get-tuple-element.27), channel_id=1, source_target_pairs={{0,4},{4,0},{8,12},{12,8},{16,20},{20,16},{24,28},{28,24},{1,5},{5... | collective-permute-start | bytes 368648 | tf_op jit(solution)/shard_map/ppermute | solution.py:427
  23.4 0.0 collective-permute-start.7
  23.4 0.0 copy-start.12
  23.4 1.5 %collective-permute-start.8 = (f32[5,3,16,128]{3,2,1,0:T(8,128)S(1)}, f32[5,3,16,128]{3,2,1,0:T(8,128)S(1)}, u32[]{:S(2)}, u32[]{:S(2)}) collective-permute-start(f32[5,3,16,128]{3,2,1,0:T(8,128)S(1)} %get-tuple-element.29), channel_id=1, source_target_pairs={{0,2},{2,0},{1,3},{3,1},{4,6},{6,4},{5,7},{7,5},{8,10},{10,8},{9,1... | collective-permute-start | bytes 368648 | tf_op jit(solution)/shard_map/ppermute | solution.py:441
  24.9 0.0 collective-permute-done.5.refs_0_
  24.9 0.0 copy-done.10
  24.9 0.0 copy-done.7
  24.9 0.9 %shard_map.107.part_ref = f32[5,16,16,128]{3,2,1,0:T(8,128)S(1)} custom-call(f32[5,16,16,128]{3,2,1,0:T(8,128)S(1)} %get-tuple-element.25.mid, f32[5,16,16,128]{3,2,1,0:T(8,128)S(1)} %get-tuple-element.26.base, f32[3,16,16,128]{3,2,1,0:T(8,128)S(1)} %copy-done, f32[16,16,128]{2,1,0:T(8,128)S(1)} %copy-done.2, f32[16,16,128]{2,1,0:T(8,128)S(1)} %copy-done.7, ...), custom_call_target="tpu_custom_call" | custom-call | flops 2621440000 | bytes 39813120 | tf_op jit(solution)/shard_map/pallas_call | solution.py:452
  25.8 0.0 copy-start.3
  25.8 3.8 %collective-permute-done.6.refs_0_ = f32[5,3,16,128]{3,2,1,0:T(8,128)S(1)} collective-permute-done((f32[5,3,16,128]{3,2,1,0:T(8,128)S(1)}, f32[5,3,16,128]{3,2,1,0:T(8,128)S(1)}, u32[]{:S(2)}, u32[]{:S(2)}) %collective-permute-start.6) | collective-permute-done | bytes 122912 | tf_op jit(solution)/shard_map/ppermute | solution.py:427
  29.6 0.0 collective-permute-done.7.refs_1_
  29.6 0.0 collective-permute-done.8.refs_2_
  29.6 0.0 copy-done.12
  29.6 1.1 %shard_map.108 = (f32[5,16,16,128]{3,2,1,0:T(8,128)S(1)}, f32[5,16,16,128]{3,2,1,0:T(8,128)}, f32[8,128]{1,0:T(8,128)S(1)}) custom-call(f32[5,16,16,128]{3,2,1,0:T(8,128)S(1)} %shard_map.107.part_ref, f32[3,16,16,128]{3,2,1,0:T(8,128)S(1)} %copy-done, f32[16,16,128]{2,1,0:T(8,128)S(1)} %copy-done.2, ...), custom_call_target="tpu_custom_call", output_to_operand_aliasing={{0}: (0, {})} | custom-call | flops 655360000 | bytes 29941760 | tf_op jit(solution)/shard_map/pallas_call | solution.py:452
  30.7 0.0 all-to-all-done.sums_ref
  30.7 0.0 copy-done.3
  30.8 0.8 %shard_map.110 = f32[5,1,32]{2,1,0:T(1,128)} custom-call(f32[32,1,640]{2,1,0:T(1,128)S(1)} %all-to-all-done.sums_ref, f32[1,128,128]{2,1,0:T(8,128)S(1)} %copy-done.3, f32[8,128]{1,0:T(8,128)S(1)} %get-tuple-element.33._), custom_call_target="tpu_custom_call" | custom-call | bytes 1521920 | tf_op jit(solution)/shard_map/pallas_call | solution.py:452
Async XLA Ops:
  0.6 2.2 %copy-start.1 = (f32[5,16,16,128]{3,2,1,0:T(8,128)S(1)}, f32[5,16,16,128]{3,2,1,0:T(8,128)}, u32[]{:S(2)}) copy-start(f32[5,16,16,128]{3,2,1,0:T(8,128)} %adj.3) | copy-start | bytes 1966084
  0.6 7.2 %copy-start = (f32[3,16,16,128]{3,2,1,0:T(8,128)S(1)}, f32[3,16,16,128]{3,2,1,0:T(8,128)}, u32[]{:S(2)}) copy-start(f32[3,16,16,128]{3,2,1,0:T(8,128)} %vel.11) | copy-start | bytes 1179652
  0.6 7.2 %copy-start.2 = (f32[16,16,128]{2,1,0:T(8,128)S(1)}, f32[16,16,128]{2,1,0:T(8,128)}, u32[]{:S(2)}) copy-start(f32[16,16,128]{2,1,0:T(8,128)} %c.11) | copy-start | bytes 393220
  2.8 5.1 %copy-start.8 = (f32[8,128]{1,0:T(8,128)S(1)}, f32[8,128]{1,0:T(8,128)}, u32[]{:S(2)}) copy-start(f32[8,128]{1,0:T(8,128)} %get-tuple-element.18._) | copy-start | bytes 12292
  2.8 5.0 %collective-permute-start = (f32[5,16,16,128]{3,2,1,0:T(8,128)S(1)}, f32[5,16,16,128]{3,2,1,0:T(8,128)S(1)}, u32[]{:S(2)}, u32[]{:S(2)}) collective-permute-start(f32[5,16,16,128]{3,2,1,0:T(8,128)S(1)} %copy-done.1), channel_id=1, source_target_pairs={{0,1},{1,0},{2,3},{3,2},{4,5},{5,4},{6,7},{7,6},{8,9},{9,8},{10,11... | collective-permute-start | bytes 1966088 | tf_op jit(solution)/shard_map/ppermute | solution.py:441
  3.4 9.4 %collective-permute-start.4 = (f32[2,3,16,128]{3,2,1,0:T(8,128)}, f32[2,3,16,128]{3,2,1,0:T(8,128)S(1)}, u32[]{:S(2)}, u32[]{:S(2)}) collective-permute-start(f32[2,3,16,128]{3,2,1,0:T(8,128)} %get-tuple-element.24), channel_id=1, source_target_pairs={{0,1},{1,0},{2,3},{3,2},{4,5},{5,4},{6,7},{7,6},{8,9},{9,8},{10,11... | collective-permute-start | bytes 147464 | tf_op jit(solution)/shard_map/ppermute | solution.py:441
  3.4 10.8 %collective-permute-start.1 = (f32[7,3,16,128]{3,2,1,0:T(8,128)}, f32[7,3,16,128]{3,2,1,0:T(8,128)S(1)}, u32[]{:S(2)}, u32[]{:S(2)}) collective-permute-start(f32[7,3,16,128]{3,2,1,0:T(8,128)} %get-tuple-element.21), channel_id=1, source_target_pairs={{0,4},{4,0},{8,12},{12,8},{16,20},{20,16},{24,28},{28,24},{1,5},{5... | collective-permute-start | bytes 516104 | tf_op jit(solution)/shard_map/ppermute | solution.py:427
  6.4 1.5 %copy-start.4 = (s32[1,1,1,32,1]{3,4,2,1,0:T(1,128)S(1)}, s32[1,1,1,32,1]{3,4,2,1,0:T(1,128)}, u32[]{:S(2)}) copy-start(s32[1,1,1,32,1]{3,4,2,1,0:T(1,128)} %param.15) | copy-start | bytes 388
  6.4 7.9 %collective-permute-start.2 = (f32[7,3,16,128]{3,2,1,0:T(8,128)}, f32[7,3,16,128]{3,2,1,0:T(8,128)S(1)}, u32[]{:S(2)}, u32[]{:S(2)}) collective-permute-start(f32[7,3,16,128]{3,2,1,0:T(8,128)} %get-tuple-element.22), channel_id=1, source_target_pairs={{0,1},{1,0},{4,8},{5,9},{8,4},{9,5},{12,16},{13,17},{16,12},{17,13... | collective-permute-start | bytes 516104 | tf_op jit(solution)/shard_map/ppermute | solution.py:436
  6.4 7.9 %collective-permute-start.3 = (f32[7,3,16,128]{3,2,1,0:T(8,128)}, f32[7,3,16,128]{3,2,1,0:T(8,128)S(1)}, u32[]{:S(2)}, u32[]{:S(2)}) collective-permute-start(f32[7,3,16,128]{3,2,1,0:T(8,128)} %get-tuple-element.23), channel_id=1, source_target_pairs={{0,2},{2,0},{1,3},{3,1},{4,6},{6,4},{5,7},{7,5},{8,10},{10,8},{9,1... | collective-permute-start | bytes 516104 | tf_op jit(solution)/shard_map/ppermute | solution.py:441
  7.9 1.1 %copy-start.5 = (f32[5,16,16,128]{3,2,1,0:T(8,128)S(1)}, f32[5,16,16,128]{3,2,1,0:T(8,128)}, u32[]{:S(2)}) copy-start(f32[5,16,16,128]{3,2,1,0:T(8,128)} %source.1) | copy-start | bytes 1966084
  9.0 0.9 %copy-start.6 = (f32[16,16,128]{2,1,0:T(8,128)S(1)}, f32[16,16,128]{2,1,0:T(8,128)}, u32[]{:S(2)}) copy-start(f32[16,16,128]{2,1,0:T(8,128)} %sponge.3) | copy-start | bytes 393220
  9.9 1.0 %copy-start.9 = (bf16[1376,128]{1,0:T(8,128)(2,1)S(1)}, bf16[1376,128]{1,0:T(8,128)(2,1)}, u32[]{:S(2)}) copy-start(bf16[1376,128]{1,0:T(8,128)(2,1)} %constant.4.clone.table) | copy-start | bytes 1056772
  10.9 0.8 %copy-start.11 = (bf16[256,128]{1,0:T(8,128)(2,1)S(1)}, bf16[256,128]{1,0:T(8,128)(2,1)}, u32[]{:S(2)}) copy-start(bf16[256,128]{1,0:T(8,128)(2,1)} %constant.5.clone.refs_1_.edge) | copy-start | bytes 196612
  14.6 10.3 %collective-permute-start.5 = (f32[5,16,16,128]{3,2,1,0:T(8,128)S(1)}, f32[5,16,16,128]{3,2,1,0:T(8,128)S(1)}, u32[]{:S(2)}, u32[]{:S(2)}) collective-permute-start(f32[5,16,16,128]{3,2,1,0:T(8,128)S(1)} %get-tuple-element.25.mid), channel_id=1, source_target_pairs={{0,1},{1,0},{2,3},{3,2},{4,5},{5,4},{6,7},{7,6},{8,9},{9,8},{10,11... | collective-permute-start | bytes 1966088 | tf_op jit(solution)/shard_map/ppermute | solution.py:441
  14.7 10.2 %copy-start.10 = (bf16[1376,128]{1,0:T(8,128)(2,1)S(1)}, bf16[1376,128]{1,0:T(8,128)(2,1)}, u32[]{:S(2)}) copy-start(bf16[1376,128]{1,0:T(8,128)(2,1)} %constant.4.clone.table) | copy-start | bytes 1056772
  15.8 9.2 %copy-start.7 = (f32[16,16,128]{2,1,0:T(8,128)S(1)}, f32[16,16,128]{2,1,0:T(8,128)}, u32[]{:S(2)}) copy-start(f32[16,16,128]{2,1,0:T(8,128)} %sponge.3) | copy-start | bytes 393220
  15.8 15.0 %all-to-all-start = ((f32[32,1,640]{2,1,0:T(1,128)}), f32[32,1,640]{2,1,0:T(1,128)S(1)}, u32[]{:S(2)}, u32[]{:S(2)}) async-start(f32[32,1,640]{2,1,0:T(1,128)} %shard_map.109), calls=%async_computation | async-start | bytes 163840 | tf_op jit(solution)/shard_map/all_to_all | solution.py:512
  21.6 8.0 %collective-permute-start.6 = (f32[5,3,16,128]{3,2,1,0:T(8,128)S(1)}, f32[5,3,16,128]{3,2,1,0:T(8,128)S(1)}, u32[]{:S(2)}, u32[]{:S(2)}) collective-permute-start(f32[5,3,16,128]{3,2,1,0:T(8,128)S(1)} %get-tuple-element.27), channel_id=1, source_target_pairs={{0,4},{4,0},{8,12},{12,8},{16,20},{20,16},{24,28},{28,24},{1,5},{5... | collective-permute-start | bytes 368648 | tf_op jit(solution)/shard_map/ppermute | solution.py:427
  23.4 6.2 %collective-permute-start.7 = (f32[5,3,16,128]{3,2,1,0:T(8,128)S(1)}, f32[5,3,16,128]{3,2,1,0:T(8,128)S(1)}, u32[]{:S(2)}, u32[]{:S(2)}) collective-permute-start(f32[5,3,16,128]{3,2,1,0:T(8,128)S(1)} %get-tuple-element.28), channel_id=1, source_target_pairs={{0,1},{1,0},{4,8},{5,9},{8,4},{9,5},{12,16},{13,17},{16,12},{17,13... | collective-permute-start | bytes 368648 | tf_op jit(solution)/shard_map/ppermute | solution.py:436
  23.4 6.2 %copy-start.12 = (bf16[256,128]{1,0:T(8,128)(2,1)S(1)}, bf16[256,128]{1,0:T(8,128)(2,1)}, u32[]{:S(2)}) copy-start(bf16[256,128]{1,0:T(8,128)(2,1)} %constant.5.clone.refs_1_.edge) | copy-start | bytes 196612
  23.4 6.2 %collective-permute-start.8 = (f32[5,3,16,128]{3,2,1,0:T(8,128)S(1)}, f32[5,3,16,128]{3,2,1,0:T(8,128)S(1)}, u32[]{:S(2)}, u32[]{:S(2)}) collective-permute-start(f32[5,3,16,128]{3,2,1,0:T(8,128)S(1)} %get-tuple-element.29), channel_id=1, source_target_pairs={{0,2},{2,0},{1,3},{3,1},{4,6},{6,4},{5,7},{7,5},{8,10},{10,8},{9,1... | collective-permute-start | bytes 368648 | tf_op jit(solution)/shard_map/ppermute | solution.py:441
  25.8 4.9 %copy-start.3 = (f32[1,128,128]{2,1,0:T(8,128)S(1)}, f32[1,128,128]{2,1,0:T(8,128)}, u32[]{:S(2)}) copy-start(f32[1,128,128]{2,1,0:T(8,128)} %basis_ref.1) | copy-start | bytes 196612

commit v8 on v6

--- a/solution.py
+++ b/solution.py
@@ -412,8 +412,11 @@
     total = sums_ref[0]
     for i in range(1, sums_ref.shape[0]):
         total = total + sums_ref[i]
-    modes = lax.dot_general(
-        jnp.concatenate(jnp.split(total, 5, axis=1), axis=0), basis_ref[0], (((1,), (0,)), ((), ())), precision=lax.Precision.HIGHEST, preferred_element_type=F32
+    parts = halves(jnp.concatenate(jnp.split(total, 5, axis=1), axis=0))
+    basis_high, basis_low = halves(basis_ref[0])
+    modes = dot(
+        jnp.concatenate([*parts, *parts], axis=1),
+        jnp.concatenate([basis_high, basis_high, basis_low, basis_low], axis=0),
     )
     mine = lax.axis_index("ty") * lax.axis_size("tz") + lax.axis_index("tz")
     width = modes.shape[1]

time: 31.9 us -> 31.9 us (level)
  no operation moved by 1% of the time
where the time goes in v8:
time: 31.9 us; the launch traced here: 31.6 us
  starting transfers between devices  14.3 us (45%)
  Pallas kernels  7.38 us (23%)
  waiting for transfers between devices  5.24 us (16%)
  local copies, waits for them, and re-layouts  3.85 us (12%)
  between operations  0.8 us (3%)
    pallas_call x7, Pallas kernels, call(): pl.pallas_call(kernel, out_shape=list(outs), in_specs=[away.get(i, VMEM)...  7.38 us
    all_to_all x1, starting transfers between devices, on_device(): lax.all_to_all(sums, ('ax', 'ty', 'tz'), split_axis=0, concat_axis=0, til...  5.83 us
    ppermute x2, waiting for transfers between devices, swap_x(): near = lax.ppermute(first, 'ax', [(i, i ^ 1) for i in range(count)])  5.22 us
    ppermute x2, starting transfers between devices, swap_x(): near = lax.ppermute(first, 'ax', [(i, i ^ 1) for i in range(count)])  4.79 us
    unnamed x26, local copies, waits for them, and re-layouts  3.85 us
    ppermute x5, starting transfers between devices, ring(): lax.ppermute(v, axis, [(i, (i + step) % count) for i in range(count)])  3.68 us
  transfers between devices with their start and end apart: 10, of which 2 were waited for; matrix products, arithmetic and copies ran while one was open for 0% of the time, Pallas kernels for 20%

profile of v8, /device:TPU:0, one launch (start us, length us, event | category | flops | bytes accessed | tf_op | source)
XLA Modules:
  0.0 31.6 jit_solution(8327652735797819640)
XLA Ops:
  0.6 0.0 copy-start.1
  0.6 0.5 %collective-permute-start = (f32[5,16,16,128]{3,2,1,0:T(8,128)}, f32[5,16,16,128]{3,2,1,0:T(8,128)S(1)}, u32[]{:S(2)}, u32[]{:S(2)}) collective-permute-start(f32[5,16,16,128]{3,2,1,0:T(8,128)} %adj.3), channel_id=1, source_target_pairs={{0,1},{1,0},{2,3},{3,2},{4,5},{5,4},{6,7},{7,6},{8,9},{9,8},{10,11... | collective-permute-start | bytes 1966088 | tf_op jit(solution)/shard_map/ppermute | solution.py:446
  1.2 0.0 copy-start
  1.2 0.0 copy-start.2
  1.2 2.1 %shard_map.104 = (f32[7,3,16,128]{3,2,1,0:T(8,128)}, f32[7,3,16,128]{3,2,1,0:T(8,128)}, f32[7,3,16,128]{3,2,1,0:T(8,128)}, f32[2,3,16,128]{3,2,1,0:T(8,128)}, f32[8,128]{1,0:T(8,128)}) custom-call(f32[5,16,16,128]{3,2,1,0:T(8,128)} %adj.3, f32[3,16,16,128]{3,2,1,0:T(8,128)} %vel.11, f32[16,16,128]{2,1,0:T(8,128)} %c.11, s32[1,32]{1,0:T(1,128)} %bitcast.2), custom_call_target="tpu_custom_call" | custom-call | flops 20000000 | bytes 17491200 | tf_op jit(solution)/shard_map/pallas_call | solution.py:457
  3.3 0.0 copy-start.8
  3.3 0.1 collective-permute-start.4
  3.4 3.0 %collective-permute-start.1 = (f32[7,3,16,128]{3,2,1,0:T(8,128)}, f32[7,3,16,128]{3,2,1,0:T(8,128)S(1)}, u32[]{:S(2)}, u32[]{:S(2)}) collective-permute-start(f32[7,3,16,128]{3,2,1,0:T(8,128)} %get-tuple-element.19), channel_id=1, source_target_pairs={{0,4},{4,0},{8,12},{12,8},{16,20},{20,16},{24,28},{28,24},{1,5},{5... | collective-permute-start | bytes 516104 | tf_op jit(solution)/shard_map/ppermute | solution.py:432
  6.4 0.0 collective-permute-start.2
  6.4 0.0 copy-start.4
  6.4 1.5 %collective-permute-start.3 = (f32[7,3,16,128]{3,2,1,0:T(8,128)}, f32[7,3,16,128]{3,2,1,0:T(8,128)S(1)}, u32[]{:S(2)}, u32[]{:S(2)}) collective-permute-start(f32[7,3,16,128]{3,2,1,0:T(8,128)} %get-tuple-element.21), channel_id=1, source_target_pairs={{0,2},{2,0},{1,3},{3,1},{4,6},{6,4},{5,7},{7,5},{8,10},{10,8},{9,1... | collective-permute-start | bytes 516104 | tf_op jit(solution)/shard_map/ppermute | solution.py:446
  7.9 0.0 collective-permute-done.refs_2_
  7.9 0.0 copy-done.1
  7.9 0.0 copy-done
  7.9 0.0 copy-done.2
  7.9 0.0 copy-done.8
  7.9 0.0 copy-done.4
  7.9 0.0 copy-start.5
  7.9 1.1 %copy-done.5 = f32[5,16,16,128]{3,2,1,0:T(8,128)S(1)} copy-done((f32[5,16,16,128]{3,2,1,0:T(8,128)S(1)}, f32[5,16,16,128]{3,2,1,0:T(8,128)}, u32[]{:S(2)}) %copy-start.5) | copy-done | bytes 655384
  9.0 0.0 copy-start.6
  9.0 0.9 %copy-done.6 = f32[16,16,128]{2,1,0:T(8,128)S(1)} copy-done((f32[16,16,128]{2,1,0:T(8,128)S(1)}, f32[16,16,128]{2,1,0:T(8,128)}, u32[]{:S(2)}) %copy-start.6) | copy-done | bytes 131096
  9.9 0.0 copy-start.9
  9.9 1.0 %copy-done.9 = bf16[1376,128]{1,0:T(8,128)(2,1)S(1)} copy-done((bf16[1376,128]{1,0:T(8,128)(2,1)S(1)}, bf16[1376,128]{1,0:T(8,128)(2,1)}, u32[]{:S(2)}) %copy-start.9) | copy-done | bytes 352280
  10.9 0.0 copy-start.11
  10.9 0.8 %copy-done.11 = bf16[256,128]{1,0:T(8,128)(2,1)S(1)} copy-done((bf16[256,128]{1,0:T(8,128)(2,1)S(1)}, bf16[256,128]{1,0:T(8,128)(2,1)}, u32[]{:S(2)}) %copy-start.11) | copy-done | bytes 65560
  11.7 1.0 %shard_map.105 = (f32[5,16,16,128]{3,2,1,0:T(8,128)S(1)}, f32[5,16,16,128]{3,2,1,0:T(8,128)S(1)}, f32[2,16,128]{2,1,0:T(8,128)S(1)}, bf16[864,128]{1,0:T(8,128)(2,1)S(1)}) custom-call(f32[5,16,16,128]{3,2,1,0:T(8,128)S(1)} %copy-done.1, f32[3,16,16,128]{3,2,1,0:T(8,128)S(1)} %copy-done, f32[16,16,128]{2,1,0:T(8,128)S(1)} %copy-done.2, ...), custom_call_target="tpu_custom_call" | custom-call | flops 2621440000 | bytes 52307200 | tf_op jit(solution)/shard_map/pallas_call | solution.py:457
  12.8 0.0 collective-permute-done.4.refs_3_
  12.8 1.5 %collective-permute-done.1.refs_0_ = f32[7,3,16,128]{3,2,1,0:T(8,128)S(1)} collective-permute-done((f32[7,3,16,128]{3,2,1,0:T(8,128)}, f32[7,3,16,128]{3,2,1,0:T(8,128)S(1)}, u32[]{:S(2)}, u32[]{:S(2)}) %collective-permute-start.1) | collective-permute-done | bytes 172064 | tf_op jit(solution)/shard_map/ppermute | solution.py:432
  14.2 0.0 collective-permute-done.2.refs_1_
  14.3 0.0 collective-permute-done.3.refs_2_
  14.3 0.4 %shard_map.106 = (f32[5,16,16,128]{3,2,1,0:T(8,128)S(1)}, f32[5,3,16,128]{3,2,1,0:T(8,128)S(1)}, f32[5,3,16,128]{3,2,1,0:T(8,128)S(1)}, f32[5,3,16,128]{3,2,1,0:T(8,128)S(1)}) custom-call(f32[5,16,16,128]{3,2,1,0:T(8,128)S(1)} %get-tuple-element.18.part_ref, f32[3,16,16,128]{3,2,1,0:T(8,128)S(1)} %copy-done, f32[16,16,128]{2,1,0:T(8,128)S(1)} %copy-done.2, ...), custom_call_target="tpu_custom_call" | custom-call | flops 655360000 | bytes 28999680 | tf_op jit(solution)/shard_map/pallas_call | solution.py:457
  14.6 0.1 collective-permute-start.5
  14.7 0.0 copy-start.10
  14.7 1.0 %shard_map.109 = f32[32,1,640]{2,1,0:T(1,128)} custom-call(f32[5,16,16,128]{3,2,1,0:T(8,128)S(1)} %get-tuple-element.23.mid, f32[5,16,16,128]{3,2,1,0:T(8,128)S(1)} %get-tuple-element.24.base, f32[3,16,16,128]{3,2,1,0:T(8,128)S(1)} %copy-done, f32[16,16,128]{2,1,0:T(8,128)S(1)} %copy-done.2, f32[2,16,128]{2,1,0:T(8,128)S(1)} %get-tuple-element.29.sponge, ...), custom_call_target="tpu_custom_call" | custom-call | flops 655360000 | bytes 29410560 | tf_op jit(solution)/shard_map/pallas_call | solution.py:457
  15.8 0.0 copy-start.7
  15.8 5.8 %all-to-all-start = ((f32[32,1,640]{2,1,0:T(1,128)}), f32[32,1,640]{2,1,0:T(1,128)S(1)}, u32[]{:S(2)}, u32[]{:S(2)}) async-start(f32[32,1,640]{2,1,0:T(1,128)} %shard_map.109), calls=%async_computation | async-start | bytes 163840 | tf_op jit(solution)/shard_map/all_to_all | solution.py:514
  21.6 1.8 %collective-permute-start.6 = (f32[5,3,16,128]{3,2,1,0:T(8,128)S(1)}, f32[5,3,16,128]{3,2,1,0:T(8,128)S(1)}, u32[]{:S(2)}, u32[]{:S(2)}) collective-permute-start(f32[5,3,16,128]{3,2,1,0:T(8,128)S(1)} %get-tuple-element.25), channel_id=1, source_target_pairs={{0,4},{4,0},{8,12},{12,8},{16,20},{20,16},{24,28},{28,24},{1,5},{5... | collective-permute-start | bytes 368648 | tf_op jit(solution)/shard_map/ppermute | solution.py:432
  23.4 0.0 collective-permute-start.7
  23.4 0.0 copy-start.12
  23.4 1.5 %collective-permute-start.8 = (f32[5,3,16,128]{3,2,1,0:T(8,128)S(1)}, f32[5,3,16,128]{3,2,1,0:T(8,128)S(1)}, u32[]{:S(2)}, u32[]{:S(2)}) collective-permute-start(f32[5,3,16,128]{3,2,1,0:T(8,128)S(1)} %get-tuple-element.27), channel_id=1, source_target_pairs={{0,2},{2,0},{1,3},{3,1},{4,6},{6,4},{5,7},{7,5},{8,10},{10,8},{9,1... | collective-permute-start | bytes 368648 | tf_op jit(solution)/shard_map/ppermute | solution.py:446
  24.9 0.0 collective-permute-done.5.refs_0_
  24.9 0.0 copy-done.10
  24.9 0.0 copy-done.7
  24.9 0.9 %shard_map.107.part_ref = f32[5,16,16,128]{3,2,1,0:T(8,128)S(1)} custom-call(f32[5,16,16,128]{3,2,1,0:T(8,128)S(1)} %get-tuple-element.23.mid, f32[5,16,16,128]{3,2,1,0:T(8,128)S(1)} %get-tuple-element.24.base, f32[3,16,16,128]{3,2,1,0:T(8,128)S(1)} %copy-done, f32[16,16,128]{2,1,0:T(8,128)S(1)} %copy-done.2, f32[16,16,128]{2,1,0:T(8,128)S(1)} %copy-done.7, ...), custom_call_target="tpu_custom_call" | custom-call | flops 2621440000 | bytes 39813120 | tf_op jit(solution)/shard_map/pallas_call | solution.py:457
  25.9 0.0 copy-start.3
  25.9 3.8 %collective-permute-done.6.refs_0_ = f32[5,3,16,128]{3,2,1,0:T(8,128)S(1)} collective-permute-done((f32[5,3,16,128]{3,2,1,0:T(8,128)S(1)}, f32[5,3,16,128]{3,2,1,0:T(8,128)S(1)}, u32[]{:S(2)}, u32[]{:S(2)}) %collective-permute-start.6) | collective-permute-done | bytes 122912 | tf_op jit(solution)/shard_map/ppermute | solution.py:432
  29.6 0.0 collective-permute-done.7.refs_1_
  29.6 0.0 collective-permute-done.8.refs_2_
  29.6 0.0 copy-done.12
  29.6 1.1 %shard_map.108 = (f32[5,16,16,128]{3,2,1,0:T(8,128)}, f32[8,128]{1,0:T(8,128)S(1)}) custom-call(f32[5,16,16,128]{3,2,1,0:T(8,128)S(1)} %shard_map.107.part_ref, f32[3,16,16,128]{3,2,1,0:T(8,128)S(1)} %copy-done, f32[16,16,128]{2,1,0:T(8,128)S(1)} %copy-done.2, bf16[256,128]{1,0:T(8,128)(2,1)S(1)} %copy-done.12, ...), custom_call_target="tpu_custom_call" | custom-call | flops 655360000 | bytes 23388160 | tf_op jit(solution)/shard_map/pallas_call | solution.py:457
  30.7 0.0 all-to-all-done.sums_ref
  30.7 0.0 copy-done.3
  30.8 0.8 %shard_map.110 = f32[5,1,32]{2,1,0:T(1,128)} custom-call(f32[32,1,640]{2,1,0:T(1,128)S(1)} %all-to-all-done.sums_ref, f32[1,128,128]{2,1,0:T(8,128)S(1)} %copy-done.3, f32[8,128]{1,0:T(8,128)S(1)} %get-tuple-element.31._), custom_call_target="tpu_custom_call" | custom-call | bytes 1521920 | tf_op jit(solution)/shard_map/pallas_call | solution.py:457
Async XLA Ops:
  0.6 7.2 %copy-start.1 = (f32[5,16,16,128]{3,2,1,0:T(8,128)S(1)}, f32[5,16,16,128]{3,2,1,0:T(8,128)}, u32[]{:S(2)}) copy-start(f32[5,16,16,128]{3,2,1,0:T(8,128)} %adj.3) | copy-start | bytes 1966084
  0.6 7.2 %collective-permute-start = (f32[5,16,16,128]{3,2,1,0:T(8,128)}, f32[5,16,16,128]{3,2,1,0:T(8,128)S(1)}, u32[]{:S(2)}, u32[]{:S(2)}) collective-permute-start(f32[5,16,16,128]{3,2,1,0:T(8,128)} %adj.3), channel_id=1, source_target_pairs={{0,1},{1,0},{2,3},{3,2},{4,5},{5,4},{6,7},{7,6},{8,9},{9,8},{10,11... | collective-permute-start | bytes 1966088 | tf_op jit(solution)/shard_map/ppermute | solution.py:446
  1.2 6.7 %copy-start = (f32[3,16,16,128]{3,2,1,0:T(8,128)S(1)}, f32[3,16,16,128]{3,2,1,0:T(8,128)}, u32[]{:S(2)}) copy-start(f32[3,16,16,128]{3,2,1,0:T(8,128)} %vel.11) | copy-start | bytes 1179652
  1.2 6.7 %copy-start.2 = (f32[16,16,128]{2,1,0:T(8,128)S(1)}, f32[16,16,128]{2,1,0:T(8,128)}, u32[]{:S(2)}) copy-start(f32[16,16,128]{2,1,0:T(8,128)} %c.11) | copy-start | bytes 393220
  3.3 4.6 %copy-start.8 = (f32[8,128]{1,0:T(8,128)S(1)}, f32[8,128]{1,0:T(8,128)}, u32[]{:S(2)}) copy-start(f32[8,128]{1,0:T(8,128)} %get-tuple-element.17._) | copy-start | bytes 12292
  3.3 9.5 %collective-permute-start.4 = (f32[2,3,16,128]{3,2,1,0:T(8,128)}, f32[2,3,16,128]{3,2,1,0:T(8,128)S(1)}, u32[]{:S(2)}, u32[]{:S(2)}) collective-permute-start(f32[2,3,16,128]{3,2,1,0:T(8,128)} %get-tuple-element.22), channel_id=1, source_target_pairs={{0,1},{1,0},{2,3},{3,2},{4,5},{5,4},{6,7},{7,6},{8,9},{9,8},{10,11... | collective-permute-start | bytes 147464 | tf_op jit(solution)/shard_map/ppermute | solution.py:446
  3.4 10.8 %collective-permute-start.1 = (f32[7,3,16,128]{3,2,1,0:T(8,128)}, f32[7,3,16,128]{3,2,1,0:T(8,128)S(1)}, u32[]{:S(2)}, u32[]{:S(2)}) collective-permute-start(f32[7,3,16,128]{3,2,1,0:T(8,128)} %get-tuple-element.19), channel_id=1, source_target_pairs={{0,4},{4,0},{8,12},{12,8},{16,20},{20,16},{24,28},{28,24},{1,5},{5... | collective-permute-start | bytes 516104 | tf_op jit(solution)/shard_map/ppermute | solution.py:432
  6.4 7.9 %collective-permute-start.2 = (f32[7,3,16,128]{3,2,1,0:T(8,128)}, f32[7,3,16,128]{3,2,1,0:T(8,128)S(1)}, u32[]{:S(2)}, u32[]{:S(2)}) collective-permute-start(f32[7,3,16,128]{3,2,1,0:T(8,128)} %get-tuple-element.20), channel_id=1, source_target_pairs={{0,1},{1,0},{4,8},{5,9},{8,4},{9,5},{12,16},{13,17},{16,12},{17,13... | collective-permute-start | bytes 516104 | tf_op jit(solution)/shard_map/ppermute | solution.py:441
  6.4 1.5 %copy-start.4 = (s32[1,1,1,32,1]{3,4,2,1,0:T(1,128)S(1)}, s32[1,1,1,32,1]{3,4,2,1,0:T(1,128)}, u32[]{:S(2)}) copy-start(s32[1,1,1,32,1]{3,4,2,1,0:T(1,128)} %param.15) | copy-start | bytes 388
  6.4 7.9 %collective-permute-start.3 = (f32[7,3,16,128]{3,2,1,0:T(8,128)}, f32[7,3,16,128]{3,2,1,0:T(8,128)S(1)}, u32[]{:S(2)}, u32[]{:S(2)}) collective-permute-start(f32[7,3,16,128]{3,2,1,0:T(8,128)} %get-tuple-element.21), channel_id=1, source_target_pairs={{0,2},{2,0},{1,3},{3,1},{4,6},{6,4},{5,7},{7,5},{8,10},{10,8},{9,1... | collective-permute-start | bytes 516104 | tf_op jit(solution)/shard_map/ppermute | solution.py:446
  7.9 1.1 %copy-start.5 = (f32[5,16,16,128]{3,2,1,0:T(8,128)S(1)}, f32[5,16,16,128]{3,2,1,0:T(8,128)}, u32[]{:S(2)}) copy-start(f32[5,16,16,128]{3,2,1,0:T(8,128)} %source.1) | copy-start | bytes 1966084
  9.0 0.9 %copy-start.6 = (f32[16,16,128]{2,1,0:T(8,128)S(1)}, f32[16,16,128]{2,1,0:T(8,128)}, u32[]{:S(2)}) copy-start(f32[16,16,128]{2,1,0:T(8,128)} %sponge.3) | copy-start | bytes 393220
  9.9 1.0 %copy-start.9 = (bf16[1376,128]{1,0:T(8,128)(2,1)S(1)}, bf16[1376,128]{1,0:T(8,128)(2,1)}, u32[]{:S(2)}) copy-start(bf16[1376,128]{1,0:T(8,128)(2,1)} %constant.4.clone.table) | copy-start | bytes 1056772
  10.9 0.8 %copy-start.11 = (bf16[256,128]{1,0:T(8,128)(2,1)S(1)}, bf16[256,128]{1,0:T(8,128)(2,1)}, u32[]{:S(2)}) copy-start(bf16[256,128]{1,0:T(8,128)(2,1)} %constant.5.clone.refs_1_.edge) | copy-start | bytes 196612
  14.6 10.3 %collective-permute-start.5 = (f32[5,16,16,128]{3,2,1,0:T(8,128)S(1)}, f32[5,16,16,128]{3,2,1,0:T(8,128)S(1)}, u32[]{:S(2)}, u32[]{:S(2)}) collective-permute-start(f32[5,16,16,128]{3,2,1,0:T(8,128)S(1)} %get-tuple-element.23.mid), channel_id=1, source_target_pairs={{0,1},{1,0},{2,3},{3,2},{4,5},{5,4},{6,7},{7,6},{8,9},{9,8},{10,11... | collective-permute-start | bytes 1966088 | tf_op jit(solution)/shard_map/ppermute | solution.py:446
  14.7 10.2 %copy-start.10 = (bf16[1376,128]{1,0:T(8,128)(2,1)S(1)}, bf16[1376,128]{1,0:T(8,128)(2,1)}, u32[]{:S(2)}) copy-start(bf16[1376,128]{1,0:T(8,128)(2,1)} %constant.4.clone.table) | copy-start | bytes 1056772
  15.8 9.2 %copy-start.7 = (f32[16,16,128]{2,1,0:T(8,128)S(1)}, f32[16,16,128]{2,1,0:T(8,128)}, u32[]{:S(2)}) copy-start(f32[16,16,128]{2,1,0:T(8,128)} %sponge.3) | copy-start | bytes 393220
  15.8 15.0 %all-to-all-start = ((f32[32,1,640]{2,1,0:T(1,128)}), f32[32,1,640]{2,1,0:T(1,128)S(1)}, u32[]{:S(2)}, u32[]{:S(2)}) async-start(f32[32,1,640]{2,1,0:T(1,128)} %shard_map.109), calls=%async_computation | async-start | bytes 163840 | tf_op jit(solution)/shard_map/all_to_all | solution.py:514
  21.6 8.0 %collective-permute-start.6 = (f32[5,3,16,128]{3,2,1,0:T(8,128)S(1)}, f32[5,3,16,128]{3,2,1,0:T(8,128)S(1)}, u32[]{:S(2)}, u32[]{:S(2)}) collective-permute-start(f32[5,3,16,128]{3,2,1,0:T(8,128)S(1)} %get-tuple-element.25), channel_id=1, source_target_pairs={{0,4},{4,0},{8,12},{12,8},{16,20},{20,16},{24,28},{28,24},{1,5},{5... | collective-permute-start | bytes 368648 | tf_op jit(solution)/shard_map/ppermute | solution.py:432
  23.4 6.2 %collective-permute-start.7 = (f32[5,3,16,128]{3,2,1,0:T(8,128)S(1)}, f32[5,3,16,128]{3,2,1,0:T(8,128)S(1)}, u32[]{:S(2)}, u32[]{:S(2)}) collective-permute-start(f32[5,3,16,128]{3,2,1,0:T(8,128)S(1)} %get-tuple-element.26), channel_id=1, source_target_pairs={{0,1},{1,0},{4,8},{5,9},{8,4},{9,5},{12,16},{13,17},{16,12},{17,13... | collective-permute-start | bytes 368648 | tf_op jit(solution)/shard_map/ppermute | solution.py:441
  23.4 6.2 %copy-start.12 = (bf16[256,128]{1,0:T(8,128)(2,1)S(1)}, bf16[256,128]{1,0:T(8,128)(2,1)}, u32[]{:S(2)}) copy-start(bf16[256,128]{1,0:T(8,128)(2,1)} %constant.5.clone.refs_1_.edge) | copy-start | bytes 196612
  23.4 6.2 %collective-permute-start.8 = (f32[5,3,16,128]{3,2,1,0:T(8,128)S(1)}, f32[5,3,16,128]{3,2,1,0:T(8,128)S(1)}, u32[]{:S(2)}, u32[]{:S(2)}) collective-permute-start(f32[5,3,16,128]{3,2,1,0:T(8,128)S(1)} %get-tuple-element.27), channel_id=1, source_target_pairs={{0,2},{2,0},{1,3},{3,1},{4,6},{6,4},{5,7},{7,5},{8,10},{10,8},{9,1... | collective-permute-start | bytes 368648 | tf_op jit(solution)/shard_map/ppermute | solution.py:446
  25.9 4.9 %copy-start.3 = (f32[1,128,128]{2,1,0:T(8,128)S(1)}, f32[1,128,128]{2,1,0:T(8,128)}, u32[]{:S(2)}) copy-start(f32[1,128,128]{2,1,0:T(8,128)} %basis_ref.1) | copy-start | bytes 196612
